TPU v7x, 256 devices: a whole 4x4x8 slice. The times are simulated.
256 devices in a mesh: row: 16 (over z, y_hi), col: 16 (over y_lo, x, core).
Axes of the slice: x: 4, y: 4 (y_hi: 2, y_lo: 2; y = y_hi * 2 + y_lo), z: 8, core: 2. Of those that a mesh axis runs over, the one named last changes fastest.
Arguments:
- anc_inverse: float32 [20480, 20480], P('row', 'col'), may hold values from -6 to 6
- l_store: float32 [16, 20480, 256], P('col', 'row'), may hold values from -0.0546875 to 0.0546875
- diag_inv: float32 [16, 256, 256], P('col'), may hold values from -6 to 6
- block_lists: int32 [4, 96], replicated, may hold values from 0 to 159, as said below
- block_counts: int32 [4], replicated, may hold values from 48 to 96, as said below
- sibling_columns: int32 [4], replicated, may hold values from 0 to 15, as said below
Outputs:
- upper_out: float32 [4, 256, 20480], P(None, 'row', 'col')
- lower_out: float32 [16, 20480, 256], P('col', 'row')
- diag_out: float32 [16, 256, 256], P('col')
Inputs may be any that keep to these rules, and one draw needn't show every extreme that they name: `block_lists`: in each sibling's row the entries are distinct block indices; entries at positions from block_counts onward are ignored. `block_counts`: some sibling uses all 96 entries. `sibling_columns`: distinct columns for distinct siblings.
All inputs are finite; a program needn't handle non-finite values.
Results may differ from a plain program's by a relative error of at most 0.00011.
Values sent between devices are 32-bit elements; how exact they have to be, the bound alone decides.
No kernel may reach another device: no remote copies, remote signals or barrier semaphores. Data moves between devices by JAX's collectives and lax.ppermute only.
A program may use at most 64 MiB of HBM per device.

v0:
```python
import functools

import jax
import jax.numpy as jnp
from jax import lax
from jax.experimental import pallas as pl
from jax.experimental.pallas import tpu as pltpu
from jax.sharding import Mesh
from jax.sharding import PartitionSpec as P

BLK = 128
SUB = 8
ROW = ("row_0", "row_1")
COL = ("col_y", "col_x", "core")
CAPS = (28,)

ROW_BLOCK, ROW_START, COL_BLOCK, COL_START = 0, 64, 72, 136
PIECE, ROW_SLOT, COL_SLOT, SOURCE, OWNER, PRESENT, AT_ROW = 144, 160, 224, 288, 352, 360, 361

SMEM = pl.BlockSpec(memory_space=pltpu.SMEM)
VMEM = pl.BlockSpec(memory_space=pltpu.VMEM)


def swapped(x, axis, bit):
    length = lax.axis_size(axis)
    return lax.ppermute(x, axis, [(i, i ^ bit) for i in range(length)])


def turned(x, axis, shift):
    length = lax.axis_size(axis)
    return lax.ppermute(x, axis, [(i, (i + shift) % length) for i in range(length)])


def member_blocks(block_lists, block_counts, block_total):
    block_ids = jnp.arange(block_total, dtype=jnp.int32)
    valid_entry = jnp.arange(block_lists.shape[1], dtype=jnp.int32)[None, :] < block_counts[:, None]
    entry_hits = (block_lists[:, :, None] == block_ids[None, None, :]) & valid_entry[:, :, None]
    return jnp.any(entry_hits, axis=1).astype(jnp.int32)


def slot_tables(listed):
    sib, blocks = listed.shape
    flat = listed.reshape(-1)
    place = jnp.arange(sib * blocks, dtype=jnp.int32)
    before = jnp.sum(jnp.where(place[None, :] < place[:, None], flat[None, :], 0), axis=1)
    here = (before[None, :] == place[:, None]) & (flat[None, :] > 0)
    code = jnp.sum(jnp.where(here, place[None, :], 0), axis=1)
    bounds = jnp.arange(sib + 1, dtype=jnp.int32) * blocks
    start = jnp.sum(jnp.where(place[None, :] < bounds[:, None], flat[None, :], 0), axis=1)
    slot = jnp.where(flat > 0, before, -1)
    return code, start, slot


def padded(values, length):
    return jnp.pad(values.astype(jnp.int32), (0, length - values.shape[0]))


def pick_kernel(cap, tab, x_ref, o_ref):
    def one(q, carry):
        o_ref[q] = x_ref[tab[SOURCE + q]]
        return carry

    lax.fori_loop(0, cap, one, 0)


def product_kernel(cap, sib, tab, g0, g1, c0, c1, ah, al, u_ref, ph_ref, pl_ref, p_ref, lhs, acc):
    parts = (g0, g1, c0, c1)
    for i in range(4 * len(parts)):
        at = pl.multiple_of(tab[PIECE + i] * SUB, SUB)
        p_ref[:, pl.ds(at, SUB), :] = parts[i // 4][i % 4]
    chunks, _, rows, _ = u_ref.shape

    def tile(ref, b, t):
        return ref[
            pl.ds(pl.multiple_of(b * BLK, BLK), BLK), pl.ds(pl.multiple_of(t * BLK, BLK), BLK)
        ]

    def square(ref, b0, b1, t0, t1):
        top = jnp.concatenate([tile(ref, b0, t0), tile(ref, b0, t1)], axis=1)
        low = jnp.concatenate([tile(ref, b1, t0), tile(ref, b1, t1)], axis=1)
        return jnp.concatenate([top, low], axis=0)

    def sibling(j, outer):
        r0 = tab[ROW_START + j]
        r1 = tab[ROW_START + j + 1]
        n0 = tab[COL_START + j]
        n1 = tab[COL_START + j + 1]
        quads = (r1 - r0 + 3) // 4

        def listed_panel(q):
            return jnp.where(q < r1, p_ref[jnp.minimum(q, cap - 1)], 0.0)

        def split(i, carry):
            q = r0 + 2 * i
            block = jnp.concatenate([listed_panel(q), listed_panel(q + 1)], axis=0)
            hi = block.astype(jnp.bfloat16)
            lo = (block - hi.astype(jnp.float32)).astype(jnp.bfloat16)

            @pl.when(q < r1)
            def _():
                ph_ref[q] = hi[:BLK]
                pl_ref[q] = lo[:BLK]

            @pl.when(q + 1 < r1)
            def _():
                ph_ref[q + 1] = hi[BLK:]
                pl_ref[q + 1] = lo[BLK:]

            across = hi.T
            lhs[i] = jnp.concatenate([across, across, lo.T], axis=1)
            return carry

        lax.fori_loop(0, 2 * quads, split, 0)

        def columns(o, carry):
            s = n0 + 2 * o
            t0 = tab[COL_BLOCK + s]
            t1 = tab[COL_BLOCK + s + 1]
            acc[...] = jnp.zeros_like(acc)

            def rows_of(i, inner):
                terms = []
                for k in range(2):
                    b0 = tab[ROW_BLOCK + r0 + 4 * i + 2 * k]
                    b1 = tab[ROW_BLOCK + r0 + 4 * i + 2 * k + 1]
                    hi = square(ah, b0, b1, t0, t1)
                    lo = square(al, b0, b1, t0, t1)
                    terms.append(
                        jnp.dot(
                            lhs[2 * i + k],
                            jnp.concatenate([hi, lo, hi], axis=0),
                            preferred_element_type=jnp.float32,
                        )
                    )
                acc[...] += terms[0] + terms[1]
                return inner

            lax.fori_loop(0, quads, rows_of, 0)
            for z in range(chunks):
                u_ref[z, s] = -acc[z * rows : (z + 1) * rows, :BLK]

            @pl.when(s + 1 < n1)
            def _():
                for z in range(chunks):
                    u_ref[z, s + 1] = -acc[z * rows : (z + 1) * rows, BLK:]

            return carry

        lax.fori_loop(0, (n1 - n0 + 1) // 2, columns, 0)
        return outer

    if cap < sib * (ah.shape[0] // BLK):
        for j in range(sib):
            sibling(j, 0)
    else:
        lax.fori_loop(0, sib, sibling, 0)

    def clear(s, carry):
        u_ref[:, s] = jnp.zeros((chunks, rows, BLK), jnp.float32)
        return carry

    lax.fori_loop(tab[COL_START + sib], cap, clear, 0)


def unpack_kernel(base, tab, x_ref, o_ref):
    sib, _, cells = o_ref.shape
    blocks = cells // BLK

    def sibling(j, carry):
        for b in range(blocks):
            slot = tab[base + j * blocks + b]
            o_ref[j, :, b * BLK : (b + 1) * BLK] = jnp.where(
                slot >= 0, x_ref[jnp.maximum(slot, 0)], 0.0
            )
        return carry

    lax.fori_loop(0, sib, sibling, 0)


def inner_kernel(sib, tab, x_ref, hi_ref, lo_ref, o_ref):
    def sibling(j, carry):
        def one(q, total):
            x = x_ref[q]
            x_hi = x.astype(jnp.bfloat16)
            x_lo = (x - x_hi.astype(jnp.float32)).astype(jnp.bfloat16)
            hi = hi_ref[q]
            return total + jnp.dot(
                jnp.concatenate([x_hi, x_lo, x_hi], axis=1),
                jnp.concatenate([hi, hi, lo_ref[q]], axis=0),
                preferred_element_type=jnp.float32,
            )

        o_ref[j] = lax.fori_loop(
            tab[ROW_START + j],
            tab[ROW_START + j + 1],
            one,
            jnp.zeros(o_ref.shape[1:], jnp.float32),
        )
        return carry

    lax.fori_loop(0, sib, sibling, 0)


def slots_kernel(tab, x_ref, inner_ref, o_ref):
    sib, _, cells = x_ref.shape

    def clear(d, carry):
        o_ref[d] = jnp.zeros(o_ref.shape[1:], jnp.float32)
        return carry

    lax.fori_loop(0, o_ref.shape[0], clear, 0)
    for j in range(sib):
        at = tab[OWNER + j]
        o_ref[at, :, :cells] = x_ref[j]
        o_ref[at, :, cells:] = inner_ref[j]


def finish_kernel(tab, x_ref, diag_ref, lower_ref, out_ref):
    n_row = x_ref.shape[0]
    cells = lower_ref.shape[0]
    places = [lax.rem(2 * n_row - r - tab[AT_ROW], n_row) for r in range(n_row)]
    for b in range(cells // BLK):
        stack = jnp.concatenate([x_ref[p, :, b * BLK : (b + 1) * BLK] for p in places], axis=0)
        lower_ref[b * BLK : (b + 1) * BLK, :] = stack.T
    total = jnp.concatenate([x_ref[p, :, cells:] for p in places], axis=0)
    out_ref[...] = jnp.where(tab[PRESENT] > 0, diag_ref[...] - total, 0.0)


def ring_term(u, z, first, last, lead):
    part = lax.dynamic_index_in_dim(u, (z + 2 * u.shape[0]) % u.shape[0], 0, keepdims=False)
    part = part[first:last]
    return part if lead == 1 else part.reshape(lead, -1, *part.shape[1:])


def halves(parts, half, rows):
    return jnp.concatenate([lax.dynamic_slice_in_dim(x, half * rows, rows, 1) for x in parts])


def listed_products(cap, sib, table, scattered, a_hi, a_lo):
    row_cells, col_cells = a_hi.shape
    pieces, blocks, sub, width = scattered.shape
    near_chunks = lax.axis_size("row_0")
    half_rows = width // (near_chunks * lax.axis_size("row_1"))
    own = pl.pallas_call(
        functools.partial(pick_kernel, cap),
        out_shape=jax.ShapeDtypeStruct((cap, sub, width), jnp.float32),
        in_specs=[SMEM, VMEM],
        out_specs=VMEM,
        compiler_params=pltpu.CompilerParams(vmem_limit_bytes=8 << 20),
    )(table, scattered.reshape(pieces * blocks, sub, width))
    if cap < sib * blocks:
        right = turned(own, "col_x", 1)
        left = turned(own, "col_x", -1)
        beside = swapped(own, "col_y", 1)
        right_beside = turned(beside, "col_x", 1)
        left_beside = turned(beside, "col_x", -1)
        right_two = turned(right, "col_x", 1)
        left_two = turned(left_beside, "col_x", -1)
        g0 = jnp.stack([own, beside, right, left])
        g1 = jnp.stack([right_beside, left_beside, right_two, left_two])
        c0 = swapped(g0, "core", 1)
        c1 = swapped(g1, "core", 1)
    else:
        all_pieces = lax.all_to_all(
            jnp.broadcast_to(own[None], (pieces, *own.shape)), COL, 0, 0, tiled=True
        )
        order = piece_columns()
        parts = jnp.concatenate(
            [lax.dynamic_index_in_dim(all_pieces, order[i], 0) for i in range(pieces)]
        )
        g0, g1, c0, c1 = (parts[i : i + 4] for i in range(0, pieces, 4))
    chunk = width // near_chunks
    u, p_hi, p_lo = pl.pallas_call(
        functools.partial(product_kernel, cap, sib),
        out_shape=(
            jax.ShapeDtypeStruct((near_chunks, cap, chunk, BLK), jnp.float32),
            jax.ShapeDtypeStruct((cap, BLK, width), jnp.bfloat16),
            jax.ShapeDtypeStruct((cap, BLK, width), jnp.bfloat16),
        ),
        in_specs=[SMEM] + [VMEM] * 6,
        out_specs=(VMEM, VMEM, VMEM),
        scratch_shapes=[
            pltpu.VMEM((cap, BLK, width), jnp.float32),
            pltpu.VMEM((row_cells // BLK // 2 + 1, width, 6 * BLK), jnp.bfloat16),
            pltpu.VMEM((width, 2 * BLK), jnp.float32),
        ],
        compiler_params=pltpu.CompilerParams(vmem_limit_bytes=40 << 20),
    )(table, g0, g1, c0, c1, a_hi, a_lo)
    z = lax.axis_index("row_0")
    if cap < sib * blocks:
        strands = [(0, cap // 2, 1, 1), (cap // 2, cap, 2, -1)]
        near = [ring_term(u, z - way, first, last, lead) for first, last, lead, way in strands]
        for step in range(1, near_chunks):
            near = [
                turned(x, "row_0", way) + ring_term(u, z - way * (1 + step), first, last, lead)
                for x, (first, last, lead, way) in zip(near, strands)
            ]
        near = [x.reshape(-1, *x.shape[-2:]) for x in near]
    else:
        near = [jnp.sum(lax.all_to_all(u, "row_0", 0, 0, tiled=True), axis=0)]
    half = lax.axis_index("row_1")
    sent = halves(near, 1 - half, half_rows)
    kept = halves(near, half, half_rows)
    n_row = lax.axis_size(ROW)
    n_col = lax.axis_size(COL)
    spots = [(r, c) for r in range(n_row) for c in range(n_col)]
    across = [(r * n_col + c, r * n_col + (-r - c) % n_col) for r, c in spots]
    over = [(r * n_col + c, (r ^ 1) * n_col + (-(r ^ 1) - c) % n_col) for r, c in spots]
    along = [(r * n_col + k, (-r - k) % n_row * n_col + k) for r, k in spots]
    midway = lax.ppermute(kept, ROW + COL, across) + lax.ppermute(sent, ROW + COL, over)
    moved = lax.ppermute(midway, ROW + COL, along)
    total = kept + swapped(sent, "row_1", 1)
    unpack = lambda base, x: pl.pallas_call(
        functools.partial(unpack_kernel, base),
        out_shape=jax.ShapeDtypeStruct((sib, half_rows, col_cells), jnp.float32),
        in_specs=[SMEM, VMEM],
        out_specs=VMEM,
        compiler_params=pltpu.CompilerParams(vmem_limit_bytes=8 << 20),
        cost_estimate=pl.CostEstimate(flops=0, transcendentals=0, bytes_accessed=1 << 20),
    )(table, x)
    upper_part = unpack(COL_SLOT, total)
    inner = pl.pallas_call(
        functools.partial(inner_kernel, sib),
        out_shape=jax.ShapeDtypeStruct((sib, half_rows, width), jnp.float32),
        in_specs=[SMEM] + [VMEM] * 3,
        out_specs=VMEM,
        compiler_params=pltpu.CompilerParams(vmem_limit_bytes=12 << 20),
    )(table, moved, p_hi, p_lo)
    return upper_part, unpack(ROW_SLOT, moved), inner


def piece_columns():
    y = lax.axis_index("col_y")
    x = lax.axis_index("col_x")
    core = lax.axis_index("core")
    n_x = lax.axis_size("col_x")
    places = [(y, x), (1 - y, x), (y, x - 1), (y, x + 1)]
    places += [(1 - y, x - 1), (1 - y, x + 1), (y, x - 2), (1 - y, x + 2)]
    return jnp.stack(
        [
            (py * n_x + (px + n_x) % n_x) * 2 + pc
            for pc in (core, 1 - core)
            for py, px in places
        ]
    ).astype(jnp.int32)


def per_device(anc_inverse, l_store, diag_inv, block_lists, block_counts, sibling_columns):
    row_cells, col_cells = anc_inverse.shape
    width = l_store.shape[2]
    sib = sibling_columns.shape[0]
    n_col = lax.axis_size(COL)
    n_row = lax.axis_size(ROW)
    row_index = lax.axis_index(ROW)
    col_index = lax.axis_index(COL)
    blocks = row_cells // BLK
    cut = l_store[0].reshape(blocks, n_col, SUB, width).transpose(1, 0, 2, 3)
    scattered = lax.all_to_all(cut, COL, 0, 0, tiled=True)
    rounded = lax.reduce_precision(anc_inverse, 8, 7)
    a_hi = rounded.astype(jnp.bfloat16)
    a_lo = (anc_inverse - rounded).astype(jnp.bfloat16)

    listed = member_blocks(block_lists, block_counts, n_row * blocks)
    groups = listed.reshape(sib, n_row, blocks)
    most = jnp.max(jnp.sum(groups, axis=(0, 2)))
    row_code, row_start, row_slot = slot_tables(
        lax.dynamic_index_in_dim(groups, row_index, 1, keepdims=False)
    )
    col_code, col_start, col_slot = slot_tables(
        lax.dynamic_index_in_dim(groups, col_index, 1, keepdims=False)
    )
    owner = jnp.sum(
        jnp.where(
            (row_code // blocks)[:, None] == jnp.arange(sib, dtype=jnp.int32)[None, :],
            sibling_columns[None, :],
            0,
        ),
        axis=1,
    )
    table = jnp.concatenate(
        [
            padded(row_code % blocks, 64),
            padded(row_start, 8),
            padded(col_code % blocks, 64),
            padded(col_start, 8),
            padded(piece_columns(), 16),
            padded(row_slot, 64),
            padded(col_slot, 64),
            padded(owner * blocks + row_code % blocks, 64),
            padded(sibling_columns, 8),
            jnp.stack([jnp.any(sibling_columns == col_index).astype(jnp.int32), row_index]),
        ]
    )
    caps = [c for c in CAPS if c < sib * blocks] + [sib * blocks]
    which = sum((most > c).astype(jnp.int32) for c in caps[:-1])
    upper_part, moved, inner = lax.switch(
        which,
        [functools.partial(listed_products, c, sib) for c in caps],
        table,
        scattered,
        a_hi,
        a_lo,
    )
    for bit in (1, 4):
        others = []
        for away in (bit, 2 * bit, 3 * bit):
            pairs = [
                (r * n_col + k, (r ^ away) * n_col + (k + r - (r ^ away)) % n_col)
                for r in range(n_row)
                for k in range(n_col)
            ]
            others.append(lax.ppermute(inner, ROW + COL, pairs))
        inner = (inner + others[0]) + (others[1] + others[2])
    slots = pl.pallas_call(
        slots_kernel,
        out_shape=jax.ShapeDtypeStruct((n_col, width // n_row, row_cells + width), jnp.float32),
        in_specs=[SMEM] + [VMEM] * 2,
        out_specs=VMEM,
        compiler_params=pltpu.CompilerParams(vmem_limit_bytes=8 << 20),
    )(table, moved, inner)
    gathered = lax.all_to_all(slots, COL, 0, 0, tiled=True)
    lower, diag = pl.pallas_call(
        finish_kernel,
        out_shape=(
            jax.ShapeDtypeStruct((row_cells, width), jnp.float32),
            jax.ShapeDtypeStruct((width, width), jnp.float32),
        ),
        in_specs=[SMEM] + [VMEM] * 2,
        out_specs=(VMEM, VMEM),
        compiler_params=pltpu.CompilerParams(vmem_limit_bytes=12 << 20),
    )(table, gathered, diag_inv[0])
    return (upper_part, lower[None], diag[None])


def solution(mesh):
    finer = Mesh(mesh.devices.reshape(8, 2, 2, 4, 2), ROW + COL)
    return jax.shard_map(
        per_device,
        mesh=finer,
        in_specs=(P(ROW, COL), P(COL, ROW, None), P(COL, None, None), P(), P(), P()),
        out_specs=(P(None, ROW, COL), P(COL, ROW, None), P(COL, None, None)),
        check_vma=False,
    )
```

profile of v0, /device:TPU:1, one launch (start us, length us, event | category | flops | bytes accessed | tf_op | source)
XLA Modules:
  0.0 235.2 jit_solution(4553907414714399552)
XLA Ops:
  0.6 2.5 %copy.12 = f32[16,10,8,256]{3,2,1,0:T(8,128)} copy(f32[16,10,8,256]{3,2,0,1:T(8,128)} %bitcast.77) | data formatting | bytes 2621440 | tf_op jit(solution)/shard_map/transpose | solution.py:357
  3.1 7.0 %all-to-all-start.2 = ((f32[16,10,8,256]{3,2,1,0:T(8,128)}), f32[16,10,8,256]{3,2,1,0:T(8,128)S(1)}, u32[]{:S(2)}, u32[]{:S(2)}) async-start(f32[16,10,8,256]{3,2,1,0:T(8,128)} %copy.12), calls=%async_computation.2 | async-start | bytes 2621440 | tf_op jit(solution)/shard_map/all_to_all | solution.py:358
  11.1 0.6 compare_reduce_fusion
  13.2 0.6 reduce_max.9
  14.6 6.6 %fusion.8 = (bf16[1280,1280]{1,0:T(8,128)(2,1)}, bf16[1280,1280]{1,0:T(8,128)(2,1)}) fusion(f32[1280,1280]{1,0:T(8,128)} %param.8), kind=kLoop, calls=%fused_computation.56 | loop fusion | flops 6553600 | bytes 13107200 | tf_op jit(solution)/shard_map/convert_element_type | solution.py:361
  21.2 7.6 %all-to-all-done.2 = f32[16,10,8,256]{3,2,1,0:T(8,128)S(1)} async-done(((f32[16,10,8,256]{3,2,1,0:T(8,128)}), f32[16,10,8,256]{3,2,1,0:T(8,128)S(1)}, u32[]{:S(2)}, u32[]{:S(2)}) %all-to-all-start.2) | async-done | bytes 1310752 | tf_op jit(solution)/shard_map/all_to_all | solution.py:358
  28.8 147.7 %conditional.1 = (f32[4,16,1280]{2,1,0:T(8,128)S(1)}, f32[4,16,1280]{2,1,0:T(8,128)S(1)}, f32[4,16,256]{2,1,0:T(8,128)S(1)}) conditional(s32[]{:T(128)} %clamp.3, (f32[16,10,8,256]{3,2,1,0:T(8,128)S(1)}, s32[362]{0:T(512)S(1)}, bf16[1280,1280]{1,0:T(8,128)(2,1)}, bf16[1280,1280]{1,0:T(8,128)(2,1)}) %tuple.16, (f32[16,10,8,256]{3,2,1,0:T(8,128)S(1)}, ...), branch_computations={%region_12.13_spmd, %region_13.15_spmd} | conditional | flops 5243044 | bytes 121374848 | solution.py:396
  28.8 0.7 branch_0_fun.5
  29.5 0.4 collective-permute-start
  30.1 5.9 %collective-permute-done = f32[28,8,256]{2,1,0:T(8,128)S(1)} collective-permute-done((f32[28,8,256]{2,1,0:T(8,128)S(1)}, f32[28,8,256]{2,1,0:T(8,128)S(1)}, u32[]{:S(2)}, u32[]{:S(2)}) %collective-permute-start) | collective-permute-done | bytes 229408 | tf_op jit(solution)/shard_map/cond/branch_0_fun/ppermute | solution.py:26
  36.0 1.4 collective-permute-start.4
  37.8 1.1 collective-permute-start.3
  39.0 2.5 %collective-permute-done.4 = f32[28,8,256]{2,1,0:T(8,128)S(1)} collective-permute-done((f32[28,8,256]{2,1,0:T(8,128)S(1)}, f32[28,8,256]{2,1,0:T(8,128)S(1)}, u32[]{:S(2)}, u32[]{:S(2)}) %collective-permute-start.4) | collective-permute-done | bytes 229408 | tf_op jit(solution)/shard_map/cond/branch_0_fun/ppermute | solution.py:31
  41.5 3.4 %collective-permute-start.6 = (f32[28,8,256]{2,1,0:T(8,128)S(1)}, f32[28,8,256]{2,1,0:T(8,128)S(1)}, u32[]{:S(2)}, u32[]{:S(2)}) collective-permute-start(f32[28,8,256]{2,1,0:T(8,128)S(1)} %collective-permute-done.4), channel_id=1, source_target_pairs={{0,6},{2,0},{4,2},{6,4},{1,7},{3,1},{5,3},{7,5},{8,14},{10,8},{12,... | collective-permute-start | bytes 688136 | tf_op jit(solution)/shard_map/cond/branch_0_fun/ppermute | solution.py:31
  44.9 1.5 collective-permute-done.2
  46.5 4.7 %collective-permute-start.7 = (f32[4,28,8,256]{3,2,1,0:T(8,128)S(1)}, f32[4,28,8,256]{3,2,1,0:T(8,128)S(1)}, u32[]{:S(2)}, u32[]{:S(2)}) collective-permute-start(f32[4,28,8,256]{3,2,1,0:T(8,128)S(1)} %pad_maximum_fusion.g0), channel_id=1, source_target_pairs={{0,1},{1,0},{2,3},{3,2},{4,5},{5,4},{6,7},{7,6},{8,9},{9,8},{10,11... | collective-permute-start | bytes 2752520 | tf_op jit(solution)/shard_map/cond/branch_0_fun/ppermute | solution.py:26
  51.4 2.6 %collective-permute-start.8 = (f32[4,28,8,256]{3,2,1,0:T(8,128)S(1)}, f32[4,28,8,256]{3,2,1,0:T(8,128)}, u32[]{:S(2)}, u32[]{:S(2)}) collective-permute-start(f32[4,28,8,256]{3,2,1,0:T(8,128)S(1)} %pad_maximum_fusion.1.g1), channel_id=1, source_target_pairs={{0,1},{1,0},{2,3},{3,2},{4,5},{5,4},{6,7},{7,6},{8,9},{9,8},{10,11... | collective-permute-start | bytes 2752520 | tf_op jit(solution)/shard_map/cond/branch_0_fun/ppermute | solution.py:26
  54.0 2.2 collective-permute-done.8.c1
  56.3 10.6 %branch_0_fun.6 = (f32[8,28,32,128]{3,2,1,0:T(8,128)S(1)}, bf16[28,128,256]{2,1,0:T(8,128)(2,1)S(1)}, bf16[28,128,256]{2,1,0:T(8,128)(2,1)S(1)}) custom-call(s32[362]{0:T(512)S(1)} %get-tuple-element.16.tab, f32[4,28,8,256]{3,2,1,0:T(8,128)S(1)} %pad_maximum_fusion.g0, f32[4,28,8,256]{3,2,1,0:T(8,128)S(1)} %pad_maximum_fusion.1.g1, ...), custom_call_target="tpu_custom_call" | custom-call | tf_op jit(solution)/shard_map/cond/branch_0_fun/pallas_call | solution.py:273
  66.9 1.3 copy-done.3
  68.2 1.2 copy-done.5
  69.7 1.5 copy-done
  71.2 8.9 %collective-permute-start.9 = (f32[14,32,128]{2,1,0:T(8,128)S(1)}, f32[14,32,128]{2,1,0:T(8,128)S(1)}, u32[]{:S(2)}, u32[]{:S(2)}) collective-permute-start(f32[14,32,128]{2,1,0:T(8,128)S(1)} %get-tuple-element.59), channel_id=1, source_target_pairs={{0,32},{32,64},{64,96},{96,128},{128,160},{160,192},{192,224},{224... | collective-permute-start | bytes 688136 | tf_op jit(solution)/shard_map/cond/branch_0_fun/ppermute | solution.py:31
  80.1 3.2 %collective-permute-start.16 = (f32[2,7,32,128]{3,2,1,0:T(8,128)S(1)}, f32[2,7,32,128]{3,2,1,0:T(8,128)S(1)}, u32[]{:S(2)}, u32[]{:S(2)}) collective-permute-start(f32[2,7,32,128]{3,2,1,0:T(8,128)S(1)} %bitcast.93), channel_id=1, source_target_pairs={{0,224},{32,0},{64,32},{96,64},{128,96},{160,128},{192,160},{224,1... | collective-permute-start | bytes 688136 | tf_op jit(solution)/shard_map/cond/branch_0_fun/ppermute | solution.py:31
  83.3 3.4 %collective-permute-done.9 = f32[14,32,128]{2,1,0:T(8,128)S(1)} collective-permute-done((f32[14,32,128]{2,1,0:T(8,128)S(1)}, f32[14,32,128]{2,1,0:T(8,128)S(1)}, u32[]{:S(2)}, u32[]{:S(2)}) %collective-permute-start.9) | collective-permute-done | bytes 229408 | tf_op jit(solution)/shard_map/cond/branch_0_fun/ppermute | solution.py:31
  86.7 1.0 fusion.6
  87.8 2.7 %collective-permute-start.17 = (f32[2,7,32,128]{3,2,1,0:T(8,128)S(1)}, f32[2,7,32,128]{3,2,1,0:T(8,128)S(1)}, u32[]{:S(2)}, u32[]{:S(2)}) collective-permute-start(f32[2,7,32,128]{3,2,1,0:T(8,128)S(1)} %add.525), channel_id=1, source_target_pairs={{0,224},{32,0},{64,32},{96,64},{128,96},{160,128},{192,160},{224,1... | collective-permute-start | bytes 688136 | tf_op jit(solution)/shard_map/cond/branch_0_fun/ppermute | solution.py:31
  90.5 3.3 %collective-permute-done.10 = f32[14,32,128]{2,1,0:T(8,128)S(1)} collective-permute-done((f32[14,32,128]{2,1,0:T(8,128)S(1)}, f32[14,32,128]{2,1,0:T(8,128)S(1)}, u32[]{:S(2)}, u32[]{:S(2)}) %collective-permute-start.10) | collective-permute-done | bytes 229408 | tf_op jit(solution)/shard_map/cond/branch_0_fun/ppermute | solution.py:31
  93.8 1.0 fusion.5
  95.0 2.7 %collective-permute-start.18 = (f32[2,7,32,128]{3,2,1,0:T(8,128)S(1)}, f32[2,7,32,128]{3,2,1,0:T(8,128)S(1)}, u32[]{:S(2)}, u32[]{:S(2)}) collective-permute-start(f32[2,7,32,128]{3,2,1,0:T(8,128)S(1)} %add.529), channel_id=1, source_target_pairs={{0,224},{32,0},{64,32},{96,64},{128,96},{160,128},{192,160},{224,1... | collective-permute-start | bytes 688136 | tf_op jit(solution)/shard_map/cond/branch_0_fun/ppermute | solution.py:31
  97.7 3.7 %collective-permute-done.11 = f32[14,32,128]{2,1,0:T(8,128)S(1)} collective-permute-done((f32[14,32,128]{2,1,0:T(8,128)S(1)}, f32[14,32,128]{2,1,0:T(8,128)S(1)}, u32[]{:S(2)}, u32[]{:S(2)}) %collective-permute-start.11) | collective-permute-done | bytes 229408 | tf_op jit(solution)/shard_map/cond/branch_0_fun/ppermute | solution.py:31
  101.4 1.0 fusion.4
  102.5 2.7 %collective-permute-start.19 = (f32[2,7,32,128]{3,2,1,0:T(8,128)S(1)}, f32[2,7,32,128]{3,2,1,0:T(8,128)S(1)}, u32[]{:S(2)}, u32[]{:S(2)}) collective-permute-start(f32[2,7,32,128]{3,2,1,0:T(8,128)S(1)} %add.533), channel_id=1, source_target_pairs={{0,224},{32,0},{64,32},{96,64},{128,96},{160,128},{192,160},{224,1... | collective-permute-start | bytes 688136 | tf_op jit(solution)/shard_map/cond/branch_0_fun/ppermute | solution.py:31
  105.2 4.8 %collective-permute-done.12 = f32[14,32,128]{2,1,0:T(8,128)S(1)} collective-permute-done((f32[14,32,128]{2,1,0:T(8,128)S(1)}, f32[14,32,128]{2,1,0:T(8,128)S(1)}, u32[]{:S(2)}, u32[]{:S(2)}) %collective-permute-start.12) | collective-permute-done | bytes 229408 | tf_op jit(solution)/shard_map/cond/branch_0_fun/ppermute | solution.py:31
  110.1 1.0 fusion.3
  111.2 2.7 %collective-permute-start.20 = (f32[2,7,32,128]{3,2,1,0:T(8,128)S(1)}, f32[2,7,32,128]{3,2,1,0:T(8,128)S(1)}, u32[]{:S(2)}, u32[]{:S(2)}) collective-permute-start(f32[2,7,32,128]{3,2,1,0:T(8,128)S(1)} %add.537), channel_id=1, source_target_pairs={{0,224},{32,0},{64,32},{96,64},{128,96},{160,128},{192,160},{224,1... | collective-permute-start | bytes 688136 | tf_op jit(solution)/shard_map/cond/branch_0_fun/ppermute | solution.py:31
  113.9 5.8 %collective-permute-done.13 = f32[14,32,128]{2,1,0:T(8,128)S(1)} collective-permute-done((f32[14,32,128]{2,1,0:T(8,128)S(1)}, f32[14,32,128]{2,1,0:T(8,128)S(1)}, u32[]{:S(2)}, u32[]{:S(2)}) %collective-permute-start.13) | collective-permute-done | bytes 229408 | tf_op jit(solution)/shard_map/cond/branch_0_fun/ppermute | solution.py:31
  119.7 1.0 fusion.2
  120.8 2.7 %collective-permute-start.21 = (f32[2,7,32,128]{3,2,1,0:T(8,128)S(1)}, f32[2,7,32,128]{3,2,1,0:T(8,128)S(1)}, u32[]{:S(2)}, u32[]{:S(2)}) collective-permute-start(f32[2,7,32,128]{3,2,1,0:T(8,128)S(1)} %add.541), channel_id=1, source_target_pairs={{0,224},{32,0},{64,32},{96,64},{128,96},{160,128},{192,160},{224,1... | collective-permute-start | bytes 688136 | tf_op jit(solution)/shard_map/cond/branch_0_fun/ppermute | solution.py:31
  123.6 4.9 %collective-permute-done.14 = f32[14,32,128]{2,1,0:T(8,128)S(1)} collective-permute-done((f32[14,32,128]{2,1,0:T(8,128)S(1)}, f32[14,32,128]{2,1,0:T(8,128)S(1)}, u32[]{:S(2)}, u32[]{:S(2)}) %collective-permute-start.14) | collective-permute-done | bytes 229408 | tf_op jit(solution)/shard_map/cond/branch_0_fun/ppermute | solution.py:31
  128.5 1.0 fusion.1
  129.6 2.7 %collective-permute-start.22 = (f32[2,7,32,128]{3,2,1,0:T(8,128)S(1)}, f32[2,7,32,128]{3,2,1,0:T(8,128)S(1)}, u32[]{:S(2)}, u32[]{:S(2)}) collective-permute-start(f32[2,7,32,128]{3,2,1,0:T(8,128)S(1)} %add.545), channel_id=1, source_target_pairs={{0,224},{32,0},{64,32},{96,64},{128,96},{160,128},{192,160},{224,1... | collective-permute-start | bytes 688136 | tf_op jit(solution)/shard_map/cond/branch_0_fun/ppermute | solution.py:31
  132.3 4.0 %collective-permute-done.15 = f32[14,32,128]{2,1,0:T(8,128)S(1)} collective-permute-done((f32[14,32,128]{2,1,0:T(8,128)S(1)}, f32[14,32,128]{2,1,0:T(8,128)S(1)}, u32[]{:S(2)}, u32[]{:S(2)}) %collective-permute-start.15) | collective-permute-done | bytes 229408 | tf_op jit(solution)/shard_map/cond/branch_0_fun/ppermute | solution.py:31
  136.4 1.0 fusion
  137.6 12.3 %collective-permute-start.25 = (f32[28,16,128]{2,1,0:T(8,128)S(1)}, f32[28,16,128]{2,1,0:T(8,128)S(1)}, u32[]{:S(2)}, u32[]{:S(2)}) collective-permute-start(f32[28,16,128]{2,1,0:T(8,128)S(1)} %pad_maximum_fusion.3), channel_id=1, source_target_pairs={{0,31},{1,30},{2,29},{3,28},{4,27},{5,26},{6,25},{7,24},{8,23},{9,... | collective-permute-start | bytes 688136 | tf_op jit(solution)/shard_map/cond/branch_0_fun/ppermute | solution.py:310
  150.0 2.1 collective-permute-start.24
  152.0 0.9 collective-permute-done.25
  152.9 6.1 %collective-permute-done.24 = f32[28,16,128]{2,1,0:T(8,128)S(1)} collective-permute-done((f32[28,16,128]{2,1,0:T(8,128)S(1)}, f32[28,16,128]{2,1,0:T(8,128)S(1)}, u32[]{:S(2)}, u32[]{:S(2)}) %collective-permute-start.24) | collective-permute-done | bytes 229408 | tf_op jit(solution)/shard_map/cond/branch_0_fun/ppermute | solution.py:310
  159.0 1.9 collective-permute-start.26
  161.0 0.7 branch_0_fun.7
  161.6 11.3 %collective-permute-done.26.x_ref = f32[28,16,128]{2,1,0:T(8,128)S(1)} collective-permute-done((f32[28,16,128]{2,1,0:T(8,128)S(1)}, f32[28,16,128]{2,1,0:T(8,128)S(1)}, u32[]{:S(2)}, u32[]{:S(2)}) %collective-permute-start.26) | collective-permute-done | bytes 229408 | tf_op jit(solution)/shard_map/cond/branch_0_fun/ppermute | solution.py:311
  172.9 0.7 branch_0_fun.8
  173.6 2.7 %branch_0_fun.9 = f32[4,16,256]{2,1,0:T(8,128)S(1)} custom-call(s32[362]{0:T(512)S(1)} %get-tuple-element.16.tab, f32[28,16,128]{2,1,0:T(8,128)S(1)} %collective-permute-done.26.x_ref, bf16[28,128,256]{2,1,0:T(8,128)(2,1)S(1)} %copy-done.4, bf16[28,128,256]{2,1,0:T(8,128)(2,1)S(1)} %copy-done.6), custom_call_target="tpu_custom_call" | custom-call | tf_op jit(solution)/shard_map/cond/branch_0_fun/pallas_call | solution.py:322
  176.5 1.2 collective-permute-start.31
  177.7 3.2 %collective-permute-start.32 = (f32[4,16,256]{2,1,0:T(8,128)S(1)}, f32[4,16,256]{2,1,0:T(8,128)S(1)}, u32[]{:S(2)}, u32[]{:S(2)}) collective-permute-start(f32[4,16,256]{2,1,0:T(8,128)S(1)} %get-tuple-element.40), channel_id=1, source_target_pairs={{0,46},{1,47},{2,32},{3,33},{4,34},{5,35},{6,36},{7,37},{8,38},{9,... | collective-permute-start | bytes 196616 | tf_op jit(solution)/shard_map/ppermute | solution.py:412
  180.9 2.5 %collective-permute-start.33 = (f32[4,16,256]{2,1,0:T(8,128)S(1)}, f32[4,16,256]{2,1,0:T(8,128)S(1)}, u32[]{:S(2)}, u32[]{:S(2)}) collective-permute-start(f32[4,16,256]{2,1,0:T(8,128)S(1)} %get-tuple-element.40), channel_id=1, source_target_pairs={{0,61},{1,62},{2,63},{3,48},{4,49},{5,50},{6,51},{7,52},{8,53},{9,... | collective-permute-start | bytes 196616 | tf_op jit(solution)/shard_map/ppermute | solution.py:412
  183.4 0.6 collective-permute-done.32
  184.0 4.8 %collective-permute-done.33 = f32[4,16,256]{2,1,0:T(8,128)S(1)} collective-permute-done((f32[4,16,256]{2,1,0:T(8,128)S(1)}, f32[4,16,256]{2,1,0:T(8,128)S(1)}, u32[]{:S(2)}, u32[]{:S(2)}) %collective-permute-start.33) | collective-permute-done | bytes 65568 | tf_op jit(solution)/shard_map/ppermute | solution.py:412
  188.9 2.2 collective-permute-start.35
  191.1 6.8 %collective-permute-start.36 = (f32[4,16,256]{2,1,0:T(8,128)S(1)}, f32[4,16,256]{2,1,0:T(8,128)S(1)}, u32[]{:S(2)}, u32[]{:S(2)}) collective-permute-start(f32[4,16,256]{2,1,0:T(8,128)S(1)} %add_add_fusion.1), channel_id=1, source_target_pairs={{0,196},{1,197},{2,198},{3,199},{4,200},{5,201},{6,202},{7,203},{8... | collective-permute-start | bytes 196616 | tf_op jit(solution)/shard_map/ppermute | solution.py:412
  197.9 2.8 %collective-permute-done.36 = f32[4,16,256]{2,1,0:T(8,128)S(1)} collective-permute-done((f32[4,16,256]{2,1,0:T(8,128)S(1)}, f32[4,16,256]{2,1,0:T(8,128)S(1)}, u32[]{:S(2)}, u32[]{:S(2)}) %collective-permute-start.36) | collective-permute-done | bytes 65568 | tf_op jit(solution)/shard_map/ppermute | solution.py:412
  200.7 0.7 shard_map.85
  201.5 31.7 %all_to_all.18.x_ref = f32[16,16,1536]{2,1,0:T(8,128)S(1)} all-to-all(f32[16,16,1536]{2,1,0:T(8,128)S(1)} %shard_map.85), channel_id=1, replica_groups=mesh['row_0'=8,'row_1'=2,'col_y'=2,'col_x'=4,'core'=2] {'col_y','col_x',..., dimensions={0} | all-to-all | bytes 3145728 | tf_op jit(solution)/shard_map/all_to_all | solution.py:421
  233.2 2.0 shard_map.86
  (92 shorter events, 3.9 us)
Async XLA Ops:
  3.1 7.0 %copy-start.12 = (s32[4]{0:T(128)S(1)}, s32[4]{0:T(128)}, u32[]{:S(2)}) copy-start(s32[4]{0:T(128)} %param.12) | copy-start | bytes 52
  3.1 7.0 %copy-start.11 = (s32[4,96]{1,0:T(4,128)S(1)}, s32[4,96]{1,0:T(4,128)}, u32[]{:S(2)}) copy-start(s32[4,96]{1,0:T(4,128)} %param.11) | copy-start | bytes 4612
  3.1 7.9 %copy-start.13 = (s32[4]{0:T(128)S(1)}, s32[4]{0:T(128)}, u32[]{:S(2)}) copy-start(s32[4]{0:T(128)} %param.13) | copy-start | bytes 52
  3.1 25.6 %all-to-all-start.2 = ((f32[16,10,8,256]{3,2,1,0:T(8,128)}), f32[16,10,8,256]{3,2,1,0:T(8,128)S(1)}, u32[]{:S(2)}, u32[]{:S(2)}) async-start(f32[16,10,8,256]{3,2,1,0:T(8,128)} %copy.12), calls=%async_computation.2 | async-start | bytes 2621440 | tf_op jit(solution)/shard_map/all_to_all | solution.py:358
  29.5 6.5 %collective-permute-start = (f32[28,8,256]{2,1,0:T(8,128)S(1)}, f32[28,8,256]{2,1,0:T(8,128)S(1)}, u32[]{:S(2)}, u32[]{:S(2)}) collective-permute-start(f32[28,8,256]{2,1,0:T(8,128)S(1)} %branch_0_fun.5), channel_id=1, source_target_pairs={{0,8},{8,0},{1,9},{9,1},{2,10},{10,2},{3,11},{11,3},{4,12},{12,4},... | collective-permute-start | bytes 688136 | tf_op jit(solution)/shard_map/cond/branch_0_fun/ppermute | solution.py:26
  29.9 9.1 %collective-permute-start.1 = (f32[28,8,256]{2,1,0:T(8,128)S(1)}, f32[28,8,256]{2,1,0:T(8,128)S(1)}, u32[]{:S(2)}, u32[]{:S(2)}) collective-permute-start(f32[28,8,256]{2,1,0:T(8,128)S(1)} %branch_0_fun.5), channel_id=1, source_target_pairs={{0,2},{2,4},{4,6},{6,0},{1,3},{3,5},{5,7},{7,1},{8,10},{10,12},{12... | collective-permute-start | bytes 688136 | tf_op jit(solution)/shard_map/cond/branch_0_fun/ppermute | solution.py:31
  36.0 5.5 %collective-permute-start.4 = (f32[28,8,256]{2,1,0:T(8,128)S(1)}, f32[28,8,256]{2,1,0:T(8,128)S(1)}, u32[]{:S(2)}, u32[]{:S(2)}) collective-permute-start(f32[28,8,256]{2,1,0:T(8,128)S(1)} %collective-permute-done), channel_id=1, source_target_pairs={{0,6},{2,0},{4,2},{6,4},{1,7},{3,1},{5,3},{7,5},{8,14},{10,8},{12,... | collective-permute-start | bytes 688136 | tf_op jit(solution)/shard_map/cond/branch_0_fun/ppermute | solution.py:31
  37.5 9.0 %collective-permute-start.2 = (f32[28,8,256]{2,1,0:T(8,128)S(1)}, f32[28,8,256]{2,1,0:T(8,128)S(1)}, u32[]{:S(2)}, u32[]{:S(2)}) collective-permute-start(f32[28,8,256]{2,1,0:T(8,128)S(1)} %branch_0_fun.5), channel_id=1, source_target_pairs={{0,6},{2,0},{4,2},{6,4},{1,7},{3,1},{5,3},{7,5},{8,14},{10,8},{12,... | collective-permute-start | bytes 688136 | tf_op jit(solution)/shard_map/cond/branch_0_fun/ppermute | solution.py:31
  37.8 13.5 %collective-permute-start.3 = (f32[28,8,256]{2,1,0:T(8,128)S(1)}, f32[28,8,256]{2,1,0:T(8,128)S(1)}, u32[]{:S(2)}, u32[]{:S(2)}) collective-permute-start(f32[28,8,256]{2,1,0:T(8,128)S(1)} %collective-permute-done), channel_id=1, source_target_pairs={{0,2},{2,4},{4,6},{6,0},{1,3},{3,5},{5,7},{7,1},{8,10},{10,12},{12... | collective-permute-start | bytes 688136 | tf_op jit(solution)/shard_map/cond/branch_0_fun/ppermute | solution.py:31
  38.9 12.3 %collective-permute-start.5 = (f32[28,8,256]{2,1,0:T(8,128)S(1)}, f32[28,8,256]{2,1,0:T(8,128)S(1)}, u32[]{:S(2)}, u32[]{:S(2)}) collective-permute-start(f32[28,8,256]{2,1,0:T(8,128)S(1)} %collective-permute-done.1), channel_id=1, source_target_pairs={{0,2},{2,4},{4,6},{6,0},{1,3},{3,5},{5,7},{7,1},{8,10},{10,12},{12... | collective-permute-start | bytes 688136 | tf_op jit(solution)/shard_map/cond/branch_0_fun/ppermute | solution.py:31
  41.5 9.8 %collective-permute-start.6 = (f32[28,8,256]{2,1,0:T(8,128)S(1)}, f32[28,8,256]{2,1,0:T(8,128)S(1)}, u32[]{:S(2)}, u32[]{:S(2)}) collective-permute-start(f32[28,8,256]{2,1,0:T(8,128)S(1)} %collective-permute-done.4), channel_id=1, source_target_pairs={{0,6},{2,0},{4,2},{6,4},{1,7},{3,1},{5,3},{7,5},{8,14},{10,8},{12,... | collective-permute-start | bytes 688136 | tf_op jit(solution)/shard_map/cond/branch_0_fun/ppermute | solution.py:31
  46.5 7.5 %collective-permute-start.7 = (f32[4,28,8,256]{3,2,1,0:T(8,128)S(1)}, f32[4,28,8,256]{3,2,1,0:T(8,128)S(1)}, u32[]{:S(2)}, u32[]{:S(2)}) collective-permute-start(f32[4,28,8,256]{3,2,1,0:T(8,128)S(1)} %pad_maximum_fusion.g0), channel_id=1, source_target_pairs={{0,1},{1,0},{2,3},{3,2},{4,5},{5,4},{6,7},{7,6},{8,9},{9,8},{10,11... | collective-permute-start | bytes 2752520 | tf_op jit(solution)/shard_map/cond/branch_0_fun/ppermute | solution.py:26
  51.4 4.8 %collective-permute-start.8 = (f32[4,28,8,256]{3,2,1,0:T(8,128)S(1)}, f32[4,28,8,256]{3,2,1,0:T(8,128)}, u32[]{:S(2)}, u32[]{:S(2)}) collective-permute-start(f32[4,28,8,256]{3,2,1,0:T(8,128)S(1)} %pad_maximum_fusion.1.g1), channel_id=1, source_target_pairs={{0,1},{1,0},{2,3},{3,2},{4,5},{5,4},{6,7},{7,6},{8,9},{9,8},{10,11... | collective-permute-start | bytes 2752520 | tf_op jit(solution)/shard_map/cond/branch_0_fun/ppermute | solution.py:26
  66.9 1.3 copy-start.3
  68.2 1.2 copy-start.5
  69.4 1.8 copy-start
  71.2 15.5 %collective-permute-start.9 = (f32[14,32,128]{2,1,0:T(8,128)S(1)}, f32[14,32,128]{2,1,0:T(8,128)S(1)}, u32[]{:S(2)}, u32[]{:S(2)}) collective-permute-start(f32[14,32,128]{2,1,0:T(8,128)S(1)} %get-tuple-element.59), channel_id=1, source_target_pairs={{0,32},{32,64},{64,96},{96,128},{128,160},{160,192},{192,224},{224... | collective-permute-start | bytes 688136 | tf_op jit(solution)/shard_map/cond/branch_0_fun/ppermute | solution.py:31
  80.1 7.7 %collective-permute-start.16 = (f32[2,7,32,128]{3,2,1,0:T(8,128)S(1)}, f32[2,7,32,128]{3,2,1,0:T(8,128)S(1)}, u32[]{:S(2)}, u32[]{:S(2)}) collective-permute-start(f32[2,7,32,128]{3,2,1,0:T(8,128)S(1)} %bitcast.93), channel_id=1, source_target_pairs={{0,224},{32,0},{64,32},{96,64},{128,96},{160,128},{192,160},{224,1... | collective-permute-start | bytes 688136 | tf_op jit(solution)/shard_map/cond/branch_0_fun/ppermute | solution.py:31
  87.7 6.2 %collective-permute-start.10 = (f32[14,32,128]{2,1,0:T(8,128)S(1)}, f32[14,32,128]{2,1,0:T(8,128)S(1)}, u32[]{:S(2)}, u32[]{:S(2)}) collective-permute-start(f32[14,32,128]{2,1,0:T(8,128)S(1)} %fusion.6), channel_id=1, source_target_pairs={{0,32},{32,64},{64,96},{96,128},{128,160},{160,192},{192,224},{224... | collective-permute-start | bytes 688136 | tf_op jit(solution)/shard_map/cond/branch_0_fun/ppermute | solution.py:31
  87.8 7.1 %collective-permute-start.17 = (f32[2,7,32,128]{3,2,1,0:T(8,128)S(1)}, f32[2,7,32,128]{3,2,1,0:T(8,128)S(1)}, u32[]{:S(2)}, u32[]{:S(2)}) collective-permute-start(f32[2,7,32,128]{3,2,1,0:T(8,128)S(1)} %add.525), channel_id=1, source_target_pairs={{0,224},{32,0},{64,32},{96,64},{128,96},{160,128},{192,160},{224,1... | collective-permute-start | bytes 688136 | tf_op jit(solution)/shard_map/cond/branch_0_fun/ppermute | solution.py:31
  94.8 6.6 %collective-permute-start.11 = (f32[14,32,128]{2,1,0:T(8,128)S(1)}, f32[14,32,128]{2,1,0:T(8,128)S(1)}, u32[]{:S(2)}, u32[]{:S(2)}) collective-permute-start(f32[14,32,128]{2,1,0:T(8,128)S(1)} %fusion.5), channel_id=1, source_target_pairs={{0,32},{32,64},{64,96},{96,128},{128,160},{160,192},{192,224},{224... | collective-permute-start | bytes 688136 | tf_op jit(solution)/shard_map/cond/branch_0_fun/ppermute | solution.py:31
  95.0 7.5 %collective-permute-start.18 = (f32[2,7,32,128]{3,2,1,0:T(8,128)S(1)}, f32[2,7,32,128]{3,2,1,0:T(8,128)S(1)}, u32[]{:S(2)}, u32[]{:S(2)}) collective-permute-start(f32[2,7,32,128]{3,2,1,0:T(8,128)S(1)} %add.529), channel_id=1, source_target_pairs={{0,224},{32,0},{64,32},{96,64},{128,96},{160,128},{192,160},{224,1... | collective-permute-start | bytes 688136 | tf_op jit(solution)/shard_map/cond/branch_0_fun/ppermute | solution.py:31
  102.4 7.7 %collective-permute-start.12 = (f32[14,32,128]{2,1,0:T(8,128)S(1)}, f32[14,32,128]{2,1,0:T(8,128)S(1)}, u32[]{:S(2)}, u32[]{:S(2)}) collective-permute-start(f32[14,32,128]{2,1,0:T(8,128)S(1)} %fusion.4), channel_id=1, source_target_pairs={{0,32},{32,64},{64,96},{96,128},{128,160},{160,192},{192,224},{224... | collective-permute-start | bytes 688136 | tf_op jit(solution)/shard_map/cond/branch_0_fun/ppermute | solution.py:31
  102.5 8.6 %collective-permute-start.19 = (f32[2,7,32,128]{3,2,1,0:T(8,128)S(1)}, f32[2,7,32,128]{3,2,1,0:T(8,128)S(1)}, u32[]{:S(2)}, u32[]{:S(2)}) collective-permute-start(f32[2,7,32,128]{3,2,1,0:T(8,128)S(1)} %add.533), channel_id=1, source_target_pairs={{0,224},{32,0},{64,32},{96,64},{128,96},{160,128},{192,160},{224,1... | collective-permute-start | bytes 688136 | tf_op jit(solution)/shard_map/cond/branch_0_fun/ppermute | solution.py:31
  111.0 8.7 %collective-permute-start.13 = (f32[14,32,128]{2,1,0:T(8,128)S(1)}, f32[14,32,128]{2,1,0:T(8,128)S(1)}, u32[]{:S(2)}, u32[]{:S(2)}) collective-permute-start(f32[14,32,128]{2,1,0:T(8,128)S(1)} %fusion.3), channel_id=1, source_target_pairs={{0,32},{32,64},{64,96},{96,128},{128,160},{160,192},{192,224},{224... | collective-permute-start | bytes 688136 | tf_op jit(solution)/shard_map/cond/branch_0_fun/ppermute | solution.py:31
  111.2 9.6 %collective-permute-start.20 = (f32[2,7,32,128]{3,2,1,0:T(8,128)S(1)}, f32[2,7,32,128]{3,2,1,0:T(8,128)S(1)}, u32[]{:S(2)}, u32[]{:S(2)}) collective-permute-start(f32[2,7,32,128]{3,2,1,0:T(8,128)S(1)} %add.537), channel_id=1, source_target_pairs={{0,224},{32,0},{64,32},{96,64},{128,96},{160,128},{192,160},{224,1... | collective-permute-start | bytes 688136 | tf_op jit(solution)/shard_map/cond/branch_0_fun/ppermute | solution.py:31
  120.7 7.8 %collective-permute-start.14 = (f32[14,32,128]{2,1,0:T(8,128)S(1)}, f32[14,32,128]{2,1,0:T(8,128)S(1)}, u32[]{:S(2)}, u32[]{:S(2)}) collective-permute-start(f32[14,32,128]{2,1,0:T(8,128)S(1)} %fusion.2), channel_id=1, source_target_pairs={{0,32},{32,64},{64,96},{96,128},{128,160},{160,192},{192,224},{224... | collective-permute-start | bytes 688136 | tf_op jit(solution)/shard_map/cond/branch_0_fun/ppermute | solution.py:31
  120.8 8.7 %collective-permute-start.21 = (f32[2,7,32,128]{3,2,1,0:T(8,128)S(1)}, f32[2,7,32,128]{3,2,1,0:T(8,128)S(1)}, u32[]{:S(2)}, u32[]{:S(2)}) collective-permute-start(f32[2,7,32,128]{3,2,1,0:T(8,128)S(1)} %add.541), channel_id=1, source_target_pairs={{0,224},{32,0},{64,32},{96,64},{128,96},{160,128},{192,160},{224,1... | collective-permute-start | bytes 688136 | tf_op jit(solution)/shard_map/cond/branch_0_fun/ppermute | solution.py:31
  129.5 6.9 %collective-permute-start.15 = (f32[14,32,128]{2,1,0:T(8,128)S(1)}, f32[14,32,128]{2,1,0:T(8,128)S(1)}, u32[]{:S(2)}, u32[]{:S(2)}) collective-permute-start(f32[14,32,128]{2,1,0:T(8,128)S(1)} %fusion.1), channel_id=1, source_target_pairs={{0,32},{32,64},{64,96},{96,128},{128,160},{160,192},{192,224},{224... | collective-permute-start | bytes 688136 | tf_op jit(solution)/shard_map/cond/branch_0_fun/ppermute | solution.py:31
  129.6 7.7 %collective-permute-start.22 = (f32[2,7,32,128]{3,2,1,0:T(8,128)S(1)}, f32[2,7,32,128]{3,2,1,0:T(8,128)S(1)}, u32[]{:S(2)}, u32[]{:S(2)}) collective-permute-start(f32[2,7,32,128]{3,2,1,0:T(8,128)S(1)} %add.545), channel_id=1, source_target_pairs={{0,224},{32,0},{64,32},{96,64},{128,96},{160,128},{192,160},{224,1... | collective-permute-start | bytes 688136 | tf_op jit(solution)/shard_map/cond/branch_0_fun/ppermute | solution.py:31
  137.4 36.2 %copy-start.6 = (bf16[28,128,256]{2,1,0:T(8,128)(2,1)S(1)}, bf16[28,128,256]{2,1,0:T(8,128)(2,1)}, u32[]{:S(2)}) copy-start(bf16[28,128,256]{2,1,0:T(8,128)(2,1)} %copy-done.5) | copy-start | bytes 5505028 | tf_op jit(solution)/shard_map/cond
  137.5 12.5 %collective-permute-start.23 = (f32[28,16,128]{2,1,0:T(8,128)S(1)}, f32[28,16,128]{2,1,0:T(8,128)S(1)}, u32[]{:S(2)}, u32[]{:S(2)}) collective-permute-start(f32[28,16,128]{2,1,0:T(8,128)S(1)} %pad_maximum_fusion.3), channel_id=1, source_target_pairs={{0,16},{16,0},{1,17},{17,1},{2,18},{18,2},{3,19},{19,3},{4,20},{20... | collective-permute-start | bytes 688136 | tf_op jit(solution)/shard_map/cond/branch_0_fun/ppermute | solution.py:26
  137.6 15.3 %collective-permute-start.25 = (f32[28,16,128]{2,1,0:T(8,128)S(1)}, f32[28,16,128]{2,1,0:T(8,128)S(1)}, u32[]{:S(2)}, u32[]{:S(2)}) collective-permute-start(f32[28,16,128]{2,1,0:T(8,128)S(1)} %pad_maximum_fusion.3), channel_id=1, source_target_pairs={{0,31},{1,30},{2,29},{3,28},{4,27},{5,26},{6,25},{7,24},{8,23},{9,... | collective-permute-start | bytes 688136 | tf_op jit(solution)/shard_map/cond/branch_0_fun/ppermute | solution.py:310
  149.9 23.7 %copy-start.4 = (bf16[28,128,256]{2,1,0:T(8,128)(2,1)S(1)}, bf16[28,128,256]{2,1,0:T(8,128)(2,1)}, u32[]{:S(2)}) copy-start(bf16[28,128,256]{2,1,0:T(8,128)(2,1)} %copy-done.3) | copy-start | bytes 5505028 | tf_op jit(solution)/shard_map/cond
  150.0 9.0 %collective-permute-start.24 = (f32[28,16,128]{2,1,0:T(8,128)S(1)}, f32[28,16,128]{2,1,0:T(8,128)S(1)}, u32[]{:S(2)}, u32[]{:S(2)}) collective-permute-start(f32[28,16,128]{2,1,0:T(8,128)S(1)} %get-tuple-element.68), channel_id=1, source_target_pairs={{0,0},{1,15},{2,14},{3,13},{4,12},{5,11},{6,10},{7,9},{8,8},{9,7},... | collective-permute-start | bytes 688136 | tf_op jit(solution)/shard_map/cond/branch_0_fun/ppermute | solution.py:310
  159.0 13.9 %collective-permute-start.26 = (f32[28,16,128]{2,1,0:T(8,128)S(1)}, f32[28,16,128]{2,1,0:T(8,128)S(1)}, u32[]{:S(2)}, u32[]{:S(2)}) collective-permute-start(f32[28,16,128]{2,1,0:T(8,128)S(1)} %add.552), channel_id=1, source_target_pairs={{0,0},{1,241},{2,226},{3,211},{4,196},{5,181},{6,166},{7,151},{8,1... | collective-permute-start | bytes 688136 | tf_op jit(solution)/shard_map/cond/branch_0_fun/ppermute | solution.py:311
  176.5 25.0 %copy-start.10 = (f32[4,16,1280]{2,1,0:T(8,128)}, f32[4,16,1280]{2,1,0:T(8,128)S(1)}, u32[]{:S(2)}) copy-start(f32[4,16,1280]{2,1,0:T(8,128)S(1)} %get-tuple-element.35) | copy-start | bytes 983044
  176.5 6.9 %collective-permute-start.31 = (f32[4,16,256]{2,1,0:T(8,128)S(1)}, f32[4,16,256]{2,1,0:T(8,128)S(1)}, u32[]{:S(2)}, u32[]{:S(2)}) collective-permute-start(f32[4,16,256]{2,1,0:T(8,128)S(1)} %get-tuple-element.40), channel_id=1, source_target_pairs={{0,31},{1,16},{2,17},{3,18},{4,19},{5,20},{6,21},{7,22},{8,23},{9,... | collective-permute-start | bytes 196616 | tf_op jit(solution)/shard_map/ppermute | solution.py:412
  177.7 6.3 %collective-permute-start.32 = (f32[4,16,256]{2,1,0:T(8,128)S(1)}, f32[4,16,256]{2,1,0:T(8,128)S(1)}, u32[]{:S(2)}, u32[]{:S(2)}) collective-permute-start(f32[4,16,256]{2,1,0:T(8,128)S(1)} %get-tuple-element.40), channel_id=1, source_target_pairs={{0,46},{1,47},{2,32},{3,33},{4,34},{5,35},{6,36},{7,37},{8,38},{9,... | collective-permute-start | bytes 196616 | tf_op jit(solution)/shard_map/ppermute | solution.py:412
  180.9 7.9 %collective-permute-start.33 = (f32[4,16,256]{2,1,0:T(8,128)S(1)}, f32[4,16,256]{2,1,0:T(8,128)S(1)}, u32[]{:S(2)}, u32[]{:S(2)}) collective-permute-start(f32[4,16,256]{2,1,0:T(8,128)S(1)} %get-tuple-element.40), channel_id=1, source_target_pairs={{0,61},{1,62},{2,63},{3,48},{4,49},{5,50},{6,51},{7,52},{8,53},{9,... | collective-permute-start | bytes 196616 | tf_op jit(solution)/shard_map/ppermute | solution.py:412
  188.8 9.1 %collective-permute-start.34 = (f32[4,16,256]{2,1,0:T(8,128)S(1)}, f32[4,16,256]{2,1,0:T(8,128)S(1)}, u32[]{:S(2)}, u32[]{:S(2)}) collective-permute-start(f32[4,16,256]{2,1,0:T(8,128)S(1)} %add_add_fusion.1), channel_id=1, source_target_pairs={{0,76},{1,77},{2,78},{3,79},{4,64},{5,65},{6,66},{7,67},{8,68},{9,... | collective-permute-start | bytes 196616 | tf_op jit(solution)/shard_map/ppermute | solution.py:412
  188.9 9.0 %collective-permute-start.35 = (f32[4,16,256]{2,1,0:T(8,128)S(1)}, f32[4,16,256]{2,1,0:T(8,128)S(1)}, u32[]{:S(2)}, u32[]{:S(2)}) collective-permute-start(f32[4,16,256]{2,1,0:T(8,128)S(1)} %add_add_fusion.1), channel_id=1, source_target_pairs={{0,136},{1,137},{2,138},{3,139},{4,140},{5,141},{6,142},{7,143},{8... | collective-permute-start | bytes 196616 | tf_op jit(solution)/shard_map/ppermute | solution.py:412
  191.1 9.6 %collective-permute-start.36 = (f32[4,16,256]{2,1,0:T(8,128)S(1)}, f32[4,16,256]{2,1,0:T(8,128)S(1)}, u32[]{:S(2)}, u32[]{:S(2)}) collective-permute-start(f32[4,16,256]{2,1,0:T(8,128)S(1)} %add_add_fusion.1), channel_id=1, source_target_pairs={{0,196},{1,197},{2,198},{3,199},{4,200},{5,201},{6,202},{7,203},{8... | collective-permute-start | bytes 196616 | tf_op jit(solution)/shard_map/ppermute | solution.py:412
  201.5 31.7 %copy-start.7 = (f32[1,256,256]{2,1,0:T(8,128)S(1)}, f32[1,256,256]{2,1,0:T(8,128)}, u32[]{:S(2)}) copy-start(f32[1,256,256]{2,1,0:T(8,128)} %param.10) | copy-start | bytes 786436
where the time goes:
time: 235 us
  starting transfers between devices  82.4 us (35%)
  waiting for transfers between devices  76.4 us (33%)
  blocking collectives  31.7 us (13%)
  Pallas kernels  18.2 us (8%)
  other arithmetic  16.4 us (7%)
  local copies, waits for them, and re-layouts  7.36 us (3%)
    ppermute x20, starting transfers between devices, turned(): lax.ppermute(x, axis, [(i, (i + shift) % length) for i in range(length)])  35.4 us
    ppermute x20, waiting for transfers between devices, turned(): lax.ppermute(x, axis, [(i, (i + shift) % length) for i in range(length)])  34.2 us
    all_to_all x1, blocking collectives, per_device(): gathered = lax.all_to_all(slots, COL, 0, 0, tiled=True)  31.7 us
    ppermute x6, starting transfers between devices, per_device(): others.append(lax.ppermute(inner, ROW + COL, pairs))  15.9 us
    ppermute x1, starting transfers between devices, listed_products(): lax.ppermute(sent, ROW + COL, over)  12.3 us
    ppermute x1, waiting for transfers between devices, listed_products(): moved = lax.ppermute(midway, ROW + COL, along)  11.3 us
    pallas_call x1, Pallas kernels, listed_products(): pl.pallas_call(functools.partial(product_kernel, cap, sib), out_shape=(ja...  10.6 us
    ppermute x6, waiting for transfers between devices, per_device(): others.append(lax.ppermute(inner, ROW + COL, pairs))  8.25 us
  transfers between devices with their start and end apart: 34, of which 19 were waited for; matrix products, arithmetic and copies ran while one was open for 7% of the time, Pallas kernels for 0%

commit v1 on v0

--- a/solution.py
+++ b/solution.py
@@ -65,8 +65,9 @@
 
 def product_kernel(cap, sib, tab, g0, g1, c0, c1, ah, al, u_ref, ph_ref, pl_ref, p_ref, lhs, acc):
     parts = (g0, g1, c0, c1)
+    fast = cap < sib * (ah.shape[0] // BLK)
     for i in range(4 * len(parts)):
-        at = pl.multiple_of(tab[PIECE + i] * SUB, SUB)
+        at = pl.multiple_of(tab[PIECE + i] * SUB, SUB) if fast else i * SUB
         p_ref[:, pl.ds(at, SUB), :] = parts[i // 4][i % 4]
     chunks, _, rows, _ = u_ref.shape
 
@@ -149,7 +150,7 @@
         lax.fori_loop(0, (n1 - n0 + 1) // 2, columns, 0)
         return outer
 
-    if cap < sib * (ah.shape[0] // BLK):
+    if fast:
         for j in range(sib):
             sibling(j, 0)
     else:
@@ -201,8 +202,8 @@
     lax.fori_loop(0, sib, sibling, 0)
 
 
-def slots_kernel(tab, x_ref, inner_ref, o_ref):
-    sib, _, cells = x_ref.shape
+def place_kernel(tab, x_ref, o_ref):
+    sib = x_ref.shape[0]
 
     def clear(d, carry):
         o_ref[d] = jnp.zeros(o_ref.shape[1:], jnp.float32)
@@ -210,19 +211,22 @@
 
     lax.fori_loop(0, o_ref.shape[0], clear, 0)
     for j in range(sib):
-        at = tab[OWNER + j]
-        o_ref[at, :, :cells] = x_ref[j]
-        o_ref[at, :, cells:] = inner_ref[j]
-
-
-def finish_kernel(tab, x_ref, diag_ref, lower_ref, out_ref):
-    n_row = x_ref.shape[0]
-    cells = lower_ref.shape[0]
-    places = [lax.rem(2 * n_row - r - tab[AT_ROW], n_row) for r in range(n_row)]
-    for b in range(cells // BLK):
+        o_ref[tab[OWNER + j]] = x_ref[j]
+
+
+def source_columns(tab, n_row):
+    return [lax.rem(2 * n_row - r - tab[AT_ROW], n_row) for r in range(n_row)]
+
+
+def lower_kernel(tab, x_ref, lower_ref):
+    places = source_columns(tab, x_ref.shape[0])
+    for b in range(lower_ref.shape[0] // BLK):
         stack = jnp.concatenate([x_ref[p, :, b * BLK : (b + 1) * BLK] for p in places], axis=0)
         lower_ref[b * BLK : (b + 1) * BLK, :] = stack.T
-    total = jnp.concatenate([x_ref[p, :, cells:] for p in places], axis=0)
+
+
+def diag_kernel(tab, x_ref, diag_ref, out_ref):
+    total = jnp.concatenate([x_ref[p] for p in source_columns(tab, x_ref.shape[0])], axis=0)
     out_ref[...] = jnp.where(tab[PRESENT] > 0, diag_ref[...] - total, 0.0)
 
 
@@ -264,11 +268,7 @@
         all_pieces = lax.all_to_all(
             jnp.broadcast_to(own[None], (pieces, *own.shape)), COL, 0, 0, tiled=True
         )
-        order = piece_columns()
-        parts = jnp.concatenate(
-            [lax.dynamic_index_in_dim(all_pieces, order[i], 0) for i in range(pieces)]
-        )
-        g0, g1, c0, c1 = (parts[i : i + 4] for i in range(0, pieces, 4))
+        g0, g1, c0, c1 = (all_pieces[i : i + 4] for i in range(0, pieces, 4))
     chunk = width // near_chunks
     u, p_hi, p_lo = pl.pallas_call(
         functools.partial(product_kernel, cap, sib),
@@ -284,7 +284,7 @@
             pltpu.VMEM((row_cells // BLK // 2 + 1, width, 6 * BLK), jnp.bfloat16),
             pltpu.VMEM((width, 2 * BLK), jnp.float32),
         ],
-        compiler_params=pltpu.CompilerParams(vmem_limit_bytes=40 << 20),
+        compiler_params=pltpu.CompilerParams(vmem_limit_bytes=(26 if cap < sib * blocks else 34) << 20),
     )(table, g0, g1, c0, c1, a_hi, a_lo)
     z = lax.axis_index("row_0")
     if cap < sib * blocks:
@@ -401,6 +401,14 @@
         a_hi,
         a_lo,
     )
+    place = lambda x: pl.pallas_call(
+        place_kernel,
+        out_shape=jax.ShapeDtypeStruct((n_col, *x.shape[1:]), jnp.float32),
+        in_specs=[SMEM, VMEM],
+        out_specs=VMEM,
+        compiler_params=pltpu.CompilerParams(vmem_limit_bytes=8 << 20),
+    )(table, x)
+    gathered = lax.all_to_all(place(moved), COL, 0, 0, tiled=True)
     for bit in (1, 4):
         others = []
         for away in (bit, 2 * bit, 3 * bit):
@@ -411,24 +419,23 @@
             ]
             others.append(lax.ppermute(inner, ROW + COL, pairs))
         inner = (inner + others[0]) + (others[1] + others[2])
-    slots = pl.pallas_call(
-        slots_kernel,
-        out_shape=jax.ShapeDtypeStruct((n_col, width // n_row, row_cells + width), jnp.float32),
-        in_specs=[SMEM] + [VMEM] * 2,
+    gathered, inner = lax.optimization_barrier((gathered, inner))
+    parts = lax.all_to_all(place(inner), COL, 0, 0, tiled=True)
+    lower = pl.pallas_call(
+        lower_kernel,
+        out_shape=jax.ShapeDtypeStruct((row_cells, width), jnp.float32),
+        in_specs=[SMEM, VMEM],
         out_specs=VMEM,
         compiler_params=pltpu.CompilerParams(vmem_limit_bytes=8 << 20),
-    )(table, moved, inner)
-    gathered = lax.all_to_all(slots, COL, 0, 0, tiled=True)
-    lower, diag = pl.pallas_call(
-        finish_kernel,
-        out_shape=(
-            jax.ShapeDtypeStruct((row_cells, width), jnp.float32),
-            jax.ShapeDtypeStruct((width, width), jnp.float32),
-        ),
-        in_specs=[SMEM] + [VMEM] * 2,
-        out_specs=(VMEM, VMEM),
-        compiler_params=pltpu.CompilerParams(vmem_limit_bytes=12 << 20),
-    )(table, gathered, diag_inv[0])
+        cost_estimate=pl.CostEstimate(flops=0, transcendentals=0, bytes_accessed=3 << 20),
+    )(table, gathered)
+    diag = pl.pallas_call(
+        diag_kernel,
+        out_shape=jax.ShapeDtypeStruct((width, width), jnp.float32),
+        in_specs=[SMEM, VMEM, VMEM],
+        out_specs=VMEM,
+        compiler_params=pltpu.CompilerParams(vmem_limit_bytes=4 << 20),
+    )(table, parts, diag_inv[0])
     return (upper_part, lower[None], diag[None])
 
 

time: 235 us -> 239 us (1.017)
  blocking collectives: 31.7 us -> 0 us
  starting transfers between devices: 82.4 us -> 108 us
  Pallas kernels: 18.2 us -> 28.1 us
    all_to_all x1 -> x0, blocking collectives: 31.7 us -> none  [per_device(): gathered = lax.all_to_all(slots, COL, 0, 0, tiled=True)]
    all_to_all x0 -> x2, starting transfers between devices: none -> 25.9 us  [the longest x1 13.1 us: per_device(): gathered = lax.all_to_all(place(moved), COL, 0, 0, tiled=True)]
    ppermute x20, starting transfers between devices: 35.4 us -> 27.4 us  [turned(): lax.ppermute(x, axis, [(i, (i + shift) % length) for i in range(length)])]
    ppermute x1, starting transfers between devices: 1.92 us -> 7.31 us  [listed_products(): moved = lax.ppermute(midway, ROW + COL, along)]
    ppermute x6, waiting for transfers between devices: 8.25 us -> 13.6 us  [per_device(): others.append(lax.ppermute(inner, ROW + COL, pairs))]
    all_to_all x0 -> x2, waiting for transfers between devices: none -> 5.15 us  [the longest x1 5.15 us: per_device(): parts = lax.all_to_all(place(inner), COL, 0, 0, tiled=True)]
    ppermute x1, waiting for transfers between devices: 11.3 us -> 6.46 us  [listed_products(): moved = lax.ppermute(midway, ROW + COL, along)]
    pallas_call x2 -> x4, Pallas kernels: 2.76 us -> 6.87 us  [the longest x2 3.54 us: per_device(): pl.pallas_call(place_kernel, out_shape=jax.ShapeDtypeStruct((n_col, *x.sh...]
  transfers between devices with their start and end apart: 34 -> 36, of which waited for: 19 -> 20; matrix products, arithmetic and copies ran while one was open for 7% -> 7% of each run, Pallas kernels for 0% -> 1%
where the time goes in v1:
time: 239 us; the launch traced here: 240 us
  starting transfers between devices  108 us (45%)
  waiting for transfers between devices  78.7 us (33%)
  Pallas kernels  28.1 us (12%)
  other arithmetic  16.3 us (7%)
  local copies, waits for them, and re-layouts  6.01 us (3%)
    ppermute x20, waiting for transfers between devices, turned(): lax.ppermute(x, axis, [(i, (i + shift) % length) for i in range(length)])  32.6 us
    ppermute x20, starting transfers between devices, turned(): lax.ppermute(x, axis, [(i, (i + shift) % length) for i in range(length)])  27.4 us
    ppermute x6, starting transfers between devices, per_device(): others.append(lax.ppermute(inner, ROW + COL, pairs))  15.9 us
    ppermute x6, waiting for transfers between devices, per_device(): others.append(lax.ppermute(inner, ROW + COL, pairs))  13.6 us
    pallas_call x1, Pallas kernels, listed_products(): pl.pallas_call(functools.partial(product_kernel, cap, sib), out_shape=(ja...  13.6 us
    all_to_all x1, starting transfers between devices, per_device(): gathered = lax.all_to_all(place(moved), COL, 0, 0, tiled=True)  13.1 us
    all_to_all x1, starting transfers between devices, per_device(): parts = lax.all_to_all(place(inner), COL, 0, 0, tiled=True)  12.8 us
    ppermute x4, starting transfers between devices, swapped(): return lax.ppermute(x, axis, [(i, i ^ bit) for i in range(length)])  11.7 us
  transfers between devices with their start and end apart: 36, of which 20 were waited for; matrix products, arithmetic and copies ran while one was open for 7% of the time, Pallas kernels for 1%

profile of v1, /device:TPU:1, one launch (start us, length us, event | category | flops | bytes accessed | tf_op | source)
XLA Modules:
  0.0 240.1 jit_solution(11098201507453812220)
XLA Ops:
  0.7 2.5 %copy.12 = f32[16,10,8,256]{3,2,1,0:T(8,128)} copy(f32[16,10,8,256]{3,2,0,1:T(8,128)} %bitcast.77) | data formatting | bytes 2621440 | tf_op jit(solution)/shard_map/transpose | solution.py:357
  3.2 6.8 %all-to-all-start.2 = ((f32[16,10,8,256]{3,2,1,0:T(8,128)}), f32[16,10,8,256]{3,2,1,0:T(8,128)S(1)}, u32[]{:S(2)}, u32[]{:S(2)}) async-start(f32[16,10,8,256]{3,2,1,0:T(8,128)} %copy.12), calls=%async_computation.2 | async-start | bytes 2621440 | tf_op jit(solution)/shard_map/all_to_all | solution.py:358
  11.0 0.6 compare_reduce_fusion
  13.1 0.6 reduce_max.9
  14.5 6.6 %fusion.8 = (bf16[1280,1280]{1,0:T(8,128)(2,1)}, bf16[1280,1280]{1,0:T(8,128)(2,1)}) fusion(f32[1280,1280]{1,0:T(8,128)} %param.8), kind=kLoop, calls=%fused_computation.36 | loop fusion | flops 6553600 | bytes 13107200 | tf_op jit(solution)/shard_map/convert_element_type | solution.py:361
  21.1 7.6 %all-to-all-done.2 = f32[16,10,8,256]{3,2,1,0:T(8,128)S(1)} async-done(((f32[16,10,8,256]{3,2,1,0:T(8,128)}), f32[16,10,8,256]{3,2,1,0:T(8,128)S(1)}, u32[]{:S(2)}, u32[]{:S(2)}) %all-to-all-start.2) | async-done | bytes 1310752 | tf_op jit(solution)/shard_map/all_to_all | solution.py:358
  28.7 144.0 %conditional.1 = (f32[4,16,1280]{2,1,0:T(8,128)}, f32[4,16,1280]{2,1,0:T(8,128)}, f32[4,16,256]{2,1,0:T(8,128)S(1)}) conditional(s32[]{:T(128)} %clamp.3, (f32[16,10,8,256]{3,2,1,0:T(8,128)S(1)}, s32[362]{0:T(512)S(1)}, bf16[1280,1280]{1,0:T(8,128)(2,1)}, bf16[1280,1280]{1,0:T(8,128)(2,1)}) %tuple.17, (f32[16,10,8,256]{3,2,1,0:T(8,128)S(1)}, ...), branch_computations={%region_12.13_spmd, %region_13.15_spmd} | conditional | flops 2408704 | bytes 126616064 | solution.py:396
  28.7 0.7 branch_0_fun.5
  30.0 5.9 %collective-permute-done = f32[28,8,256]{2,1,0:T(8,128)S(1)} collective-permute-done((f32[28,8,256]{2,1,0:T(8,128)S(1)}, f32[28,8,256]{2,1,0:T(8,128)S(1)}, u32[]{:S(2)}, u32[]{:S(2)}) %collective-permute-start) | collective-permute-done | bytes 229408 | tf_op jit(solution)/shard_map/cond/branch_0_fun/ppermute | solution.py:26
  35.9 1.4 collective-permute-start.4
  37.7 1.1 collective-permute-start.3
  38.9 2.5 %collective-permute-done.4 = f32[28,8,256]{2,1,0:T(8,128)S(1)} collective-permute-done((f32[28,8,256]{2,1,0:T(8,128)S(1)}, f32[28,8,256]{2,1,0:T(8,128)S(1)}, u32[]{:S(2)}, u32[]{:S(2)}) %collective-permute-start.4) | collective-permute-done | bytes 229408 | tf_op jit(solution)/shard_map/cond/branch_0_fun/ppermute | solution.py:31
  41.4 3.4 %collective-permute-start.6 = (f32[28,8,256]{2,1,0:T(8,128)S(1)}, f32[28,8,256]{2,1,0:T(8,128)S(1)}, u32[]{:S(2)}, u32[]{:S(2)}) collective-permute-start(f32[28,8,256]{2,1,0:T(8,128)S(1)} %collective-permute-done.4), channel_id=1, source_target_pairs={{0,6},{2,0},{4,2},{6,4},{1,7},{3,1},{5,3},{7,5},{8,14},{10,8},{12,... | collective-permute-start | bytes 688136 | tf_op jit(solution)/shard_map/cond/branch_0_fun/ppermute | solution.py:31
  44.8 1.5 collective-permute-done.2
  46.4 4.7 %collective-permute-start.7 = (f32[4,28,8,256]{3,2,1,0:T(8,128)S(1)}, f32[4,28,8,256]{3,2,1,0:T(8,128)S(1)}, u32[]{:S(2)}, u32[]{:S(2)}) collective-permute-start(f32[4,28,8,256]{3,2,1,0:T(8,128)S(1)} %pad_maximum_fusion.g0), channel_id=1, source_target_pairs={{0,1},{1,0},{2,3},{3,2},{4,5},{5,4},{6,7},{7,6},{8,9},{9,8},{10,11... | collective-permute-start | bytes 2752520 | tf_op jit(solution)/shard_map/cond/branch_0_fun/ppermute | solution.py:26
  51.3 2.6 %collective-permute-start.8 = (f32[4,28,8,256]{3,2,1,0:T(8,128)S(1)}, f32[4,28,8,256]{3,2,1,0:T(8,128)}, u32[]{:S(2)}, u32[]{:S(2)}) collective-permute-start(f32[4,28,8,256]{3,2,1,0:T(8,128)S(1)} %pad_maximum_fusion.1.g1), channel_id=1, source_target_pairs={{0,1},{1,0},{2,3},{3,2},{4,5},{5,4},{6,7},{7,6},{8,9},{9,8},{10,11... | collective-permute-start | bytes 2752520 | tf_op jit(solution)/shard_map/cond/branch_0_fun/ppermute | solution.py:26
  53.9 2.2 collective-permute-done.8.c1
  56.2 13.6 %branch_0_fun.6 = (f32[8,28,32,128]{3,2,1,0:T(8,128)S(1)}, bf16[28,128,256]{2,1,0:T(8,128)(2,1)S(1)}, bf16[28,128,256]{2,1,0:T(8,128)(2,1)S(1)}) custom-call(s32[362]{0:T(512)S(1)} %get-tuple-element.16.tab, f32[4,28,8,256]{3,2,1,0:T(8,128)S(1)} %pad_maximum_fusion.g0, f32[4,28,8,256]{3,2,1,0:T(8,128)S(1)} %pad_maximum_fusion.1.g1, ...), custom_call_target="tpu_custom_call" | custom-call | tf_op jit(solution)/shard_map/cond/branch_0_fun/pallas_call | solution.py:273
  69.8 1.7 copy-done.1
  72.8 3.9 %collective-permute-start.16 = (f32[2,7,32,128]{3,2,1,0:T(8,128)S(1)}, f32[2,7,32,128]{3,2,1,0:T(8,128)S(1)}, u32[]{:S(2)}, u32[]{:S(2)}) collective-permute-start(f32[2,7,32,128]{3,2,1,0:T(8,128)S(1)} %bitcast.95), channel_id=1, source_target_pairs={{0,224},{32,0},{64,32},{96,64},{128,96},{160,128},{192,160},{224,1... | collective-permute-start | bytes 688136 | tf_op jit(solution)/shard_map/cond/branch_0_fun/ppermute | solution.py:31
  76.7 3.9 %collective-permute-done.9 = f32[14,32,128]{2,1,0:T(8,128)S(1)} collective-permute-done((f32[14,32,128]{2,1,0:T(8,128)S(1)}, f32[14,32,128]{2,1,0:T(8,128)S(1)}, u32[]{:S(2)}, u32[]{:S(2)}) %collective-permute-start.9) | collective-permute-done | bytes 229408 | tf_op jit(solution)/shard_map/cond/branch_0_fun/ppermute | solution.py:31
  80.6 1.0 fusion.6
  81.7 2.7 %collective-permute-start.17 = (f32[2,7,32,128]{3,2,1,0:T(8,128)S(1)}, f32[2,7,32,128]{3,2,1,0:T(8,128)S(1)}, u32[]{:S(2)}, u32[]{:S(2)}) collective-permute-start(f32[2,7,32,128]{3,2,1,0:T(8,128)S(1)} %add.381), channel_id=1, source_target_pairs={{0,224},{32,0},{64,32},{96,64},{128,96},{160,128},{192,160},{224,1... | collective-permute-start | bytes 688136 | tf_op jit(solution)/shard_map/cond/branch_0_fun/ppermute | solution.py:31
  84.4 3.3 %collective-permute-done.10 = f32[14,32,128]{2,1,0:T(8,128)S(1)} collective-permute-done((f32[14,32,128]{2,1,0:T(8,128)S(1)}, f32[14,32,128]{2,1,0:T(8,128)S(1)}, u32[]{:S(2)}, u32[]{:S(2)}) %collective-permute-start.10) | collective-permute-done | bytes 229408 | tf_op jit(solution)/shard_map/cond/branch_0_fun/ppermute | solution.py:31
  87.7 1.0 fusion.5
  88.8 2.7 %collective-permute-start.18 = (f32[2,7,32,128]{3,2,1,0:T(8,128)S(1)}, f32[2,7,32,128]{3,2,1,0:T(8,128)S(1)}, u32[]{:S(2)}, u32[]{:S(2)}) collective-permute-start(f32[2,7,32,128]{3,2,1,0:T(8,128)S(1)} %add.385), channel_id=1, source_target_pairs={{0,224},{32,0},{64,32},{96,64},{128,96},{160,128},{192,160},{224,1... | collective-permute-start | bytes 688136 | tf_op jit(solution)/shard_map/cond/branch_0_fun/ppermute | solution.py:31
  91.6 3.3 %collective-permute-done.11 = f32[14,32,128]{2,1,0:T(8,128)S(1)} collective-permute-done((f32[14,32,128]{2,1,0:T(8,128)S(1)}, f32[14,32,128]{2,1,0:T(8,128)S(1)}, u32[]{:S(2)}, u32[]{:S(2)}) %collective-permute-start.11) | collective-permute-done | bytes 229408 | tf_op jit(solution)/shard_map/cond/branch_0_fun/ppermute | solution.py:31
  94.8 1.0 fusion.4
  96.0 2.7 %collective-permute-start.19 = (f32[2,7,32,128]{3,2,1,0:T(8,128)S(1)}, f32[2,7,32,128]{3,2,1,0:T(8,128)S(1)}, u32[]{:S(2)}, u32[]{:S(2)}) collective-permute-start(f32[2,7,32,128]{3,2,1,0:T(8,128)S(1)} %add.389), channel_id=1, source_target_pairs={{0,224},{32,0},{64,32},{96,64},{128,96},{160,128},{192,160},{224,1... | collective-permute-start | bytes 688136 | tf_op jit(solution)/shard_map/cond/branch_0_fun/ppermute | solution.py:31
  98.7 3.3 %collective-permute-done.12 = f32[14,32,128]{2,1,0:T(8,128)S(1)} collective-permute-done((f32[14,32,128]{2,1,0:T(8,128)S(1)}, f32[14,32,128]{2,1,0:T(8,128)S(1)}, u32[]{:S(2)}, u32[]{:S(2)}) %collective-permute-start.12) | collective-permute-done | bytes 229408 | tf_op jit(solution)/shard_map/cond/branch_0_fun/ppermute | solution.py:31
  102.0 1.0 fusion.3
  103.1 2.7 %collective-permute-start.20 = (f32[2,7,32,128]{3,2,1,0:T(8,128)S(1)}, f32[2,7,32,128]{3,2,1,0:T(8,128)S(1)}, u32[]{:S(2)}, u32[]{:S(2)}) collective-permute-start(f32[2,7,32,128]{3,2,1,0:T(8,128)S(1)} %add.393), channel_id=1, source_target_pairs={{0,224},{32,0},{64,32},{96,64},{128,96},{160,128},{192,160},{224,1... | collective-permute-start | bytes 688136 | tf_op jit(solution)/shard_map/cond/branch_0_fun/ppermute | solution.py:31
  105.8 4.1 %collective-permute-done.13 = f32[14,32,128]{2,1,0:T(8,128)S(1)} collective-permute-done((f32[14,32,128]{2,1,0:T(8,128)S(1)}, f32[14,32,128]{2,1,0:T(8,128)S(1)}, u32[]{:S(2)}, u32[]{:S(2)}) %collective-permute-start.13) | collective-permute-done | bytes 229408 | tf_op jit(solution)/shard_map/cond/branch_0_fun/ppermute | solution.py:31
  109.9 1.0 fusion.2
  111.0 2.7 %collective-permute-start.21 = (f32[2,7,32,128]{3,2,1,0:T(8,128)S(1)}, f32[2,7,32,128]{3,2,1,0:T(8,128)S(1)}, u32[]{:S(2)}, u32[]{:S(2)}) collective-permute-start(f32[2,7,32,128]{3,2,1,0:T(8,128)S(1)} %add.397), channel_id=1, source_target_pairs={{0,224},{32,0},{64,32},{96,64},{128,96},{160,128},{192,160},{224,1... | collective-permute-start | bytes 688136 | tf_op jit(solution)/shard_map/cond/branch_0_fun/ppermute | solution.py:31
  113.7 5.1 %collective-permute-done.14 = f32[14,32,128]{2,1,0:T(8,128)S(1)} collective-permute-done((f32[14,32,128]{2,1,0:T(8,128)S(1)}, f32[14,32,128]{2,1,0:T(8,128)S(1)}, u32[]{:S(2)}, u32[]{:S(2)}) %collective-permute-start.14) | collective-permute-done | bytes 229408 | tf_op jit(solution)/shard_map/cond/branch_0_fun/ppermute | solution.py:31
  118.9 1.0 fusion.1
  120.0 2.7 %collective-permute-start.22 = (f32[2,7,32,128]{3,2,1,0:T(8,128)S(1)}, f32[2,7,32,128]{3,2,1,0:T(8,128)S(1)}, u32[]{:S(2)}, u32[]{:S(2)}) collective-permute-start(f32[2,7,32,128]{3,2,1,0:T(8,128)S(1)} %add.401), channel_id=1, source_target_pairs={{0,224},{32,0},{64,32},{96,64},{128,96},{160,128},{192,160},{224,1... | collective-permute-start | bytes 688136 | tf_op jit(solution)/shard_map/cond/branch_0_fun/ppermute | solution.py:31
  122.7 5.5 %collective-permute-done.15 = f32[14,32,128]{2,1,0:T(8,128)S(1)} collective-permute-done((f32[14,32,128]{2,1,0:T(8,128)S(1)}, f32[14,32,128]{2,1,0:T(8,128)S(1)}, u32[]{:S(2)}, u32[]{:S(2)}) %collective-permute-start.15) | collective-permute-done | bytes 229408 | tf_op jit(solution)/shard_map/cond/branch_0_fun/ppermute | solution.py:31
  128.2 1.0 fusion
  129.3 4.0 %collective-permute-start.23 = (f32[28,16,128]{2,1,0:T(8,128)S(1)}, f32[28,16,128]{2,1,0:T(8,128)S(1)}, u32[]{:S(2)}, u32[]{:S(2)}) collective-permute-start(f32[28,16,128]{2,1,0:T(8,128)S(1)} %pad_maximum_fusion.3), channel_id=1, source_target_pairs={{0,16},{16,0},{1,17},{17,1},{2,18},{18,2},{3,19},{19,3},{4,20},{20... | collective-permute-start | bytes 688136 | tf_op jit(solution)/shard_map/cond/branch_0_fun/ppermute | solution.py:26
  133.3 8.9 %collective-permute-start.25 = (f32[28,16,128]{2,1,0:T(8,128)S(1)}, f32[28,16,128]{2,1,0:T(8,128)S(1)}, u32[]{:S(2)}, u32[]{:S(2)}) collective-permute-start(f32[28,16,128]{2,1,0:T(8,128)S(1)} %pad_maximum_fusion.3), channel_id=1, source_target_pairs={{0,31},{1,30},{2,29},{3,28},{4,27},{5,26},{6,25},{7,24},{8,23},{9,... | collective-permute-start | bytes 688136 | tf_op jit(solution)/shard_map/cond/branch_0_fun/ppermute | solution.py:310
  142.3 4.3 %collective-permute-start.24 = (f32[28,16,128]{2,1,0:T(8,128)S(1)}, f32[28,16,128]{2,1,0:T(8,128)S(1)}, u32[]{:S(2)}, u32[]{:S(2)}) collective-permute-start(f32[28,16,128]{2,1,0:T(8,128)S(1)} %get-tuple-element.68), channel_id=1, source_target_pairs={{0,0},{1,15},{2,14},{3,13},{4,12},{5,11},{6,10},{7,9},{8,8},{9,7},... | collective-permute-start | bytes 688136 | tf_op jit(solution)/shard_map/cond/branch_0_fun/ppermute | solution.py:310
  147.0 4.8 %collective-permute-done.24 = f32[28,16,128]{2,1,0:T(8,128)S(1)} collective-permute-done((f32[28,16,128]{2,1,0:T(8,128)S(1)}, f32[28,16,128]{2,1,0:T(8,128)S(1)}, u32[]{:S(2)}, u32[]{:S(2)}) %collective-permute-start.24) | collective-permute-done | bytes 229408 | tf_op jit(solution)/shard_map/cond/branch_0_fun/ppermute | solution.py:310
  151.8 7.3 %collective-permute-start.26 = (f32[28,16,128]{2,1,0:T(8,128)S(1)}, f32[28,16,128]{2,1,0:T(8,128)S(1)}, u32[]{:S(2)}, u32[]{:S(2)}) collective-permute-start(f32[28,16,128]{2,1,0:T(8,128)S(1)} %add.408), channel_id=1, source_target_pairs={{0,0},{1,241},{2,226},{3,211},{4,196},{5,181},{6,166},{7,151},{8,1... | collective-permute-start | bytes 688136 | tf_op jit(solution)/shard_map/cond/branch_0_fun/ppermute | solution.py:311
  159.1 1.4 branch_0_fun.7
  160.5 6.5 %collective-permute-done.26.x_ref = f32[28,16,128]{2,1,0:T(8,128)S(1)} collective-permute-done((f32[28,16,128]{2,1,0:T(8,128)S(1)}, f32[28,16,128]{2,1,0:T(8,128)S(1)}, u32[]{:S(2)}, u32[]{:S(2)}) %collective-permute-start.26) | collective-permute-done | bytes 229408 | tf_op jit(solution)/shard_map/cond/branch_0_fun/ppermute | solution.py:311
  167.0 1.4 branch_0_fun.8
  168.4 4.1 %branch_0_fun.9 = f32[4,16,256]{2,1,0:T(8,128)S(1)} custom-call(s32[362]{0:T(512)S(1)} %get-tuple-element.16.tab, f32[28,16,128]{2,1,0:T(8,128)S(1)} %collective-permute-done.26.x_ref, bf16[28,128,256]{2,1,0:T(8,128)(2,1)S(1)} %copy-done.5, bf16[28,128,256]{2,1,0:T(8,128)(2,1)S(1)} %copy-done.7), custom_call_target="tpu_custom_call" | custom-call | tf_op jit(solution)/shard_map/cond/branch_0_fun/pallas_call | solution.py:322
  172.6 2.2 shard_map.85
  174.8 13.1 %all-to-all-start.3 = ((f32[16,16,1280]{2,1,0:T(8,128)}), f32[16,16,1280]{2,1,0:T(8,128)S(1)}, u32[]{:S(2)}, u32[]{:S(2)}) async-start(f32[16,16,1280]{2,1,0:T(8,128)} %shard_map.85), calls=%async_computation.3 | async-start | bytes 2621440 | tf_op jit(solution)/shard_map/all_to_all | solution.py:411
  187.9 0.9 collective-permute-start.31
  188.8 5.9 %collective-permute-start.33 = (f32[4,16,256]{2,1,0:T(8,128)S(1)}, f32[4,16,256]{2,1,0:T(8,128)S(1)}, u32[]{:S(2)}, u32[]{:S(2)}) collective-permute-start(f32[4,16,256]{2,1,0:T(8,128)S(1)} %get-tuple-element.40), channel_id=1, source_target_pairs={{0,61},{1,62},{2,63},{3,48},{4,49},{5,50},{6,51},{7,52},{8,53},{9,... | collective-permute-start | bytes 196616 | tf_op jit(solution)/shard_map/ppermute | solution.py:420
  194.8 9.3 %collective-permute-done.31 = f32[4,16,256]{2,1,0:T(8,128)S(1)} collective-permute-done((f32[4,16,256]{2,1,0:T(8,128)S(1)}, f32[4,16,256]{2,1,0:T(8,128)S(1)}, u32[]{:S(2)}, u32[]{:S(2)}) %collective-permute-start.31) | collective-permute-done | bytes 65568 | tf_op jit(solution)/shard_map/ppermute | solution.py:420
  204.1 3.0 %collective-permute-start.34 = (f32[4,16,256]{2,1,0:T(8,128)S(1)}, f32[4,16,256]{2,1,0:T(8,128)S(1)}, u32[]{:S(2)}, u32[]{:S(2)}) collective-permute-start(f32[4,16,256]{2,1,0:T(8,128)S(1)} %add_add_fusion.1), channel_id=1, source_target_pairs={{0,76},{1,77},{2,78},{3,79},{4,64},{5,65},{6,66},{7,67},{8,68},{9,... | collective-permute-start | bytes 196616 | tf_op jit(solution)/shard_map/ppermute | solution.py:420
  207.1 2.0 collective-permute-start.35
  209.1 4.0 %collective-permute-start.36 = (f32[4,16,256]{2,1,0:T(8,128)S(1)}, f32[4,16,256]{2,1,0:T(8,128)S(1)}, u32[]{:S(2)}, u32[]{:S(2)}) collective-permute-start(f32[4,16,256]{2,1,0:T(8,128)S(1)} %add_add_fusion.1), channel_id=1, source_target_pairs={{0,196},{1,197},{2,198},{3,199},{4,200},{5,201},{6,202},{7,203},{8... | collective-permute-start | bytes 196616 | tf_op jit(solution)/shard_map/ppermute | solution.py:420
  213.1 1.9 collective-permute-done.35
  215.0 2.4 collective-permute-done.36
  217.5 1.4 shard_map.87
  218.8 12.8 %all-to-all-start.4 = ((f32[16,16,256]{2,1,0:T(8,128)}), f32[16,16,256]{2,1,0:T(8,128)S(1)}, u32[]{:S(2)}, u32[]{:S(2)}) async-start(f32[16,16,256]{2,1,0:T(8,128)} %shard_map.87), calls=%async_computation.4 | async-start | bytes 524288 | tf_op jit(solution)/shard_map/all_to_all | solution.py:423
  231.6 2.0 shard_map.86
  233.6 5.1 %all-to-all-done.4.x_ref = f32[16,16,256]{2,1,0:T(8,128)S(1)} async-done(((f32[16,16,256]{2,1,0:T(8,128)}), f32[16,16,256]{2,1,0:T(8,128)S(1)}, u32[]{:S(2)}, u32[]{:S(2)}) %all-to-all-start.4) | async-done | bytes 262176 | tf_op jit(solution)/shard_map/all_to_all | solution.py:423
  238.8 1.3 shard_map.88
  (95 shorter events, 5.5 us)
Async XLA Ops:
  0.6 9.4 %copy-start.12 = (s32[4]{0:T(128)S(1)}, s32[4]{0:T(128)}, u32[]{:S(2)}) copy-start(s32[4]{0:T(128)} %param.12) | copy-start | bytes 52
  0.6 9.5 %copy-start.11 = (s32[4,96]{1,0:T(4,128)S(1)}, s32[4,96]{1,0:T(4,128)}, u32[]{:S(2)}) copy-start(s32[4,96]{1,0:T(4,128)} %param.11) | copy-start | bytes 4612
  0.7 10.3 %copy-start.13 = (s32[4]{0:T(128)S(1)}, s32[4]{0:T(128)}, u32[]{:S(2)}) copy-start(s32[4]{0:T(128)} %param.13) | copy-start | bytes 52
  3.2 25.5 %all-to-all-start.2 = ((f32[16,10,8,256]{3,2,1,0:T(8,128)}), f32[16,10,8,256]{3,2,1,0:T(8,128)S(1)}, u32[]{:S(2)}, u32[]{:S(2)}) async-start(f32[16,10,8,256]{3,2,1,0:T(8,128)} %copy.12), calls=%async_computation.2 | async-start | bytes 2621440 | tf_op jit(solution)/shard_map/all_to_all | solution.py:358
  29.4 6.5 %collective-permute-start = (f32[28,8,256]{2,1,0:T(8,128)S(1)}, f32[28,8,256]{2,1,0:T(8,128)S(1)}, u32[]{:S(2)}, u32[]{:S(2)}) collective-permute-start(f32[28,8,256]{2,1,0:T(8,128)S(1)} %branch_0_fun.5), channel_id=1, source_target_pairs={{0,8},{8,0},{1,9},{9,1},{2,10},{10,2},{3,11},{11,3},{4,12},{12,4},... | collective-permute-start | bytes 688136 | tf_op jit(solution)/shard_map/cond/branch_0_fun/ppermute | solution.py:26
  29.8 9.1 %collective-permute-start.1 = (f32[28,8,256]{2,1,0:T(8,128)S(1)}, f32[28,8,256]{2,1,0:T(8,128)S(1)}, u32[]{:S(2)}, u32[]{:S(2)}) collective-permute-start(f32[28,8,256]{2,1,0:T(8,128)S(1)} %branch_0_fun.5), channel_id=1, source_target_pairs={{0,2},{2,4},{4,6},{6,0},{1,3},{3,5},{5,7},{7,1},{8,10},{10,12},{12... | collective-permute-start | bytes 688136 | tf_op jit(solution)/shard_map/cond/branch_0_fun/ppermute | solution.py:31
  35.9 5.5 %collective-permute-start.4 = (f32[28,8,256]{2,1,0:T(8,128)S(1)}, f32[28,8,256]{2,1,0:T(8,128)S(1)}, u32[]{:S(2)}, u32[]{:S(2)}) collective-permute-start(f32[28,8,256]{2,1,0:T(8,128)S(1)} %collective-permute-done), channel_id=1, source_target_pairs={{0,6},{2,0},{4,2},{6,4},{1,7},{3,1},{5,3},{7,5},{8,14},{10,8},{12,... | collective-permute-start | bytes 688136 | tf_op jit(solution)/shard_map/cond/branch_0_fun/ppermute | solution.py:31
  37.4 9.0 %collective-permute-start.2 = (f32[28,8,256]{2,1,0:T(8,128)S(1)}, f32[28,8,256]{2,1,0:T(8,128)S(1)}, u32[]{:S(2)}, u32[]{:S(2)}) collective-permute-start(f32[28,8,256]{2,1,0:T(8,128)S(1)} %branch_0_fun.5), channel_id=1, source_target_pairs={{0,6},{2,0},{4,2},{6,4},{1,7},{3,1},{5,3},{7,5},{8,14},{10,8},{12,... | collective-permute-start | bytes 688136 | tf_op jit(solution)/shard_map/cond/branch_0_fun/ppermute | solution.py:31
  37.7 13.5 %collective-permute-start.3 = (f32[28,8,256]{2,1,0:T(8,128)S(1)}, f32[28,8,256]{2,1,0:T(8,128)S(1)}, u32[]{:S(2)}, u32[]{:S(2)}) collective-permute-start(f32[28,8,256]{2,1,0:T(8,128)S(1)} %collective-permute-done), channel_id=1, source_target_pairs={{0,2},{2,4},{4,6},{6,0},{1,3},{3,5},{5,7},{7,1},{8,10},{10,12},{12... | collective-permute-start | bytes 688136 | tf_op jit(solution)/shard_map/cond/branch_0_fun/ppermute | solution.py:31
  38.8 12.3 %collective-permute-start.5 = (f32[28,8,256]{2,1,0:T(8,128)S(1)}, f32[28,8,256]{2,1,0:T(8,128)S(1)}, u32[]{:S(2)}, u32[]{:S(2)}) collective-permute-start(f32[28,8,256]{2,1,0:T(8,128)S(1)} %collective-permute-done.1), channel_id=1, source_target_pairs={{0,2},{2,4},{4,6},{6,0},{1,3},{3,5},{5,7},{7,1},{8,10},{10,12},{12... | collective-permute-start | bytes 688136 | tf_op jit(solution)/shard_map/cond/branch_0_fun/ppermute | solution.py:31
  41.4 9.8 %collective-permute-start.6 = (f32[28,8,256]{2,1,0:T(8,128)S(1)}, f32[28,8,256]{2,1,0:T(8,128)S(1)}, u32[]{:S(2)}, u32[]{:S(2)}) collective-permute-start(f32[28,8,256]{2,1,0:T(8,128)S(1)} %collective-permute-done.4), channel_id=1, source_target_pairs={{0,6},{2,0},{4,2},{6,4},{1,7},{3,1},{5,3},{7,5},{8,14},{10,8},{12,... | collective-permute-start | bytes 688136 | tf_op jit(solution)/shard_map/cond/branch_0_fun/ppermute | solution.py:31
  46.4 7.5 %collective-permute-start.7 = (f32[4,28,8,256]{3,2,1,0:T(8,128)S(1)}, f32[4,28,8,256]{3,2,1,0:T(8,128)S(1)}, u32[]{:S(2)}, u32[]{:S(2)}) collective-permute-start(f32[4,28,8,256]{3,2,1,0:T(8,128)S(1)} %pad_maximum_fusion.g0), channel_id=1, source_target_pairs={{0,1},{1,0},{2,3},{3,2},{4,5},{5,4},{6,7},{7,6},{8,9},{9,8},{10,11... | collective-permute-start | bytes 2752520 | tf_op jit(solution)/shard_map/cond/branch_0_fun/ppermute | solution.py:26
  51.3 4.8 %collective-permute-start.8 = (f32[4,28,8,256]{3,2,1,0:T(8,128)S(1)}, f32[4,28,8,256]{3,2,1,0:T(8,128)}, u32[]{:S(2)}, u32[]{:S(2)}) collective-permute-start(f32[4,28,8,256]{3,2,1,0:T(8,128)S(1)} %pad_maximum_fusion.1.g1), channel_id=1, source_target_pairs={{0,1},{1,0},{2,3},{3,2},{4,5},{5,4},{6,7},{7,6},{8,9},{9,8},{10,11... | collective-permute-start | bytes 2752520 | tf_op jit(solution)/shard_map/cond/branch_0_fun/ppermute | solution.py:26
  69.7 1.8 copy-start.1
  69.8 2.4 %copy-start.4 = (bf16[28,128,256]{2,1,0:T(8,128)(2,1)}, bf16[28,128,256]{2,1,0:T(8,128)(2,1)S(1)}, u32[]{:S(2)}) copy-start(bf16[28,128,256]{2,1,0:T(8,128)(2,1)S(1)} %get-tuple-element.21.hi_ref) | copy-start | bytes 5505028 | tf_op jit(solution)/shard_map/cond
  69.8 2.9 %copy-start.6 = (bf16[28,128,256]{2,1,0:T(8,128)(2,1)}, bf16[28,128,256]{2,1,0:T(8,128)(2,1)S(1)}, u32[]{:S(2)}) copy-start(bf16[28,128,256]{2,1,0:T(8,128)(2,1)S(1)} %get-tuple-element.22.lo_ref) | copy-start | bytes 5505028 | tf_op jit(solution)/shard_map/cond
  72.7 7.9 %collective-permute-start.9 = (f32[14,32,128]{2,1,0:T(8,128)S(1)}, f32[14,32,128]{2,1,0:T(8,128)S(1)}, u32[]{:S(2)}, u32[]{:S(2)}) collective-permute-start(f32[14,32,128]{2,1,0:T(8,128)S(1)} %get-tuple-element.59), channel_id=1, source_target_pairs={{0,32},{32,64},{64,96},{96,128},{128,160},{160,192},{192,224},{224... | collective-permute-start | bytes 688136 | tf_op jit(solution)/shard_map/cond/branch_0_fun/ppermute | solution.py:31
  72.8 8.9 %collective-permute-start.16 = (f32[2,7,32,128]{3,2,1,0:T(8,128)S(1)}, f32[2,7,32,128]{3,2,1,0:T(8,128)S(1)}, u32[]{:S(2)}, u32[]{:S(2)}) collective-permute-start(f32[2,7,32,128]{3,2,1,0:T(8,128)S(1)} %bitcast.95), channel_id=1, source_target_pairs={{0,224},{32,0},{64,32},{96,64},{128,96},{160,128},{192,160},{224,1... | collective-permute-start | bytes 688136 | tf_op jit(solution)/shard_map/cond/branch_0_fun/ppermute | solution.py:31
  81.6 6.2 %collective-permute-start.10 = (f32[14,32,128]{2,1,0:T(8,128)S(1)}, f32[14,32,128]{2,1,0:T(8,128)S(1)}, u32[]{:S(2)}, u32[]{:S(2)}) collective-permute-start(f32[14,32,128]{2,1,0:T(8,128)S(1)} %fusion.6), channel_id=1, source_target_pairs={{0,32},{32,64},{64,96},{96,128},{128,160},{160,192},{192,224},{224... | collective-permute-start | bytes 688136 | tf_op jit(solution)/shard_map/cond/branch_0_fun/ppermute | solution.py:31
  81.7 7.1 %collective-permute-start.17 = (f32[2,7,32,128]{3,2,1,0:T(8,128)S(1)}, f32[2,7,32,128]{3,2,1,0:T(8,128)S(1)}, u32[]{:S(2)}, u32[]{:S(2)}) collective-permute-start(f32[2,7,32,128]{3,2,1,0:T(8,128)S(1)} %add.381), channel_id=1, source_target_pairs={{0,224},{32,0},{64,32},{96,64},{128,96},{160,128},{192,160},{224,1... | collective-permute-start | bytes 688136 | tf_op jit(solution)/shard_map/cond/branch_0_fun/ppermute | solution.py:31
  88.7 6.2 %collective-permute-start.11 = (f32[14,32,128]{2,1,0:T(8,128)S(1)}, f32[14,32,128]{2,1,0:T(8,128)S(1)}, u32[]{:S(2)}, u32[]{:S(2)}) collective-permute-start(f32[14,32,128]{2,1,0:T(8,128)S(1)} %fusion.5), channel_id=1, source_target_pairs={{0,32},{32,64},{64,96},{96,128},{128,160},{160,192},{192,224},{224... | collective-permute-start | bytes 688136 | tf_op jit(solution)/shard_map/cond/branch_0_fun/ppermute | solution.py:31
  88.8 7.1 %collective-permute-start.18 = (f32[2,7,32,128]{3,2,1,0:T(8,128)S(1)}, f32[2,7,32,128]{3,2,1,0:T(8,128)S(1)}, u32[]{:S(2)}, u32[]{:S(2)}) collective-permute-start(f32[2,7,32,128]{3,2,1,0:T(8,128)S(1)} %add.385), channel_id=1, source_target_pairs={{0,224},{32,0},{64,32},{96,64},{128,96},{160,128},{192,160},{224,1... | collective-permute-start | bytes 688136 | tf_op jit(solution)/shard_map/cond/branch_0_fun/ppermute | solution.py:31
  95.8 6.2 %collective-permute-start.12 = (f32[14,32,128]{2,1,0:T(8,128)S(1)}, f32[14,32,128]{2,1,0:T(8,128)S(1)}, u32[]{:S(2)}, u32[]{:S(2)}) collective-permute-start(f32[14,32,128]{2,1,0:T(8,128)S(1)} %fusion.4), channel_id=1, source_target_pairs={{0,32},{32,64},{64,96},{96,128},{128,160},{160,192},{192,224},{224... | collective-permute-start | bytes 688136 | tf_op jit(solution)/shard_map/cond/branch_0_fun/ppermute | solution.py:31
  96.0 7.1 %collective-permute-start.19 = (f32[2,7,32,128]{3,2,1,0:T(8,128)S(1)}, f32[2,7,32,128]{3,2,1,0:T(8,128)S(1)}, u32[]{:S(2)}, u32[]{:S(2)}) collective-permute-start(f32[2,7,32,128]{3,2,1,0:T(8,128)S(1)} %add.389), channel_id=1, source_target_pairs={{0,224},{32,0},{64,32},{96,64},{128,96},{160,128},{192,160},{224,1... | collective-permute-start | bytes 688136 | tf_op jit(solution)/shard_map/cond/branch_0_fun/ppermute | solution.py:31
  103.0 6.9 %collective-permute-start.13 = (f32[14,32,128]{2,1,0:T(8,128)S(1)}, f32[14,32,128]{2,1,0:T(8,128)S(1)}, u32[]{:S(2)}, u32[]{:S(2)}) collective-permute-start(f32[14,32,128]{2,1,0:T(8,128)S(1)} %fusion.3), channel_id=1, source_target_pairs={{0,32},{32,64},{64,96},{96,128},{128,160},{160,192},{192,224},{224... | collective-permute-start | bytes 688136 | tf_op jit(solution)/shard_map/cond/branch_0_fun/ppermute | solution.py:31
  103.1 7.9 %collective-permute-start.20 = (f32[2,7,32,128]{3,2,1,0:T(8,128)S(1)}, f32[2,7,32,128]{3,2,1,0:T(8,128)S(1)}, u32[]{:S(2)}, u32[]{:S(2)}) collective-permute-start(f32[2,7,32,128]{3,2,1,0:T(8,128)S(1)} %add.393), channel_id=1, source_target_pairs={{0,224},{32,0},{64,32},{96,64},{128,96},{160,128},{192,160},{224,1... | collective-permute-start | bytes 688136 | tf_op jit(solution)/shard_map/cond/branch_0_fun/ppermute | solution.py:31
  110.9 8.0 %collective-permute-start.14 = (f32[14,32,128]{2,1,0:T(8,128)S(1)}, f32[14,32,128]{2,1,0:T(8,128)S(1)}, u32[]{:S(2)}, u32[]{:S(2)}) collective-permute-start(f32[14,32,128]{2,1,0:T(8,128)S(1)} %fusion.2), channel_id=1, source_target_pairs={{0,32},{32,64},{64,96},{96,128},{128,160},{160,192},{192,224},{224... | collective-permute-start | bytes 688136 | tf_op jit(solution)/shard_map/cond/branch_0_fun/ppermute | solution.py:31
  111.0 9.0 %collective-permute-start.21 = (f32[2,7,32,128]{3,2,1,0:T(8,128)S(1)}, f32[2,7,32,128]{3,2,1,0:T(8,128)S(1)}, u32[]{:S(2)}, u32[]{:S(2)}) collective-permute-start(f32[2,7,32,128]{3,2,1,0:T(8,128)S(1)} %add.397), channel_id=1, source_target_pairs={{0,224},{32,0},{64,32},{96,64},{128,96},{160,128},{192,160},{224,1... | collective-permute-start | bytes 688136 | tf_op jit(solution)/shard_map/cond/branch_0_fun/ppermute | solution.py:31
  119.8 48.5 %copy-start.5 = (bf16[28,128,256]{2,1,0:T(8,128)(2,1)S(1)}, bf16[28,128,256]{2,1,0:T(8,128)(2,1)}, u32[]{:S(2)}) copy-start(bf16[28,128,256]{2,1,0:T(8,128)(2,1)} %copy-done.4) | copy-start | bytes 5505028 | tf_op jit(solution)/shard_map/cond
  119.9 8.4 %collective-permute-start.15 = (f32[14,32,128]{2,1,0:T(8,128)S(1)}, f32[14,32,128]{2,1,0:T(8,128)S(1)}, u32[]{:S(2)}, u32[]{:S(2)}) collective-permute-start(f32[14,32,128]{2,1,0:T(8,128)S(1)} %fusion.1), channel_id=1, source_target_pairs={{0,32},{32,64},{64,96},{96,128},{128,160},{160,192},{192,224},{224... | collective-permute-start | bytes 688136 | tf_op jit(solution)/shard_map/cond/branch_0_fun/ppermute | solution.py:31
  120.0 48.4 %copy-start.7 = (bf16[28,128,256]{2,1,0:T(8,128)(2,1)S(1)}, bf16[28,128,256]{2,1,0:T(8,128)(2,1)}, u32[]{:S(2)}) copy-start(bf16[28,128,256]{2,1,0:T(8,128)(2,1)} %copy-done.6) | copy-start | bytes 5505028 | tf_op jit(solution)/shard_map/cond
  120.0 9.2 %collective-permute-start.22 = (f32[2,7,32,128]{3,2,1,0:T(8,128)S(1)}, f32[2,7,32,128]{3,2,1,0:T(8,128)S(1)}, u32[]{:S(2)}, u32[]{:S(2)}) collective-permute-start(f32[2,7,32,128]{3,2,1,0:T(8,128)S(1)} %add.401), channel_id=1, source_target_pairs={{0,224},{32,0},{64,32},{96,64},{128,96},{160,128},{192,160},{224,1... | collective-permute-start | bytes 688136 | tf_op jit(solution)/shard_map/cond/branch_0_fun/ppermute | solution.py:31
  129.3 12.9 %collective-permute-start.23 = (f32[28,16,128]{2,1,0:T(8,128)S(1)}, f32[28,16,128]{2,1,0:T(8,128)S(1)}, u32[]{:S(2)}, u32[]{:S(2)}) collective-permute-start(f32[28,16,128]{2,1,0:T(8,128)S(1)} %pad_maximum_fusion.3), channel_id=1, source_target_pairs={{0,16},{16,0},{1,17},{17,1},{2,18},{18,2},{3,19},{19,3},{4,20},{20... | collective-permute-start | bytes 688136 | tf_op jit(solution)/shard_map/cond/branch_0_fun/ppermute | solution.py:26
  133.3 13.7 %collective-permute-start.25 = (f32[28,16,128]{2,1,0:T(8,128)S(1)}, f32[28,16,128]{2,1,0:T(8,128)S(1)}, u32[]{:S(2)}, u32[]{:S(2)}) collective-permute-start(f32[28,16,128]{2,1,0:T(8,128)S(1)} %pad_maximum_fusion.3), channel_id=1, source_target_pairs={{0,31},{1,30},{2,29},{3,28},{4,27},{5,26},{6,25},{7,24},{8,23},{9,... | collective-permute-start | bytes 688136 | tf_op jit(solution)/shard_map/cond/branch_0_fun/ppermute | solution.py:310
  142.3 9.5 %collective-permute-start.24 = (f32[28,16,128]{2,1,0:T(8,128)S(1)}, f32[28,16,128]{2,1,0:T(8,128)S(1)}, u32[]{:S(2)}, u32[]{:S(2)}) collective-permute-start(f32[28,16,128]{2,1,0:T(8,128)S(1)} %get-tuple-element.68), channel_id=1, source_target_pairs={{0,0},{1,15},{2,14},{3,13},{4,12},{5,11},{6,10},{7,9},{8,8},{9,7},... | collective-permute-start | bytes 688136 | tf_op jit(solution)/shard_map/cond/branch_0_fun/ppermute | solution.py:310
  151.8 15.2 %collective-permute-start.26 = (f32[28,16,128]{2,1,0:T(8,128)S(1)}, f32[28,16,128]{2,1,0:T(8,128)S(1)}, u32[]{:S(2)}, u32[]{:S(2)}) collective-permute-start(f32[28,16,128]{2,1,0:T(8,128)S(1)} %add.408), channel_id=1, source_target_pairs={{0,0},{1,241},{2,226},{3,211},{4,196},{5,181},{6,166},{7,151},{8,1... | collective-permute-start | bytes 688136 | tf_op jit(solution)/shard_map/cond/branch_0_fun/ppermute | solution.py:311
  174.8 63.9 %copy-start.8 = (f32[1,256,256]{2,1,0:T(8,128)S(1)}, f32[1,256,256]{2,1,0:T(8,128)}, u32[]{:S(2)}) copy-start(f32[1,256,256]{2,1,0:T(8,128)} %param.10) | copy-start | bytes 786436
  174.8 42.6 %all-to-all-start.3 = ((f32[16,16,1280]{2,1,0:T(8,128)}), f32[16,16,1280]{2,1,0:T(8,128)S(1)}, u32[]{:S(2)}, u32[]{:S(2)}) async-start(f32[16,16,1280]{2,1,0:T(8,128)} %shard_map.85), calls=%async_computation.3 | async-start | bytes 2621440 | tf_op jit(solution)/shard_map/all_to_all | solution.py:411
  187.9 16.1 %collective-permute-start.31 = (f32[4,16,256]{2,1,0:T(8,128)S(1)}, f32[4,16,256]{2,1,0:T(8,128)S(1)}, u32[]{:S(2)}, u32[]{:S(2)}) collective-permute-start(f32[4,16,256]{2,1,0:T(8,128)S(1)} %get-tuple-element.40), channel_id=1, source_target_pairs={{0,31},{1,16},{2,17},{3,18},{4,19},{5,20},{6,21},{7,22},{8,23},{9,... | collective-permute-start | bytes 196616 | tf_op jit(solution)/shard_map/ppermute | solution.py:420
  188.8 15.2 %collective-permute-start.32 = (f32[4,16,256]{2,1,0:T(8,128)S(1)}, f32[4,16,256]{2,1,0:T(8,128)S(1)}, u32[]{:S(2)}, u32[]{:S(2)}) collective-permute-start(f32[4,16,256]{2,1,0:T(8,128)S(1)} %get-tuple-element.40), channel_id=1, source_target_pairs={{0,46},{1,47},{2,32},{3,33},{4,34},{5,35},{6,36},{7,37},{8,38},{9,... | collective-permute-start | bytes 196616 | tf_op jit(solution)/shard_map/ppermute | solution.py:420
  188.8 15.2 %collective-permute-start.33 = (f32[4,16,256]{2,1,0:T(8,128)S(1)}, f32[4,16,256]{2,1,0:T(8,128)S(1)}, u32[]{:S(2)}, u32[]{:S(2)}) collective-permute-start(f32[4,16,256]{2,1,0:T(8,128)S(1)} %get-tuple-element.40), channel_id=1, source_target_pairs={{0,61},{1,62},{2,63},{3,48},{4,49},{5,50},{6,51},{7,52},{8,53},{9,... | collective-permute-start | bytes 196616 | tf_op jit(solution)/shard_map/ppermute | solution.py:420
  204.1 9.1 %collective-permute-start.34 = (f32[4,16,256]{2,1,0:T(8,128)S(1)}, f32[4,16,256]{2,1,0:T(8,128)S(1)}, u32[]{:S(2)}, u32[]{:S(2)}) collective-permute-start(f32[4,16,256]{2,1,0:T(8,128)S(1)} %add_add_fusion.1), channel_id=1, source_target_pairs={{0,76},{1,77},{2,78},{3,79},{4,64},{5,65},{6,66},{7,67},{8,68},{9,... | collective-permute-start | bytes 196616 | tf_op jit(solution)/shard_map/ppermute | solution.py:420
  207.1 7.9 %collective-permute-start.35 = (f32[4,16,256]{2,1,0:T(8,128)S(1)}, f32[4,16,256]{2,1,0:T(8,128)S(1)}, u32[]{:S(2)}, u32[]{:S(2)}) collective-permute-start(f32[4,16,256]{2,1,0:T(8,128)S(1)} %add_add_fusion.1), channel_id=1, source_target_pairs={{0,136},{1,137},{2,138},{3,139},{4,140},{5,141},{6,142},{7,143},{8... | collective-permute-start | bytes 196616 | tf_op jit(solution)/shard_map/ppermute | solution.py:420
  209.1 8.3 %collective-permute-start.36 = (f32[4,16,256]{2,1,0:T(8,128)S(1)}, f32[4,16,256]{2,1,0:T(8,128)S(1)}, u32[]{:S(2)}, u32[]{:S(2)}) collective-permute-start(f32[4,16,256]{2,1,0:T(8,128)S(1)} %add_add_fusion.1), channel_id=1, source_target_pairs={{0,196},{1,197},{2,198},{3,199},{4,200},{5,201},{6,202},{7,203},{8... | collective-permute-start | bytes 196616 | tf_op jit(solution)/shard_map/ppermute | solution.py:420
  218.8 19.9 %all-to-all-start.4 = ((f32[16,16,256]{2,1,0:T(8,128)}), f32[16,16,256]{2,1,0:T(8,128)S(1)}, u32[]{:S(2)}, u32[]{:S(2)}) async-start(f32[16,16,256]{2,1,0:T(8,128)} %shard_map.87), calls=%async_computation.4 | async-start | bytes 524288 | tf_op jit(solution)/shard_map/all_to_all | solution.py:423

commit v2 on v1

--- a/solution.py
+++ b/solution.py
@@ -163,13 +163,13 @@
     lax.fori_loop(tab[COL_START + sib], cap, clear, 0)
 
 
-def unpack_kernel(base, tab, x_ref, o_ref):
+def unpack_kernel(tab, x_ref, o_ref):
     sib, _, cells = o_ref.shape
     blocks = cells // BLK
 
     def sibling(j, carry):
         for b in range(blocks):
-            slot = tab[base + j * blocks + b]
+            slot = tab[COL_SLOT + j * blocks + b]
             o_ref[j, :, b * BLK : (b + 1) * BLK] = jnp.where(
                 slot >= 0, x_ref[jnp.maximum(slot, 0)], 0.0
             )
@@ -180,23 +180,50 @@
 
 def inner_kernel(sib, tab, x_ref, hi_ref, lo_ref, o_ref):
     def sibling(j, carry):
-        def one(q, total):
-            x = x_ref[q]
+        r0 = tab[ROW_START + j]
+        r1 = tab[ROW_START + j + 1]
+
+        def one(i, total):
+            q = r0 + 2 * i
+            after = jnp.where(q + 1 < r1, q + 1, q)
+            x = jnp.concatenate([x_ref[q], jnp.where(after > q, x_ref[after], 0.0)], axis=1)
             x_hi = x.astype(jnp.bfloat16)
             x_lo = (x - x_hi.astype(jnp.float32)).astype(jnp.bfloat16)
-            hi = hi_ref[q]
+            hi = jnp.concatenate([hi_ref[q], hi_ref[after]], axis=0)
+            lo = jnp.concatenate([lo_ref[q], lo_ref[after]], axis=0)
             return total + jnp.dot(
                 jnp.concatenate([x_hi, x_lo, x_hi], axis=1),
-                jnp.concatenate([hi, hi, lo_ref[q]], axis=0),
+                jnp.concatenate([hi, hi, lo], axis=0),
                 preferred_element_type=jnp.float32,
             )
 
         o_ref[j] = lax.fori_loop(
-            tab[ROW_START + j],
-            tab[ROW_START + j + 1],
+            0,
+            (r1 - r0 + 1) // 2,
             one,
             jnp.zeros(o_ref.shape[1:], jnp.float32),
         )
+        return carry
+
+    lax.fori_loop(0, sib, sibling, 0)
+
+
+def slots_kernel(sib, tab, x_ref, o_ref):
+    blocks = o_ref.shape[2] // BLK
+
+    def clear(d, carry):
+        o_ref[d] = jnp.zeros(o_ref.shape[1:], jnp.float32)
+        return carry
+
+    lax.fori_loop(0, o_ref.shape[0], clear, 0)
+
+    def sibling(j, carry):
+        at = tab[OWNER + j]
+        for b in range(blocks):
+            slot = tab[ROW_SLOT + j * blocks + b]
+            o_ref[at, :, b * BLK : (b + 1) * BLK] = jnp.where(
+                slot >= 0, x_ref[jnp.maximum(slot, 0)], 0.0
+            )
         return carry
 
     lax.fori_loop(0, sib, sibling, 0)
@@ -309,24 +336,35 @@
     along = [(r * n_col + k, (-r - k) % n_row * n_col + k) for r, k in spots]
     midway = lax.ppermute(kept, ROW + COL, across) + lax.ppermute(sent, ROW + COL, over)
     moved = lax.ppermute(midway, ROW + COL, along)
+    sent, moved = lax.optimization_barrier((sent, moved))
     total = kept + swapped(sent, "row_1", 1)
-    unpack = lambda base, x: pl.pallas_call(
-        functools.partial(unpack_kernel, base),
+    upper_part = pl.pallas_call(
+        unpack_kernel,
         out_shape=jax.ShapeDtypeStruct((sib, half_rows, col_cells), jnp.float32),
         in_specs=[SMEM, VMEM],
         out_specs=VMEM,
         compiler_params=pltpu.CompilerParams(vmem_limit_bytes=8 << 20),
         cost_estimate=pl.CostEstimate(flops=0, transcendentals=0, bytes_accessed=1 << 20),
-    )(table, x)
-    upper_part = unpack(COL_SLOT, total)
+    )(table, total)
+    slots = pl.pallas_call(
+        functools.partial(slots_kernel, sib),
+        out_shape=jax.ShapeDtypeStruct((n_col, half_rows, row_cells), jnp.float32),
+        in_specs=[SMEM, VMEM],
+        out_specs=VMEM,
+        compiler_params=pltpu.CompilerParams(vmem_limit_bytes=8 << 20),
+        cost_estimate=pl.CostEstimate(flops=0, transcendentals=0, bytes_accessed=2 << 20),
+    )(table, moved)
     inner = pl.pallas_call(
         functools.partial(inner_kernel, sib),
         out_shape=jax.ShapeDtypeStruct((sib, half_rows, width), jnp.float32),
         in_specs=[SMEM] + [VMEM] * 3,
         out_specs=VMEM,
         compiler_params=pltpu.CompilerParams(vmem_limit_bytes=12 << 20),
+        cost_estimate=pl.CostEstimate(
+            flops=6 * cap * half_rows * BLK * width, transcendentals=0, bytes_accessed=6 << 20
+        ),
     )(table, moved, p_hi, p_lo)
-    return upper_part, unpack(ROW_SLOT, moved), inner
+    return upper_part, slots, inner
 
 
 def piece_columns():
@@ -393,7 +431,7 @@
     )
     caps = [c for c in CAPS if c < sib * blocks] + [sib * blocks]
     which = sum((most > c).astype(jnp.int32) for c in caps[:-1])
-    upper_part, moved, inner = lax.switch(
+    upper_part, slots, inner = lax.switch(
         which,
         [functools.partial(listed_products, c, sib) for c in caps],
         table,
@@ -408,7 +446,7 @@
         out_specs=VMEM,
         compiler_params=pltpu.CompilerParams(vmem_limit_bytes=8 << 20),
     )(table, x)
-    gathered = lax.all_to_all(place(moved), COL, 0, 0, tiled=True)
+    gathered = lax.all_to_all(slots, COL, 0, 0, tiled=True)
     for bit in (1, 4):
         others = []
         for away in (bit, 2 * bit, 3 * bit):

time: 239 us -> 238 us (level)
  waiting for transfers between devices: 78.7 us -> 91.6 us
  starting transfers between devices: 108 us -> 96.4 us
  Pallas kernels: 28.1 us -> 23.5 us
    all_to_all x1, starting transfers between devices: 13.1 us -> 4.47 us  [per_device(): gathered = lax.all_to_all(slots, COL, 0, 0, tiled=True)]
    ppermute x1, waiting for transfers between devices: 0.42 us -> 9 us  [listed_products(): lax.ppermute(sent, ROW + COL, over)]
    all_to_all x1, starting transfers between devices: 12.8 us -> 6.89 us  [per_device(): parts = lax.all_to_all(place(inner), COL, 0, 0, tiled=True)]
    ppermute x1, waiting for transfers between devices: 4.77 us -> 0.01 us  [listed_products(): lax.ppermute(kept, ROW + COL, across) + lax.ppermute(sent, ROW + COL, over)]
    ppermute x1, starting transfers between devices: 8.92 us -> 13.1 us  [listed_products(): lax.ppermute(sent, ROW + COL, over)]
    ppermute x4, starting transfers between devices: 11.7 us -> 7.79 us  [swapped(): return lax.ppermute(x, axis, [(i, i ^ bit) for i in range(length)])]
    ppermute x6, starting transfers between devices: 15.9 us -> 19.6 us  [per_device(): others.append(lax.ppermute(inner, ROW + COL, pairs))]
    ppermute x1, waiting for transfers between devices: 6.46 us -> 10.1 us  [listed_products(): moved = lax.ppermute(midway, ROW + COL, along)]
  transfers between devices with their start and end apart: 36 -> 36, of which waited for: 20 -> 21; matrix products, arithmetic and copies ran while one was open for 7% -> 7% of each run, Pallas kernels for 1% -> 3%
where the time goes in v2:
time: 238 us; the launch traced here: 237 us
  starting transfers between devices  96.4 us (41%)
  waiting for transfers between devices  91.6 us (38%)
  Pallas kernels  23.5 us (10%)
  other arithmetic  16.4 us (7%)
  local copies, waits for them, and re-layouts  6.73 us (3%)
    ppermute x20, waiting for transfers between devices, turned(): lax.ppermute(x, axis, [(i, (i + shift) % length) for i in range(length)])  32.5 us
    ppermute x20, starting transfers between devices, turned(): lax.ppermute(x, axis, [(i, (i + shift) % length) for i in range(length)])  27 us
    ppermute x6, starting transfers between devices, per_device(): others.append(lax.ppermute(inner, ROW + COL, pairs))  19.6 us
    ppermute x6, waiting for transfers between devices, per_device(): others.append(lax.ppermute(inner, ROW + COL, pairs))  17.1 us
    ppermute x1, starting transfers between devices, listed_products(): lax.ppermute(sent, ROW + COL, over)  13.1 us
    pallas_call x1, Pallas kernels, listed_products(): pl.pallas_call(functools.partial(product_kernel, cap, sib), out_shape=(ja...  12.7 us
    ppermute x4, waiting for transfers between devices, swapped(): return lax.ppermute(x, axis, [(i, i ^ bit) for i in range(length)])  10.2 us
    ppermute x1, waiting for transfers between devices, listed_products(): moved = lax.ppermute(midway, ROW + COL, along)  10.1 us
  transfers between devices with their start and end apart: 36, of which 21 were waited for; matrix products, arithmetic and copies ran while one was open for 7% of the time, Pallas kernels for 3%

profile of v2, /device:TPU:1, one launch (start us, length us, event | category | flops | bytes accessed | tf_op | source)
XLA Modules:
  0.0 237.3 jit_solution(6650575678676638135)
XLA Ops:
  0.7 2.5 %copy.12 = f32[16,10,8,256]{3,2,1,0:T(8,128)} copy(f32[16,10,8,256]{3,2,0,1:T(8,128)} %bitcast.77) | data formatting | bytes 2621440 | tf_op jit(solution)/shard_map/transpose | solution.py:395
  3.2 6.8 %all-to-all-start.2 = ((f32[16,10,8,256]{3,2,1,0:T(8,128)}), f32[16,10,8,256]{3,2,1,0:T(8,128)S(1)}, u32[]{:S(2)}, u32[]{:S(2)}) async-start(f32[16,10,8,256]{3,2,1,0:T(8,128)} %copy.12), calls=%async_computation.2 | async-start | bytes 2621440 | tf_op jit(solution)/shard_map/all_to_all | solution.py:396
  13.1 0.6 reduce_max.9
  14.5 6.6 %fusion.8 = (bf16[1280,1280]{1,0:T(8,128)(2,1)}, bf16[1280,1280]{1,0:T(8,128)(2,1)}) fusion(f32[1280,1280]{1,0:T(8,128)} %param.8), kind=kLoop, calls=%fused_computation.36 | loop fusion | flops 6553600 | bytes 13107200 | tf_op jit(solution)/shard_map/convert_element_type | solution.py:399
  21.1 7.6 %all-to-all-done.2 = f32[16,10,8,256]{3,2,1,0:T(8,128)S(1)} async-done(((f32[16,10,8,256]{3,2,1,0:T(8,128)}), f32[16,10,8,256]{3,2,1,0:T(8,128)S(1)}, u32[]{:S(2)}, u32[]{:S(2)}) %all-to-all-start.2) | async-done | bytes 1310752 | tf_op jit(solution)/shard_map/all_to_all | solution.py:396
  28.7 149.9 %conditional.1 = (f32[4,16,1280]{2,1,0:T(8,128)S(1)}, f32[16,16,1280]{2,1,0:T(8,128)}, f32[4,16,256]{2,1,0:T(8,128)S(1)}) conditional(s32[]{:T(128)} %clamp.3, (f32[16,10,8,256]{3,2,1,0:T(8,128)S(1)}, s32[362]{0:T(512)S(1)}, bf16[1280,1280]{1,0:T(8,128)(2,1)}, bf16[1280,1280]{1,0:T(8,128)(2,1)}) %tuple.19, (f32[16,10,8,256]{3,2,1,0:T(8,128)S(1)}, ...), branch_computations={%region_12.13_spmd, %region_13.15_spmd} | conditional | flops 127139856 | bytes 134283808 | solution.py:434
  28.7 0.7 branch_0_fun.5
  30.0 5.9 %collective-permute-done = f32[28,8,256]{2,1,0:T(8,128)S(1)} collective-permute-done((f32[28,8,256]{2,1,0:T(8,128)S(1)}, f32[28,8,256]{2,1,0:T(8,128)S(1)}, u32[]{:S(2)}, u32[]{:S(2)}) %collective-permute-start) | collective-permute-done | bytes 229408 | tf_op jit(solution)/shard_map/cond/branch_0_fun/ppermute | solution.py:26
  35.9 1.4 collective-permute-start.4
  37.7 1.1 collective-permute-start.3
  38.9 2.5 %collective-permute-done.4 = f32[28,8,256]{2,1,0:T(8,128)S(1)} collective-permute-done((f32[28,8,256]{2,1,0:T(8,128)S(1)}, f32[28,8,256]{2,1,0:T(8,128)S(1)}, u32[]{:S(2)}, u32[]{:S(2)}) %collective-permute-start.4) | collective-permute-done | bytes 229408 | tf_op jit(solution)/shard_map/cond/branch_0_fun/ppermute | solution.py:31
  41.4 3.4 %collective-permute-start.6 = (f32[28,8,256]{2,1,0:T(8,128)S(1)}, f32[28,8,256]{2,1,0:T(8,128)S(1)}, u32[]{:S(2)}, u32[]{:S(2)}) collective-permute-start(f32[28,8,256]{2,1,0:T(8,128)S(1)} %collective-permute-done.4), channel_id=1, source_target_pairs={{0,6},{2,0},{4,2},{6,4},{1,7},{3,1},{5,3},{7,5},{8,14},{10,8},{12,... | collective-permute-start | bytes 688136 | tf_op jit(solution)/shard_map/cond/branch_0_fun/ppermute | solution.py:31
  44.8 1.5 collective-permute-done.2
  46.4 4.7 %collective-permute-start.7 = (f32[4,28,8,256]{3,2,1,0:T(8,128)S(1)}, f32[4,28,8,256]{3,2,1,0:T(8,128)S(1)}, u32[]{:S(2)}, u32[]{:S(2)}) collective-permute-start(f32[4,28,8,256]{3,2,1,0:T(8,128)S(1)} %pad_maximum_fusion.g0), channel_id=1, source_target_pairs={{0,1},{1,0},{2,3},{3,2},{4,5},{5,4},{6,7},{7,6},{8,9},{9,8},{10,11... | collective-permute-start | bytes 2752520 | tf_op jit(solution)/shard_map/cond/branch_0_fun/ppermute | solution.py:26
  51.3 2.6 %collective-permute-start.8 = (f32[4,28,8,256]{3,2,1,0:T(8,128)S(1)}, f32[4,28,8,256]{3,2,1,0:T(8,128)}, u32[]{:S(2)}, u32[]{:S(2)}) collective-permute-start(f32[4,28,8,256]{3,2,1,0:T(8,128)S(1)} %pad_maximum_fusion.1.g1), channel_id=1, source_target_pairs={{0,1},{1,0},{2,3},{3,2},{4,5},{5,4},{6,7},{7,6},{8,9},{9,8},{10,11... | collective-permute-start | bytes 2752520 | tf_op jit(solution)/shard_map/cond/branch_0_fun/ppermute | solution.py:26
  53.9 2.2 collective-permute-done.8.c1
  56.2 12.7 %branch_0_fun.6 = (f32[8,28,32,128]{3,2,1,0:T(8,128)S(1)}, bf16[28,128,256]{2,1,0:T(8,128)(2,1)S(1)}, bf16[28,128,256]{2,1,0:T(8,128)(2,1)S(1)}) custom-call(s32[362]{0:T(512)S(1)} %get-tuple-element.16.tab, f32[4,28,8,256]{3,2,1,0:T(8,128)S(1)} %pad_maximum_fusion.g0, f32[4,28,8,256]{3,2,1,0:T(8,128)S(1)} %pad_maximum_fusion.1.g1, ...), custom_call_target="tpu_custom_call" | custom-call | tf_op jit(solution)/shard_map/cond/branch_0_fun/pallas_call | solution.py:300
  69.0 1.7 copy-done.1
  71.9 3.7 %collective-permute-start.16 = (f32[2,7,32,128]{3,2,1,0:T(8,128)S(1)}, f32[2,7,32,128]{3,2,1,0:T(8,128)S(1)}, u32[]{:S(2)}, u32[]{:S(2)}) collective-permute-start(f32[2,7,32,128]{3,2,1,0:T(8,128)S(1)} %bitcast.95), channel_id=1, source_target_pairs={{0,224},{32,0},{64,32},{96,64},{128,96},{160,128},{192,160},{224,1... | collective-permute-start | bytes 688136 | tf_op jit(solution)/shard_map/cond/branch_0_fun/ppermute | solution.py:31
  75.5 3.4 %collective-permute-done.9 = f32[14,32,128]{2,1,0:T(8,128)S(1)} collective-permute-done((f32[14,32,128]{2,1,0:T(8,128)S(1)}, f32[14,32,128]{2,1,0:T(8,128)S(1)}, u32[]{:S(2)}, u32[]{:S(2)}) %collective-permute-start.9) | collective-permute-done | bytes 229408 | tf_op jit(solution)/shard_map/cond/branch_0_fun/ppermute | solution.py:31
  78.9 1.0 fusion.6
  80.1 2.7 %collective-permute-start.17 = (f32[2,7,32,128]{3,2,1,0:T(8,128)S(1)}, f32[2,7,32,128]{3,2,1,0:T(8,128)S(1)}, u32[]{:S(2)}, u32[]{:S(2)}) collective-permute-start(f32[2,7,32,128]{3,2,1,0:T(8,128)S(1)} %add.381), channel_id=1, source_target_pairs={{0,224},{32,0},{64,32},{96,64},{128,96},{160,128},{192,160},{224,1... | collective-permute-start | bytes 688136 | tf_op jit(solution)/shard_map/cond/branch_0_fun/ppermute | solution.py:31
  82.8 3.3 %collective-permute-done.10 = f32[14,32,128]{2,1,0:T(8,128)S(1)} collective-permute-done((f32[14,32,128]{2,1,0:T(8,128)S(1)}, f32[14,32,128]{2,1,0:T(8,128)S(1)}, u32[]{:S(2)}, u32[]{:S(2)}) %collective-permute-start.10) | collective-permute-done | bytes 229408 | tf_op jit(solution)/shard_map/cond/branch_0_fun/ppermute | solution.py:31
  86.1 1.0 fusion.5
  87.2 2.7 %collective-permute-start.18 = (f32[2,7,32,128]{3,2,1,0:T(8,128)S(1)}, f32[2,7,32,128]{3,2,1,0:T(8,128)S(1)}, u32[]{:S(2)}, u32[]{:S(2)}) collective-permute-start(f32[2,7,32,128]{3,2,1,0:T(8,128)S(1)} %add.385), channel_id=1, source_target_pairs={{0,224},{32,0},{64,32},{96,64},{128,96},{160,128},{192,160},{224,1... | collective-permute-start | bytes 688136 | tf_op jit(solution)/shard_map/cond/branch_0_fun/ppermute | solution.py:31
  89.9 3.3 %collective-permute-done.11 = f32[14,32,128]{2,1,0:T(8,128)S(1)} collective-permute-done((f32[14,32,128]{2,1,0:T(8,128)S(1)}, f32[14,32,128]{2,1,0:T(8,128)S(1)}, u32[]{:S(2)}, u32[]{:S(2)}) %collective-permute-start.11) | collective-permute-done | bytes 229408 | tf_op jit(solution)/shard_map/cond/branch_0_fun/ppermute | solution.py:31
  93.2 1.0 fusion.4
  94.2 1.4 collective-permute-start.12
  95.6 1.4 collective-permute-start.19
  97.0 5.5 %collective-permute-done.12 = f32[14,32,128]{2,1,0:T(8,128)S(1)} collective-permute-done((f32[14,32,128]{2,1,0:T(8,128)S(1)}, f32[14,32,128]{2,1,0:T(8,128)S(1)}, u32[]{:S(2)}, u32[]{:S(2)}) %collective-permute-start.12) | collective-permute-done | bytes 229408 | tf_op jit(solution)/shard_map/cond/branch_0_fun/ppermute | solution.py:31
  102.6 1.0 fusion.3
  103.7 2.7 %collective-permute-start.20 = (f32[2,7,32,128]{3,2,1,0:T(8,128)S(1)}, f32[2,7,32,128]{3,2,1,0:T(8,128)S(1)}, u32[]{:S(2)}, u32[]{:S(2)}) collective-permute-start(f32[2,7,32,128]{3,2,1,0:T(8,128)S(1)} %add.393), channel_id=1, source_target_pairs={{0,224},{32,0},{64,32},{96,64},{128,96},{160,128},{192,160},{224,1... | collective-permute-start | bytes 688136 | tf_op jit(solution)/shard_map/cond/branch_0_fun/ppermute | solution.py:31
  106.4 5.2 %collective-permute-done.13 = f32[14,32,128]{2,1,0:T(8,128)S(1)} collective-permute-done((f32[14,32,128]{2,1,0:T(8,128)S(1)}, f32[14,32,128]{2,1,0:T(8,128)S(1)}, u32[]{:S(2)}, u32[]{:S(2)}) %collective-permute-start.13) | collective-permute-done | bytes 229408 | tf_op jit(solution)/shard_map/cond/branch_0_fun/ppermute | solution.py:31
  111.6 1.0 fusion.2
  112.8 2.7 %collective-permute-start.21 = (f32[2,7,32,128]{3,2,1,0:T(8,128)S(1)}, f32[2,7,32,128]{3,2,1,0:T(8,128)S(1)}, u32[]{:S(2)}, u32[]{:S(2)}) collective-permute-start(f32[2,7,32,128]{3,2,1,0:T(8,128)S(1)} %add.397), channel_id=1, source_target_pairs={{0,224},{32,0},{64,32},{96,64},{128,96},{160,128},{192,160},{224,1... | collective-permute-start | bytes 688136 | tf_op jit(solution)/shard_map/cond/branch_0_fun/ppermute | solution.py:31
  115.5 4.3 %collective-permute-done.14 = f32[14,32,128]{2,1,0:T(8,128)S(1)} collective-permute-done((f32[14,32,128]{2,1,0:T(8,128)S(1)}, f32[14,32,128]{2,1,0:T(8,128)S(1)}, u32[]{:S(2)}, u32[]{:S(2)}) %collective-permute-start.14) | collective-permute-done | bytes 229408 | tf_op jit(solution)/shard_map/cond/branch_0_fun/ppermute | solution.py:31
  119.8 1.0 fusion.1
  120.9 2.7 %collective-permute-start.22 = (f32[2,7,32,128]{3,2,1,0:T(8,128)S(1)}, f32[2,7,32,128]{3,2,1,0:T(8,128)S(1)}, u32[]{:S(2)}, u32[]{:S(2)}) collective-permute-start(f32[2,7,32,128]{3,2,1,0:T(8,128)S(1)} %add.401), channel_id=1, source_target_pairs={{0,224},{32,0},{64,32},{96,64},{128,96},{160,128},{192,160},{224,1... | collective-permute-start | bytes 688136 | tf_op jit(solution)/shard_map/cond/branch_0_fun/ppermute | solution.py:31
  123.6 3.3 %collective-permute-done.15 = f32[14,32,128]{2,1,0:T(8,128)S(1)} collective-permute-done((f32[14,32,128]{2,1,0:T(8,128)S(1)}, f32[14,32,128]{2,1,0:T(8,128)S(1)}, u32[]{:S(2)}, u32[]{:S(2)}) %collective-permute-start.15) | collective-permute-done | bytes 229408 | tf_op jit(solution)/shard_map/cond/branch_0_fun/ppermute | solution.py:31
  126.9 1.0 fusion
  128.0 6.5 %collective-permute-start.23 = (f32[28,16,128]{2,1,0:T(8,128)S(1)}, f32[28,16,128]{2,1,0:T(8,128)S(1)}, u32[]{:S(2)}, u32[]{:S(2)}) collective-permute-start(f32[28,16,128]{2,1,0:T(8,128)S(1)} %pad_maximum_fusion.2), channel_id=1, source_target_pairs={{0,0},{1,15},{2,14},{3,13},{4,12},{5,11},{6,10},{7,9},{8,8},{9,7},... | collective-permute-start | bytes 688136 | tf_op jit(solution)/shard_map/cond/branch_0_fun/ppermute | solution.py:337
  134.6 13.1 %collective-permute-start.24 = (f32[28,16,128]{2,1,0:T(8,128)S(1)}, f32[28,16,128]{2,1,0:T(8,128)S(1)}, u32[]{:S(2)}, u32[]{:S(2)}) collective-permute-start(f32[28,16,128]{2,1,0:T(8,128)S(1)} %pad_maximum_fusion.3), channel_id=1, source_target_pairs={{0,31},{1,30},{2,29},{3,28},{4,27},{5,26},{6,25},{7,24},{8,23},{9,... | collective-permute-start | bytes 688136 | tf_op jit(solution)/shard_map/cond/branch_0_fun/ppermute | solution.py:337
  147.6 9.0 %collective-permute-done.24 = f32[28,16,128]{2,1,0:T(8,128)S(1)} collective-permute-done((f32[28,16,128]{2,1,0:T(8,128)S(1)}, f32[28,16,128]{2,1,0:T(8,128)S(1)}, u32[]{:S(2)}, u32[]{:S(2)}) %collective-permute-start.24) | collective-permute-done | bytes 229408 | tf_op jit(solution)/shard_map/cond/branch_0_fun/ppermute | solution.py:337
  156.7 4.1 %collective-permute-start.25 = (f32[28,16,128]{2,1,0:T(8,128)S(1)}, f32[28,16,128]{2,1,0:T(8,128)S(1)}, u32[]{:S(2)}, u32[]{:S(2)}) collective-permute-start(f32[28,16,128]{2,1,0:T(8,128)S(1)} %add.407), channel_id=1, source_target_pairs={{0,0},{1,241},{2,226},{3,211},{4,196},{5,181},{6,166},{7,151},{8,1... | collective-permute-start | bytes 688136 | tf_op jit(solution)/shard_map/cond/branch_0_fun/ppermute | solution.py:338
  160.8 10.1 %collective-permute-done.25.x_ref = f32[28,16,128]{2,1,0:T(8,128)S(1)} collective-permute-done((f32[28,16,128]{2,1,0:T(8,128)S(1)}, f32[28,16,128]{2,1,0:T(8,128)S(1)}, u32[]{:S(2)}, u32[]{:S(2)}) %collective-permute-start.25) | collective-permute-done | bytes 229408 | tf_op jit(solution)/shard_map/cond/branch_0_fun/ppermute | solution.py:338
  171.0 1.9 branch_0_fun.8
  172.8 2.8 %branch_0_fun.9 = f32[4,16,256]{2,1,0:T(8,128)S(1)} custom-call(s32[362]{0:T(512)S(1)} %get-tuple-element.16.tab, f32[28,16,128]{2,1,0:T(8,128)S(1)} %collective-permute-done.25.x_ref, bf16[28,128,256]{2,1,0:T(8,128)(2,1)S(1)} %copy-done.5, bf16[28,128,256]{2,1,0:T(8,128)(2,1)S(1)} %copy-done.7), custom_call_target="tpu_custom_call" | custom-call | flops 88080384 | bytes 6291456 | tf_op jit(solution)/shard_map/cond/branch_0_fun/pallas_call | solution.py:357
  175.6 2.1 collective-permute-done.26
  177.7 0.7 branch_0_fun.7
  178.6 0.7 copy-done.11
  179.3 4.5 %all-to-all-start.3 = ((f32[16,16,1280]{2,1,0:T(8,128)}), f32[16,16,1280]{2,1,0:T(8,128)S(1)}, u32[]{:S(2)}, u32[]{:S(2)}) async-start(f32[16,16,1280]{2,1,0:T(8,128)} %get-tuple-element.43), calls=%async_computation.3 | async-start | bytes 2621440 | tf_op jit(solution)/shard_map/all_to_all | solution.py:449
  183.8 2.2 collective-permute-start.31
  186.0 5.2 %collective-permute-start.32 = (f32[4,16,256]{2,1,0:T(8,128)S(1)}, f32[4,16,256]{2,1,0:T(8,128)S(1)}, u32[]{:S(2)}, u32[]{:S(2)}) collective-permute-start(f32[4,16,256]{2,1,0:T(8,128)S(1)} %get-tuple-element.44), channel_id=1, source_target_pairs={{0,46},{1,47},{2,32},{3,33},{4,34},{5,35},{6,36},{7,37},{8,38},{9,... | collective-permute-start | bytes 196616 | tf_op jit(solution)/shard_map/ppermute | solution.py:458
  191.3 8.6 %collective-permute-done.31 = f32[4,16,256]{2,1,0:T(8,128)S(1)} collective-permute-done((f32[4,16,256]{2,1,0:T(8,128)S(1)}, f32[4,16,256]{2,1,0:T(8,128)S(1)}, u32[]{:S(2)}, u32[]{:S(2)}) %collective-permute-start.31) | collective-permute-done | bytes 65568 | tf_op jit(solution)/shard_map/ppermute | solution.py:458
  200.1 8.8 %collective-permute-start.34 = (f32[4,16,256]{2,1,0:T(8,128)S(1)}, f32[4,16,256]{2,1,0:T(8,128)S(1)}, u32[]{:S(2)}, u32[]{:S(2)}) collective-permute-start(f32[4,16,256]{2,1,0:T(8,128)S(1)} %add_add_fusion.1), channel_id=1, source_target_pairs={{0,76},{1,77},{2,78},{3,79},{4,64},{5,65},{6,66},{7,67},{8,68},{9,... | collective-permute-start | bytes 196616 | tf_op jit(solution)/shard_map/ppermute | solution.py:458
  208.9 2.5 %collective-permute-start.35 = (f32[4,16,256]{2,1,0:T(8,128)S(1)}, f32[4,16,256]{2,1,0:T(8,128)S(1)}, u32[]{:S(2)}, u32[]{:S(2)}) collective-permute-start(f32[4,16,256]{2,1,0:T(8,128)S(1)} %add_add_fusion.1), channel_id=1, source_target_pairs={{0,136},{1,137},{2,138},{3,139},{4,140},{5,141},{6,142},{7,143},{8... | collective-permute-start | bytes 196616 | tf_op jit(solution)/shard_map/ppermute | solution.py:458
  211.4 0.9 collective-permute-start.36
  212.3 5.0 %collective-permute-done.35 = f32[4,16,256]{2,1,0:T(8,128)S(1)} collective-permute-done((f32[4,16,256]{2,1,0:T(8,128)S(1)}, f32[4,16,256]{2,1,0:T(8,128)S(1)}, u32[]{:S(2)}, u32[]{:S(2)}) %collective-permute-start.35) | collective-permute-done | bytes 65568 | tf_op jit(solution)/shard_map/ppermute | solution.py:458
  217.3 3.2 %collective-permute-done.36 = f32[4,16,256]{2,1,0:T(8,128)S(1)} collective-permute-done((f32[4,16,256]{2,1,0:T(8,128)S(1)}, f32[4,16,256]{2,1,0:T(8,128)S(1)}, u32[]{:S(2)}, u32[]{:S(2)}) %collective-permute-start.36) | collective-permute-done | bytes 65568 | tf_op jit(solution)/shard_map/ppermute | solution.py:458
  220.6 1.4 shard_map.86
  221.9 6.9 %all-to-all-start.4 = ((f32[16,16,256]{2,1,0:T(8,128)}), f32[16,16,256]{2,1,0:T(8,128)S(1)}, u32[]{:S(2)}, u32[]{:S(2)}) async-start(f32[16,16,256]{2,1,0:T(8,128)} %shard_map.86), calls=%async_computation.4 | async-start | bytes 524288 | tf_op jit(solution)/shard_map/all_to_all | solution.py:461
  228.8 2.0 shard_map.85
  230.9 5.1 %all-to-all-done.4.x_ref = f32[16,16,256]{2,1,0:T(8,128)S(1)} async-done(((f32[16,16,256]{2,1,0:T(8,128)}), f32[16,16,256]{2,1,0:T(8,128)S(1)}, u32[]{:S(2)}, u32[]{:S(2)}) %all-to-all-start.4) | async-done | bytes 262176 | tf_op jit(solution)/shard_map/all_to_all | solution.py:461
  236.0 1.3 shard_map.87
  (97 shorter events, 6.0 us)
Async XLA Ops:
  0.6 9.4 %copy-start.13 = (s32[4]{0:T(128)S(1)}, s32[4]{0:T(128)}, u32[]{:S(2)}) copy-start(s32[4]{0:T(128)} %param.12) | copy-start | bytes 52
  0.6 9.5 %copy-start.12 = (s32[4,96]{1,0:T(4,128)S(1)}, s32[4,96]{1,0:T(4,128)}, u32[]{:S(2)}) copy-start(s32[4,96]{1,0:T(4,128)} %param.11) | copy-start | bytes 4612
  0.7 10.3 %copy-start.14 = (s32[4]{0:T(128)S(1)}, s32[4]{0:T(128)}, u32[]{:S(2)}) copy-start(s32[4]{0:T(128)} %param.13) | copy-start | bytes 52
  3.2 25.5 %all-to-all-start.2 = ((f32[16,10,8,256]{3,2,1,0:T(8,128)}), f32[16,10,8,256]{3,2,1,0:T(8,128)S(1)}, u32[]{:S(2)}, u32[]{:S(2)}) async-start(f32[16,10,8,256]{3,2,1,0:T(8,128)} %copy.12), calls=%async_computation.2 | async-start | bytes 2621440 | tf_op jit(solution)/shard_map/all_to_all | solution.py:396
  29.4 6.5 %collective-permute-start = (f32[28,8,256]{2,1,0:T(8,128)S(1)}, f32[28,8,256]{2,1,0:T(8,128)S(1)}, u32[]{:S(2)}, u32[]{:S(2)}) collective-permute-start(f32[28,8,256]{2,1,0:T(8,128)S(1)} %branch_0_fun.5), channel_id=1, source_target_pairs={{0,8},{8,0},{1,9},{9,1},{2,10},{10,2},{3,11},{11,3},{4,12},{12,4},... | collective-permute-start | bytes 688136 | tf_op jit(solution)/shard_map/cond/branch_0_fun/ppermute | solution.py:26
  29.8 9.1 %collective-permute-start.1 = (f32[28,8,256]{2,1,0:T(8,128)S(1)}, f32[28,8,256]{2,1,0:T(8,128)S(1)}, u32[]{:S(2)}, u32[]{:S(2)}) collective-permute-start(f32[28,8,256]{2,1,0:T(8,128)S(1)} %branch_0_fun.5), channel_id=1, source_target_pairs={{0,2},{2,4},{4,6},{6,0},{1,3},{3,5},{5,7},{7,1},{8,10},{10,12},{12... | collective-permute-start | bytes 688136 | tf_op jit(solution)/shard_map/cond/branch_0_fun/ppermute | solution.py:31
  35.9 5.5 %collective-permute-start.4 = (f32[28,8,256]{2,1,0:T(8,128)S(1)}, f32[28,8,256]{2,1,0:T(8,128)S(1)}, u32[]{:S(2)}, u32[]{:S(2)}) collective-permute-start(f32[28,8,256]{2,1,0:T(8,128)S(1)} %collective-permute-done), channel_id=1, source_target_pairs={{0,6},{2,0},{4,2},{6,4},{1,7},{3,1},{5,3},{7,5},{8,14},{10,8},{12,... | collective-permute-start | bytes 688136 | tf_op jit(solution)/shard_map/cond/branch_0_fun/ppermute | solution.py:31
  37.4 9.0 %collective-permute-start.2 = (f32[28,8,256]{2,1,0:T(8,128)S(1)}, f32[28,8,256]{2,1,0:T(8,128)S(1)}, u32[]{:S(2)}, u32[]{:S(2)}) collective-permute-start(f32[28,8,256]{2,1,0:T(8,128)S(1)} %branch_0_fun.5), channel_id=1, source_target_pairs={{0,6},{2,0},{4,2},{6,4},{1,7},{3,1},{5,3},{7,5},{8,14},{10,8},{12,... | collective-permute-start | bytes 688136 | tf_op jit(solution)/shard_map/cond/branch_0_fun/ppermute | solution.py:31
  37.7 13.5 %collective-permute-start.3 = (f32[28,8,256]{2,1,0:T(8,128)S(1)}, f32[28,8,256]{2,1,0:T(8,128)S(1)}, u32[]{:S(2)}, u32[]{:S(2)}) collective-permute-start(f32[28,8,256]{2,1,0:T(8,128)S(1)} %collective-permute-done), channel_id=1, source_target_pairs={{0,2},{2,4},{4,6},{6,0},{1,3},{3,5},{5,7},{7,1},{8,10},{10,12},{12... | collective-permute-start | bytes 688136 | tf_op jit(solution)/shard_map/cond/branch_0_fun/ppermute | solution.py:31
  38.8 12.3 %collective-permute-start.5 = (f32[28,8,256]{2,1,0:T(8,128)S(1)}, f32[28,8,256]{2,1,0:T(8,128)S(1)}, u32[]{:S(2)}, u32[]{:S(2)}) collective-permute-start(f32[28,8,256]{2,1,0:T(8,128)S(1)} %collective-permute-done.1), channel_id=1, source_target_pairs={{0,2},{2,4},{4,6},{6,0},{1,3},{3,5},{5,7},{7,1},{8,10},{10,12},{12... | collective-permute-start | bytes 688136 | tf_op jit(solution)/shard_map/cond/branch_0_fun/ppermute | solution.py:31
  41.4 9.8 %collective-permute-start.6 = (f32[28,8,256]{2,1,0:T(8,128)S(1)}, f32[28,8,256]{2,1,0:T(8,128)S(1)}, u32[]{:S(2)}, u32[]{:S(2)}) collective-permute-start(f32[28,8,256]{2,1,0:T(8,128)S(1)} %collective-permute-done.4), channel_id=1, source_target_pairs={{0,6},{2,0},{4,2},{6,4},{1,7},{3,1},{5,3},{7,5},{8,14},{10,8},{12,... | collective-permute-start | bytes 688136 | tf_op jit(solution)/shard_map/cond/branch_0_fun/ppermute | solution.py:31
  46.4 7.5 %collective-permute-start.7 = (f32[4,28,8,256]{3,2,1,0:T(8,128)S(1)}, f32[4,28,8,256]{3,2,1,0:T(8,128)S(1)}, u32[]{:S(2)}, u32[]{:S(2)}) collective-permute-start(f32[4,28,8,256]{3,2,1,0:T(8,128)S(1)} %pad_maximum_fusion.g0), channel_id=1, source_target_pairs={{0,1},{1,0},{2,3},{3,2},{4,5},{5,4},{6,7},{7,6},{8,9},{9,8},{10,11... | collective-permute-start | bytes 2752520 | tf_op jit(solution)/shard_map/cond/branch_0_fun/ppermute | solution.py:26
  51.3 4.8 %collective-permute-start.8 = (f32[4,28,8,256]{3,2,1,0:T(8,128)S(1)}, f32[4,28,8,256]{3,2,1,0:T(8,128)}, u32[]{:S(2)}, u32[]{:S(2)}) collective-permute-start(f32[4,28,8,256]{3,2,1,0:T(8,128)S(1)} %pad_maximum_fusion.1.g1), channel_id=1, source_target_pairs={{0,1},{1,0},{2,3},{3,2},{4,5},{5,4},{6,7},{7,6},{8,9},{9,8},{10,11... | collective-permute-start | bytes 2752520 | tf_op jit(solution)/shard_map/cond/branch_0_fun/ppermute | solution.py:26
  68.9 1.8 copy-start.1
  68.9 2.4 %copy-start.4 = (bf16[28,128,256]{2,1,0:T(8,128)(2,1)}, bf16[28,128,256]{2,1,0:T(8,128)(2,1)S(1)}, u32[]{:S(2)}) copy-start(bf16[28,128,256]{2,1,0:T(8,128)(2,1)S(1)} %get-tuple-element.23.hi_ref) | copy-start | bytes 5505028 | tf_op jit(solution)/shard_map/cond
  68.9 2.9 %copy-start.6 = (bf16[28,128,256]{2,1,0:T(8,128)(2,1)}, bf16[28,128,256]{2,1,0:T(8,128)(2,1)S(1)}, u32[]{:S(2)}) copy-start(bf16[28,128,256]{2,1,0:T(8,128)(2,1)S(1)} %get-tuple-element.24.lo_ref) | copy-start | bytes 5505028 | tf_op jit(solution)/shard_map/cond
  71.9 7.1 %collective-permute-start.9 = (f32[14,32,128]{2,1,0:T(8,128)S(1)}, f32[14,32,128]{2,1,0:T(8,128)S(1)}, u32[]{:S(2)}, u32[]{:S(2)}) collective-permute-start(f32[14,32,128]{2,1,0:T(8,128)S(1)} %get-tuple-element.61), channel_id=1, source_target_pairs={{0,32},{32,64},{64,96},{96,128},{128,160},{160,192},{192,224},{224... | collective-permute-start | bytes 688136 | tf_op jit(solution)/shard_map/cond/branch_0_fun/ppermute | solution.py:31
  71.9 8.2 %collective-permute-start.16 = (f32[2,7,32,128]{3,2,1,0:T(8,128)S(1)}, f32[2,7,32,128]{3,2,1,0:T(8,128)S(1)}, u32[]{:S(2)}, u32[]{:S(2)}) collective-permute-start(f32[2,7,32,128]{3,2,1,0:T(8,128)S(1)} %bitcast.95), channel_id=1, source_target_pairs={{0,224},{32,0},{64,32},{96,64},{128,96},{160,128},{192,160},{224,1... | collective-permute-start | bytes 688136 | tf_op jit(solution)/shard_map/cond/branch_0_fun/ppermute | solution.py:31
  79.9 6.2 %collective-permute-start.10 = (f32[14,32,128]{2,1,0:T(8,128)S(1)}, f32[14,32,128]{2,1,0:T(8,128)S(1)}, u32[]{:S(2)}, u32[]{:S(2)}) collective-permute-start(f32[14,32,128]{2,1,0:T(8,128)S(1)} %fusion.6), channel_id=1, source_target_pairs={{0,32},{32,64},{64,96},{96,128},{128,160},{160,192},{192,224},{224... | collective-permute-start | bytes 688136 | tf_op jit(solution)/shard_map/cond/branch_0_fun/ppermute | solution.py:31
  80.1 7.1 %collective-permute-start.17 = (f32[2,7,32,128]{3,2,1,0:T(8,128)S(1)}, f32[2,7,32,128]{3,2,1,0:T(8,128)S(1)}, u32[]{:S(2)}, u32[]{:S(2)}) collective-permute-start(f32[2,7,32,128]{3,2,1,0:T(8,128)S(1)} %add.381), channel_id=1, source_target_pairs={{0,224},{32,0},{64,32},{96,64},{128,96},{160,128},{192,160},{224,1... | collective-permute-start | bytes 688136 | tf_op jit(solution)/shard_map/cond/branch_0_fun/ppermute | solution.py:31
  87.0 6.2 %collective-permute-start.11 = (f32[14,32,128]{2,1,0:T(8,128)S(1)}, f32[14,32,128]{2,1,0:T(8,128)S(1)}, u32[]{:S(2)}, u32[]{:S(2)}) collective-permute-start(f32[14,32,128]{2,1,0:T(8,128)S(1)} %fusion.5), channel_id=1, source_target_pairs={{0,32},{32,64},{64,96},{96,128},{128,160},{160,192},{192,224},{224... | collective-permute-start | bytes 688136 | tf_op jit(solution)/shard_map/cond/branch_0_fun/ppermute | solution.py:31
  87.2 8.4 %collective-permute-start.18 = (f32[2,7,32,128]{3,2,1,0:T(8,128)S(1)}, f32[2,7,32,128]{3,2,1,0:T(8,128)S(1)}, u32[]{:S(2)}, u32[]{:S(2)}) collective-permute-start(f32[2,7,32,128]{3,2,1,0:T(8,128)S(1)} %add.385), channel_id=1, source_target_pairs={{0,224},{32,0},{64,32},{96,64},{128,96},{160,128},{192,160},{224,1... | collective-permute-start | bytes 688136 | tf_op jit(solution)/shard_map/cond/branch_0_fun/ppermute | solution.py:31
  94.2 8.4 %collective-permute-start.12 = (f32[14,32,128]{2,1,0:T(8,128)S(1)}, f32[14,32,128]{2,1,0:T(8,128)S(1)}, u32[]{:S(2)}, u32[]{:S(2)}) collective-permute-start(f32[14,32,128]{2,1,0:T(8,128)S(1)} %fusion.4), channel_id=1, source_target_pairs={{0,32},{32,64},{64,96},{96,128},{128,160},{160,192},{192,224},{224... | collective-permute-start | bytes 688136 | tf_op jit(solution)/shard_map/cond/branch_0_fun/ppermute | solution.py:31
  95.6 8.0 %collective-permute-start.19 = (f32[2,7,32,128]{3,2,1,0:T(8,128)S(1)}, f32[2,7,32,128]{3,2,1,0:T(8,128)S(1)}, u32[]{:S(2)}, u32[]{:S(2)}) collective-permute-start(f32[2,7,32,128]{3,2,1,0:T(8,128)S(1)} %add.389), channel_id=1, source_target_pairs={{0,224},{32,0},{64,32},{96,64},{128,96},{160,128},{192,160},{224,1... | collective-permute-start | bytes 688136 | tf_op jit(solution)/shard_map/cond/branch_0_fun/ppermute | solution.py:31
  103.6 8.1 %collective-permute-start.13 = (f32[14,32,128]{2,1,0:T(8,128)S(1)}, f32[14,32,128]{2,1,0:T(8,128)S(1)}, u32[]{:S(2)}, u32[]{:S(2)}) collective-permute-start(f32[14,32,128]{2,1,0:T(8,128)S(1)} %fusion.3), channel_id=1, source_target_pairs={{0,32},{32,64},{64,96},{96,128},{128,160},{160,192},{192,224},{224... | collective-permute-start | bytes 688136 | tf_op jit(solution)/shard_map/cond/branch_0_fun/ppermute | solution.py:31
  103.7 9.0 %collective-permute-start.20 = (f32[2,7,32,128]{3,2,1,0:T(8,128)S(1)}, f32[2,7,32,128]{3,2,1,0:T(8,128)S(1)}, u32[]{:S(2)}, u32[]{:S(2)}) collective-permute-start(f32[2,7,32,128]{3,2,1,0:T(8,128)S(1)} %add.393), channel_id=1, source_target_pairs={{0,224},{32,0},{64,32},{96,64},{128,96},{160,128},{192,160},{224,1... | collective-permute-start | bytes 688136 | tf_op jit(solution)/shard_map/cond/branch_0_fun/ppermute | solution.py:31
  112.6 7.2 %collective-permute-start.14 = (f32[14,32,128]{2,1,0:T(8,128)S(1)}, f32[14,32,128]{2,1,0:T(8,128)S(1)}, u32[]{:S(2)}, u32[]{:S(2)}) collective-permute-start(f32[14,32,128]{2,1,0:T(8,128)S(1)} %fusion.2), channel_id=1, source_target_pairs={{0,32},{32,64},{64,96},{96,128},{128,160},{160,192},{192,224},{224... | collective-permute-start | bytes 688136 | tf_op jit(solution)/shard_map/cond/branch_0_fun/ppermute | solution.py:31
  112.8 60.0 %copy-start.5 = (bf16[28,128,256]{2,1,0:T(8,128)(2,1)S(1)}, bf16[28,128,256]{2,1,0:T(8,128)(2,1)}, u32[]{:S(2)}) copy-start(bf16[28,128,256]{2,1,0:T(8,128)(2,1)} %copy-done.4) | copy-start | bytes 5505028 | tf_op jit(solution)/shard_map/cond
  112.8 8.1 %collective-permute-start.21 = (f32[2,7,32,128]{3,2,1,0:T(8,128)S(1)}, f32[2,7,32,128]{3,2,1,0:T(8,128)S(1)}, u32[]{:S(2)}, u32[]{:S(2)}) collective-permute-start(f32[2,7,32,128]{3,2,1,0:T(8,128)S(1)} %add.397), channel_id=1, source_target_pairs={{0,224},{32,0},{64,32},{96,64},{128,96},{160,128},{192,160},{224,1... | collective-permute-start | bytes 688136 | tf_op jit(solution)/shard_map/cond/branch_0_fun/ppermute | solution.py:31
  120.7 6.2 %collective-permute-start.15 = (f32[14,32,128]{2,1,0:T(8,128)S(1)}, f32[14,32,128]{2,1,0:T(8,128)S(1)}, u32[]{:S(2)}, u32[]{:S(2)}) collective-permute-start(f32[14,32,128]{2,1,0:T(8,128)S(1)} %fusion.1), channel_id=1, source_target_pairs={{0,32},{32,64},{64,96},{96,128},{128,160},{160,192},{192,224},{224... | collective-permute-start | bytes 688136 | tf_op jit(solution)/shard_map/cond/branch_0_fun/ppermute | solution.py:31
  120.9 52.0 %copy-start.7 = (bf16[28,128,256]{2,1,0:T(8,128)(2,1)S(1)}, bf16[28,128,256]{2,1,0:T(8,128)(2,1)}, u32[]{:S(2)}) copy-start(bf16[28,128,256]{2,1,0:T(8,128)(2,1)} %copy-done.6) | copy-start | bytes 5505028 | tf_op jit(solution)/shard_map/cond
  120.9 7.0 %collective-permute-start.22 = (f32[2,7,32,128]{3,2,1,0:T(8,128)S(1)}, f32[2,7,32,128]{3,2,1,0:T(8,128)S(1)}, u32[]{:S(2)}, u32[]{:S(2)}) collective-permute-start(f32[2,7,32,128]{3,2,1,0:T(8,128)S(1)} %add.401), channel_id=1, source_target_pairs={{0,224},{32,0},{64,32},{96,64},{128,96},{160,128},{192,160},{224,1... | collective-permute-start | bytes 688136 | tf_op jit(solution)/shard_map/cond/branch_0_fun/ppermute | solution.py:31
  128.0 19.6 %collective-permute-start.23 = (f32[28,16,128]{2,1,0:T(8,128)S(1)}, f32[28,16,128]{2,1,0:T(8,128)S(1)}, u32[]{:S(2)}, u32[]{:S(2)}) collective-permute-start(f32[28,16,128]{2,1,0:T(8,128)S(1)} %pad_maximum_fusion.2), channel_id=1, source_target_pairs={{0,0},{1,15},{2,14},{3,13},{4,12},{5,11},{6,10},{7,9},{8,8},{9,7},... | collective-permute-start | bytes 688136 | tf_op jit(solution)/shard_map/cond/branch_0_fun/ppermute | solution.py:337
  134.6 22.1 %collective-permute-start.24 = (f32[28,16,128]{2,1,0:T(8,128)S(1)}, f32[28,16,128]{2,1,0:T(8,128)S(1)}, u32[]{:S(2)}, u32[]{:S(2)}) collective-permute-start(f32[28,16,128]{2,1,0:T(8,128)S(1)} %pad_maximum_fusion.3), channel_id=1, source_target_pairs={{0,31},{1,30},{2,29},{3,28},{4,27},{5,26},{6,25},{7,24},{8,23},{9,... | collective-permute-start | bytes 688136 | tf_op jit(solution)/shard_map/cond/branch_0_fun/ppermute | solution.py:337
  156.7 14.2 %collective-permute-start.25 = (f32[28,16,128]{2,1,0:T(8,128)S(1)}, f32[28,16,128]{2,1,0:T(8,128)S(1)}, u32[]{:S(2)}, u32[]{:S(2)}) collective-permute-start(f32[28,16,128]{2,1,0:T(8,128)S(1)} %add.407), channel_id=1, source_target_pairs={{0,0},{1,241},{2,226},{3,211},{4,196},{5,181},{6,166},{7,151},{8,1... | collective-permute-start | bytes 688136 | tf_op jit(solution)/shard_map/cond/branch_0_fun/ppermute | solution.py:338
  170.9 6.8 %collective-permute-start.26 = (f32[28,16,128]{2,1,0:T(8,128)S(1)}, f32[28,16,128]{2,1,0:T(8,128)S(1)}, u32[]{:S(2)}, u32[]{:S(2)}) collective-permute-start(f32[28,16,128]{2,1,0:T(8,128)S(1)} %pad_maximum_fusion.3), channel_id=1, source_target_pairs={{0,16},{16,0},{1,17},{17,1},{2,18},{18,2},{3,19},{19,3},{4,20},{20... | collective-permute-start | bytes 688136 | tf_op jit(solution)/shard_map/cond/branch_0_fun/ppermute | solution.py:26
  178.6 0.7 copy-start.11
  179.3 56.7 %copy-start.8 = (f32[1,256,256]{2,1,0:T(8,128)S(1)}, f32[1,256,256]{2,1,0:T(8,128)}, u32[]{:S(2)}) copy-start(f32[1,256,256]{2,1,0:T(8,128)} %param.10) | copy-start | bytes 786436
  179.3 41.3 %all-to-all-start.3 = ((f32[16,16,1280]{2,1,0:T(8,128)}), f32[16,16,1280]{2,1,0:T(8,128)S(1)}, u32[]{:S(2)}, u32[]{:S(2)}) async-start(f32[16,16,1280]{2,1,0:T(8,128)} %get-tuple-element.43), calls=%async_computation.3 | async-start | bytes 2621440 | tf_op jit(solution)/shard_map/all_to_all | solution.py:449
  183.8 16.0 %collective-permute-start.31 = (f32[4,16,256]{2,1,0:T(8,128)S(1)}, f32[4,16,256]{2,1,0:T(8,128)S(1)}, u32[]{:S(2)}, u32[]{:S(2)}) collective-permute-start(f32[4,16,256]{2,1,0:T(8,128)S(1)} %get-tuple-element.44), channel_id=1, source_target_pairs={{0,31},{1,16},{2,17},{3,18},{4,19},{5,20},{6,21},{7,22},{8,23},{9,... | collective-permute-start | bytes 196616 | tf_op jit(solution)/shard_map/ppermute | solution.py:458
  186.0 13.9 %collective-permute-start.32 = (f32[4,16,256]{2,1,0:T(8,128)S(1)}, f32[4,16,256]{2,1,0:T(8,128)S(1)}, u32[]{:S(2)}, u32[]{:S(2)}) collective-permute-start(f32[4,16,256]{2,1,0:T(8,128)S(1)} %get-tuple-element.44), channel_id=1, source_target_pairs={{0,46},{1,47},{2,32},{3,33},{4,34},{5,35},{6,36},{7,37},{8,38},{9,... | collective-permute-start | bytes 196616 | tf_op jit(solution)/shard_map/ppermute | solution.py:458
  191.2 8.9 %collective-permute-start.33 = (f32[4,16,256]{2,1,0:T(8,128)S(1)}, f32[4,16,256]{2,1,0:T(8,128)S(1)}, u32[]{:S(2)}, u32[]{:S(2)}) collective-permute-start(f32[4,16,256]{2,1,0:T(8,128)S(1)} %get-tuple-element.44), channel_id=1, source_target_pairs={{0,61},{1,62},{2,63},{3,48},{4,49},{5,50},{6,51},{7,52},{8,53},{9,... | collective-permute-start | bytes 196616 | tf_op jit(solution)/shard_map/ppermute | solution.py:458
  200.1 12.2 %collective-permute-start.34 = (f32[4,16,256]{2,1,0:T(8,128)S(1)}, f32[4,16,256]{2,1,0:T(8,128)S(1)}, u32[]{:S(2)}, u32[]{:S(2)}) collective-permute-start(f32[4,16,256]{2,1,0:T(8,128)S(1)} %add_add_fusion.1), channel_id=1, source_target_pairs={{0,76},{1,77},{2,78},{3,79},{4,64},{5,65},{6,66},{7,67},{8,68},{9,... | collective-permute-start | bytes 196616 | tf_op jit(solution)/shard_map/ppermute | solution.py:458
  208.9 8.4 %collective-permute-start.35 = (f32[4,16,256]{2,1,0:T(8,128)S(1)}, f32[4,16,256]{2,1,0:T(8,128)S(1)}, u32[]{:S(2)}, u32[]{:S(2)}) collective-permute-start(f32[4,16,256]{2,1,0:T(8,128)S(1)} %add_add_fusion.1), channel_id=1, source_target_pairs={{0,136},{1,137},{2,138},{3,139},{4,140},{5,141},{6,142},{7,143},{8... | collective-permute-start | bytes 196616 | tf_op jit(solution)/shard_map/ppermute | solution.py:458
  211.4 9.2 %collective-permute-start.36 = (f32[4,16,256]{2,1,0:T(8,128)S(1)}, f32[4,16,256]{2,1,0:T(8,128)S(1)}, u32[]{:S(2)}, u32[]{:S(2)}) collective-permute-start(f32[4,16,256]{2,1,0:T(8,128)S(1)} %add_add_fusion.1), channel_id=1, source_target_pairs={{0,196},{1,197},{2,198},{3,199},{4,200},{5,201},{6,202},{7,203},{8... | collective-permute-start | bytes 196616 | tf_op jit(solution)/shard_map/ppermute | solution.py:458
  221.9 14.1 %all-to-all-start.4 = ((f32[16,16,256]{2,1,0:T(8,128)}), f32[16,16,256]{2,1,0:T(8,128)S(1)}, u32[]{:S(2)}, u32[]{:S(2)}) async-start(f32[16,16,256]{2,1,0:T(8,128)} %shard_map.86), calls=%async_computation.4 | async-start | bytes 524288 | tf_op jit(solution)/shard_map/all_to_all | solution.py:461

commit v3 on v2

--- a/solution.py
+++ b/solution.py
@@ -53,6 +53,18 @@
 
 def padded(values, length):
     return jnp.pad(values.astype(jnp.int32), (0, length - values.shape[0]))
+
+
+def cut_kernel(x_ref, o_ref):
+    pieces, blocks, rows, _ = o_ref.shape
+
+    def block(b, carry):
+        for p in range(pieces):
+            at = pl.multiple_of((b * pieces + p) * rows, SUB)
+            o_ref[p, b] = x_ref[pl.ds(at, rows), :]
+        return carry
+
+    lax.fori_loop(0, blocks, block, 0)
 
 
 def pick_kernel(cap, tab, x_ref, o_ref):
@@ -392,7 +404,13 @@
     row_index = lax.axis_index(ROW)
     col_index = lax.axis_index(COL)
     blocks = row_cells // BLK
-    cut = l_store[0].reshape(blocks, n_col, SUB, width).transpose(1, 0, 2, 3)
+    cut = pl.pallas_call(
+        cut_kernel,
+        out_shape=jax.ShapeDtypeStruct((n_col, blocks, SUB, width), jnp.float32),
+        in_specs=[VMEM],
+        out_specs=VMEM,
+        compiler_params=pltpu.CompilerParams(vmem_limit_bytes=4 << 20),
+    )(l_store[0])
     scattered = lax.all_to_all(cut, COL, 0, 0, tiled=True)
     rounded = lax.reduce_precision(anc_inverse, 8, 7)
     a_hi = rounded.astype(jnp.bfloat16)

time: 238 us -> 234 us (0.983)
  waiting for transfers between devices: 91.6 us -> 87.9 us
    ppermute x1, starting transfers between devices: 13.1 us -> 8.49 us  [listed_products(): lax.ppermute(sent, ROW + COL, over)]
    ppermute x1, starting transfers between devices: 6.53 us -> 3.34 us  [listed_products(): lax.ppermute(kept, ROW + COL, across) + lax.ppermute(sent, ROW + COL, over)]
    ppermute x4, starting transfers between devices: 7.79 us -> 10.8 us  [swapped(): return lax.ppermute(x, axis, [(i, i ^ bit) for i in range(length)])]
    ppermute x6, waiting for transfers between devices: 17.1 us -> 14.4 us  [per_device(): others.append(lax.ppermute(inner, ROW + COL, pairs))]
    transpose x1 -> x0, local copies, waits for them, and re-layouts: 2.53 us -> none  [per_device(): cut = l_store[0].reshape(blocks, n_col, SUB, width).transpose(1, 0, 2, 3)]
  transfers between devices with their start and end apart: 36 -> 36, of which waited for: 21 -> 19; matrix products, arithmetic and copies ran while one was open for 7% -> 7% of each run, Pallas kernels for 3% -> 3%
where the time goes in v3:
time: 234 us; the launch traced here: 232 us
  starting transfers between devices  96.6 us (41%)
  waiting for transfers between devices  87.9 us (38%)
  Pallas kernels  22.7 us (10%)
  other arithmetic  16.4 us (7%)
  local copies, waits for them, and re-layouts  5.52 us (2%)
    ppermute x20, waiting for transfers between devices, turned(): lax.ppermute(x, axis, [(i, (i + shift) % length) for i in range(length)])  32.8 us
    ppermute x20, starting transfers between devices, turned(): lax.ppermute(x, axis, [(i, (i + shift) % length) for i in range(length)])  28.8 us
    ppermute x6, starting transfers between devices, per_device(): others.append(lax.ppermute(inner, ROW + COL, pairs))  20.8 us
    ppermute x6, waiting for transfers between devices, per_device(): others.append(lax.ppermute(inner, ROW + COL, pairs))  14.4 us
    pallas_call x1, Pallas kernels, listed_products(): pl.pallas_call(functools.partial(product_kernel, cap, sib), out_shape=(ja...  11.3 us
    ppermute x1, waiting for transfers between devices, listed_products(): moved = lax.ppermute(midway, ROW + COL, along)  11.2 us
    ppermute x4, starting transfers between devices, swapped(): return lax.ppermute(x, axis, [(i, i ^ bit) for i in range(length)])  10.8 us
    ppermute x1, waiting for transfers between devices, listed_products(): lax.ppermute(sent, ROW + COL, over)  8.52 us
  transfers between devices with their start and end apart: 36, of which 19 were waited for; matrix products, arithmetic and copies ran while one was open for 7% of the time, Pallas kernels for 3%

profile of v3, /device:TPU:1, one launch (start us, length us, event | category | flops | bytes accessed | tf_op | source)
XLA Modules:
  0.0 232.0 jit_solution(2607597215598492520)
XLA Ops:
  0.7 1.3 copy-done.8
  2.0 1.3 shard_map.85
  3.3 6.8 %all-to-all-start.2 = ((f32[16,10,8,256]{3,2,1,0:T(8,128)}), f32[16,10,8,256]{3,2,1,0:T(8,128)S(1)}, u32[]{:S(2)}, u32[]{:S(2)}) async-start(f32[16,10,8,256]{3,2,1,0:T(8,128)} %shard_map.85), calls=%async_computation.2 | async-start | bytes 2621440 | tf_op jit(solution)/shard_map/all_to_all | solution.py:414
  14.6 6.6 %fusion.8 = (bf16[1280,1280]{1,0:T(8,128)(2,1)}, bf16[1280,1280]{1,0:T(8,128)(2,1)}) fusion(f32[1280,1280]{1,0:T(8,128)} %param.8), kind=kLoop, calls=%fused_computation.36 | loop fusion | flops 6553600 | bytes 13107200 | tf_op jit(solution)/shard_map/convert_element_type | solution.py:417
  21.2 7.6 %all-to-all-done.2 = f32[16,10,8,256]{3,2,1,0:T(8,128)S(1)} async-done(((f32[16,10,8,256]{3,2,1,0:T(8,128)}), f32[16,10,8,256]{3,2,1,0:T(8,128)S(1)}, u32[]{:S(2)}, u32[]{:S(2)}) %all-to-all-start.2) | async-done | bytes 1310752 | tf_op jit(solution)/shard_map/all_to_all | solution.py:414
  28.7 143.6 %conditional.1 = (f32[4,16,1280]{2,1,0:T(8,128)S(1)}, f32[16,16,1280]{2,1,0:T(8,128)}, f32[4,16,256]{2,1,0:T(8,128)S(1)}) conditional(s32[]{:T(128)} %clamp.3, (f32[16,10,8,256]{3,2,1,0:T(8,128)S(1)}, s32[362]{0:T(512)S(1)}, bf16[1280,1280]{1,0:T(8,128)(2,1)}, bf16[1280,1280]{1,0:T(8,128)(2,1)}) %tuple.19, (f32[16,10,8,256]{3,2,1,0:T(8,128)S(1)}, ...), branch_computations={%region_12.13_spmd, %region_13.15_spmd} | conditional | flops 127139856 | bytes 134283808 | solution.py:452
  28.8 0.7 branch_0_fun.5
  30.1 5.9 %collective-permute-done = f32[28,8,256]{2,1,0:T(8,128)S(1)} collective-permute-done((f32[28,8,256]{2,1,0:T(8,128)S(1)}, f32[28,8,256]{2,1,0:T(8,128)S(1)}, u32[]{:S(2)}, u32[]{:S(2)}) %collective-permute-start) | collective-permute-done | bytes 229408 | tf_op jit(solution)/shard_map/cond/branch_0_fun/ppermute | solution.py:26
  36.0 1.4 collective-permute-start.4
  37.8 1.1 collective-permute-start.3
  38.9 2.5 %collective-permute-done.4 = f32[28,8,256]{2,1,0:T(8,128)S(1)} collective-permute-done((f32[28,8,256]{2,1,0:T(8,128)S(1)}, f32[28,8,256]{2,1,0:T(8,128)S(1)}, u32[]{:S(2)}, u32[]{:S(2)}) %collective-permute-start.4) | collective-permute-done | bytes 229408 | tf_op jit(solution)/shard_map/cond/branch_0_fun/ppermute | solution.py:31
  41.5 3.4 %collective-permute-start.6 = (f32[28,8,256]{2,1,0:T(8,128)S(1)}, f32[28,8,256]{2,1,0:T(8,128)S(1)}, u32[]{:S(2)}, u32[]{:S(2)}) collective-permute-start(f32[28,8,256]{2,1,0:T(8,128)S(1)} %collective-permute-done.4), channel_id=1, source_target_pairs={{0,6},{2,0},{4,2},{6,4},{1,7},{3,1},{5,3},{7,5},{8,14},{10,8},{12,... | collective-permute-start | bytes 688136 | tf_op jit(solution)/shard_map/cond/branch_0_fun/ppermute | solution.py:31
  44.9 1.5 collective-permute-done.2
  46.5 4.7 %collective-permute-start.7 = (f32[4,28,8,256]{3,2,1,0:T(8,128)S(1)}, f32[4,28,8,256]{3,2,1,0:T(8,128)S(1)}, u32[]{:S(2)}, u32[]{:S(2)}) collective-permute-start(f32[4,28,8,256]{3,2,1,0:T(8,128)S(1)} %pad_maximum_fusion.g0), channel_id=1, source_target_pairs={{0,1},{1,0},{2,3},{3,2},{4,5},{5,4},{6,7},{7,6},{8,9},{9,8},{10,11... | collective-permute-start | bytes 2752520 | tf_op jit(solution)/shard_map/cond/branch_0_fun/ppermute | solution.py:26
  51.4 2.6 %collective-permute-start.8 = (f32[4,28,8,256]{3,2,1,0:T(8,128)S(1)}, f32[4,28,8,256]{3,2,1,0:T(8,128)}, u32[]{:S(2)}, u32[]{:S(2)}) collective-permute-start(f32[4,28,8,256]{3,2,1,0:T(8,128)S(1)} %pad_maximum_fusion.1.g1), channel_id=1, source_target_pairs={{0,1},{1,0},{2,3},{3,2},{4,5},{5,4},{6,7},{7,6},{8,9},{9,8},{10,11... | collective-permute-start | bytes 2752520 | tf_op jit(solution)/shard_map/cond/branch_0_fun/ppermute | solution.py:26
  54.0 2.2 collective-permute-done.8.c1
  56.2 11.3 %branch_0_fun.6 = (f32[8,28,32,128]{3,2,1,0:T(8,128)S(1)}, bf16[28,128,256]{2,1,0:T(8,128)(2,1)S(1)}, bf16[28,128,256]{2,1,0:T(8,128)(2,1)S(1)}) custom-call(s32[362]{0:T(512)S(1)} %get-tuple-element.16.tab, f32[4,28,8,256]{3,2,1,0:T(8,128)S(1)} %pad_maximum_fusion.g0, f32[4,28,8,256]{3,2,1,0:T(8,128)S(1)} %pad_maximum_fusion.1.g1, ...), custom_call_target="tpu_custom_call" | custom-call | tf_op jit(solution)/shard_map/cond/branch_0_fun/pallas_call | solution.py:312
  67.5 1.7 copy-done.1
  70.4 3.5 %collective-permute-start.9 = (f32[14,32,128]{2,1,0:T(8,128)S(1)}, f32[14,32,128]{2,1,0:T(8,128)S(1)}, u32[]{:S(2)}, u32[]{:S(2)}) collective-permute-start(f32[14,32,128]{2,1,0:T(8,128)S(1)} %get-tuple-element.53), channel_id=1, source_target_pairs={{0,32},{32,64},{64,96},{96,128},{128,160},{160,192},{192,224},{224... | collective-permute-start | bytes 688136 | tf_op jit(solution)/shard_map/cond/branch_0_fun/ppermute | solution.py:31
  74.0 2.0 collective-permute-start.16
  76.0 6.0 %collective-permute-done.9 = f32[14,32,128]{2,1,0:T(8,128)S(1)} collective-permute-done((f32[14,32,128]{2,1,0:T(8,128)S(1)}, f32[14,32,128]{2,1,0:T(8,128)S(1)}, u32[]{:S(2)}, u32[]{:S(2)}) %collective-permute-start.9) | collective-permute-done | bytes 229408 | tf_op jit(solution)/shard_map/cond/branch_0_fun/ppermute | solution.py:31
  82.0 1.0 fusion.6
  83.1 2.7 %collective-permute-start.17 = (f32[2,7,32,128]{3,2,1,0:T(8,128)S(1)}, f32[2,7,32,128]{3,2,1,0:T(8,128)S(1)}, u32[]{:S(2)}, u32[]{:S(2)}) collective-permute-start(f32[2,7,32,128]{3,2,1,0:T(8,128)S(1)} %add.381), channel_id=1, source_target_pairs={{0,224},{32,0},{64,32},{96,64},{128,96},{160,128},{192,160},{224,1... | collective-permute-start | bytes 688136 | tf_op jit(solution)/shard_map/cond/branch_0_fun/ppermute | solution.py:31
  85.8 5.0 %collective-permute-done.10 = f32[14,32,128]{2,1,0:T(8,128)S(1)} collective-permute-done((f32[14,32,128]{2,1,0:T(8,128)S(1)}, f32[14,32,128]{2,1,0:T(8,128)S(1)}, u32[]{:S(2)}, u32[]{:S(2)}) %collective-permute-start.10) | collective-permute-done | bytes 229408 | tf_op jit(solution)/shard_map/cond/branch_0_fun/ppermute | solution.py:31
  90.8 1.0 fusion.5
  91.9 2.7 %collective-permute-start.18 = (f32[2,7,32,128]{3,2,1,0:T(8,128)S(1)}, f32[2,7,32,128]{3,2,1,0:T(8,128)S(1)}, u32[]{:S(2)}, u32[]{:S(2)}) collective-permute-start(f32[2,7,32,128]{3,2,1,0:T(8,128)S(1)} %add.385), channel_id=1, source_target_pairs={{0,224},{32,0},{64,32},{96,64},{128,96},{160,128},{192,160},{224,1... | collective-permute-start | bytes 688136 | tf_op jit(solution)/shard_map/cond/branch_0_fun/ppermute | solution.py:31
  94.7 4.1 %collective-permute-done.11 = f32[14,32,128]{2,1,0:T(8,128)S(1)} collective-permute-done((f32[14,32,128]{2,1,0:T(8,128)S(1)}, f32[14,32,128]{2,1,0:T(8,128)S(1)}, u32[]{:S(2)}, u32[]{:S(2)}) %collective-permute-start.11) | collective-permute-done | bytes 229408 | tf_op jit(solution)/shard_map/cond/branch_0_fun/ppermute | solution.py:31
  98.7 1.0 fusion.4
  99.9 2.7 %collective-permute-start.19 = (f32[2,7,32,128]{3,2,1,0:T(8,128)S(1)}, f32[2,7,32,128]{3,2,1,0:T(8,128)S(1)}, u32[]{:S(2)}, u32[]{:S(2)}) collective-permute-start(f32[2,7,32,128]{3,2,1,0:T(8,128)S(1)} %add.389), channel_id=1, source_target_pairs={{0,224},{32,0},{64,32},{96,64},{128,96},{160,128},{192,160},{224,1... | collective-permute-start | bytes 688136 | tf_op jit(solution)/shard_map/cond/branch_0_fun/ppermute | solution.py:31
  102.6 3.3 %collective-permute-done.12 = f32[14,32,128]{2,1,0:T(8,128)S(1)} collective-permute-done((f32[14,32,128]{2,1,0:T(8,128)S(1)}, f32[14,32,128]{2,1,0:T(8,128)S(1)}, u32[]{:S(2)}, u32[]{:S(2)}) %collective-permute-start.12) | collective-permute-done | bytes 229408 | tf_op jit(solution)/shard_map/cond/branch_0_fun/ppermute | solution.py:31
  105.9 1.0 fusion.3
  107.0 2.7 %collective-permute-start.20 = (f32[2,7,32,128]{3,2,1,0:T(8,128)S(1)}, f32[2,7,32,128]{3,2,1,0:T(8,128)S(1)}, u32[]{:S(2)}, u32[]{:S(2)}) collective-permute-start(f32[2,7,32,128]{3,2,1,0:T(8,128)S(1)} %add.393), channel_id=1, source_target_pairs={{0,224},{32,0},{64,32},{96,64},{128,96},{160,128},{192,160},{224,1... | collective-permute-start | bytes 688136 | tf_op jit(solution)/shard_map/cond/branch_0_fun/ppermute | solution.py:31
  109.7 3.3 %collective-permute-done.13 = f32[14,32,128]{2,1,0:T(8,128)S(1)} collective-permute-done((f32[14,32,128]{2,1,0:T(8,128)S(1)}, f32[14,32,128]{2,1,0:T(8,128)S(1)}, u32[]{:S(2)}, u32[]{:S(2)}) %collective-permute-start.13) | collective-permute-done | bytes 229408 | tf_op jit(solution)/shard_map/cond/branch_0_fun/ppermute | solution.py:31
  113.0 1.0 fusion.2
  114.1 2.7 %collective-permute-start.21 = (f32[2,7,32,128]{3,2,1,0:T(8,128)S(1)}, f32[2,7,32,128]{3,2,1,0:T(8,128)S(1)}, u32[]{:S(2)}, u32[]{:S(2)}) collective-permute-start(f32[2,7,32,128]{3,2,1,0:T(8,128)S(1)} %add.397), channel_id=1, source_target_pairs={{0,224},{32,0},{64,32},{96,64},{128,96},{160,128},{192,160},{224,1... | collective-permute-start | bytes 688136 | tf_op jit(solution)/shard_map/cond/branch_0_fun/ppermute | solution.py:31
  116.9 3.3 %collective-permute-done.14 = f32[14,32,128]{2,1,0:T(8,128)S(1)} collective-permute-done((f32[14,32,128]{2,1,0:T(8,128)S(1)}, f32[14,32,128]{2,1,0:T(8,128)S(1)}, u32[]{:S(2)}, u32[]{:S(2)}) %collective-permute-start.14) | collective-permute-done | bytes 229408 | tf_op jit(solution)/shard_map/cond/branch_0_fun/ppermute | solution.py:31
  120.1 1.0 fusion.1
  121.3 2.7 %collective-permute-start.22 = (f32[2,7,32,128]{3,2,1,0:T(8,128)S(1)}, f32[2,7,32,128]{3,2,1,0:T(8,128)S(1)}, u32[]{:S(2)}, u32[]{:S(2)}) collective-permute-start(f32[2,7,32,128]{3,2,1,0:T(8,128)S(1)} %add.401), channel_id=1, source_target_pairs={{0,224},{32,0},{64,32},{96,64},{128,96},{160,128},{192,160},{224,1... | collective-permute-start | bytes 688136 | tf_op jit(solution)/shard_map/cond/branch_0_fun/ppermute | solution.py:31
  124.0 3.7 %collective-permute-done.15 = f32[14,32,128]{2,1,0:T(8,128)S(1)} collective-permute-done((f32[14,32,128]{2,1,0:T(8,128)S(1)}, f32[14,32,128]{2,1,0:T(8,128)S(1)}, u32[]{:S(2)}, u32[]{:S(2)}) %collective-permute-start.15) | collective-permute-done | bytes 229408 | tf_op jit(solution)/shard_map/cond/branch_0_fun/ppermute | solution.py:31
  127.7 1.0 fusion
  128.8 3.3 %collective-permute-start.23 = (f32[28,16,128]{2,1,0:T(8,128)S(1)}, f32[28,16,128]{2,1,0:T(8,128)S(1)}, u32[]{:S(2)}, u32[]{:S(2)}) collective-permute-start(f32[28,16,128]{2,1,0:T(8,128)S(1)} %pad_maximum_fusion.2), channel_id=1, source_target_pairs={{0,0},{1,15},{2,14},{3,13},{4,12},{5,11},{6,10},{7,9},{8,8},{9,7},... | collective-permute-start | bytes 688136 | tf_op jit(solution)/shard_map/cond/branch_0_fun/ppermute | solution.py:349
  132.2 8.5 %collective-permute-start.24 = (f32[28,16,128]{2,1,0:T(8,128)S(1)}, f32[28,16,128]{2,1,0:T(8,128)S(1)}, u32[]{:S(2)}, u32[]{:S(2)}) collective-permute-start(f32[28,16,128]{2,1,0:T(8,128)S(1)} %pad_maximum_fusion.3), channel_id=1, source_target_pairs={{0,31},{1,30},{2,29},{3,28},{4,27},{5,26},{6,25},{7,24},{8,23},{9,... | collective-permute-start | bytes 688136 | tf_op jit(solution)/shard_map/cond/branch_0_fun/ppermute | solution.py:349
  140.7 8.5 %collective-permute-done.24 = f32[28,16,128]{2,1,0:T(8,128)S(1)} collective-permute-done((f32[28,16,128]{2,1,0:T(8,128)S(1)}, f32[28,16,128]{2,1,0:T(8,128)S(1)}, u32[]{:S(2)}, u32[]{:S(2)}) %collective-permute-start.24) | collective-permute-done | bytes 229408 | tf_op jit(solution)/shard_map/cond/branch_0_fun/ppermute | solution.py:349
  149.2 3.8 %collective-permute-start.25 = (f32[28,16,128]{2,1,0:T(8,128)S(1)}, f32[28,16,128]{2,1,0:T(8,128)S(1)}, u32[]{:S(2)}, u32[]{:S(2)}) collective-permute-start(f32[28,16,128]{2,1,0:T(8,128)S(1)} %add.407), channel_id=1, source_target_pairs={{0,0},{1,241},{2,226},{3,211},{4,196},{5,181},{6,166},{7,151},{8,1... | collective-permute-start | bytes 688136 | tf_op jit(solution)/shard_map/cond/branch_0_fun/ppermute | solution.py:350
  153.0 11.2 %collective-permute-done.25.x_ref = f32[28,16,128]{2,1,0:T(8,128)S(1)} collective-permute-done((f32[28,16,128]{2,1,0:T(8,128)S(1)}, f32[28,16,128]{2,1,0:T(8,128)S(1)}, u32[]{:S(2)}, u32[]{:S(2)}) %collective-permute-start.25) | collective-permute-done | bytes 229408 | tf_op jit(solution)/shard_map/cond/branch_0_fun/ppermute | solution.py:350
  164.2 3.0 %collective-permute-start.26 = (f32[28,16,128]{2,1,0:T(8,128)S(1)}, f32[28,16,128]{2,1,0:T(8,128)S(1)}, u32[]{:S(2)}, u32[]{:S(2)}) collective-permute-start(f32[28,16,128]{2,1,0:T(8,128)S(1)} %pad_maximum_fusion.3), channel_id=1, source_target_pairs={{0,16},{16,0},{1,17},{17,1},{2,18},{18,2},{3,19},{19,3},{4,20},{20... | collective-permute-start | bytes 688136 | tf_op jit(solution)/shard_map/cond/branch_0_fun/ppermute | solution.py:26
  167.3 1.9 branch_0_fun.8
  169.1 2.2 branch_0_fun.9
  172.4 0.7 copy-done.12
  173.1 5.6 %all-to-all-start.3 = ((f32[16,16,1280]{2,1,0:T(8,128)}), f32[16,16,1280]{2,1,0:T(8,128)S(1)}, u32[]{:S(2)}, u32[]{:S(2)}) async-start(f32[16,16,1280]{2,1,0:T(8,128)} %get-tuple-element.43), calls=%async_computation.3 | async-start | bytes 2621440 | tf_op jit(solution)/shard_map/all_to_all | solution.py:467
  178.7 1.4 collective-permute-start.31
  180.1 5.3 %collective-permute-start.32 = (f32[4,16,256]{2,1,0:T(8,128)S(1)}, f32[4,16,256]{2,1,0:T(8,128)S(1)}, u32[]{:S(2)}, u32[]{:S(2)}) collective-permute-start(f32[4,16,256]{2,1,0:T(8,128)S(1)} %get-tuple-element.44), channel_id=1, source_target_pairs={{0,46},{1,47},{2,32},{3,33},{4,34},{5,35},{6,36},{7,37},{8,38},{9,... | collective-permute-start | bytes 196616 | tf_op jit(solution)/shard_map/ppermute | solution.py:476
  185.4 1.3 collective-permute-start.33
  186.7 8.1 %collective-permute-done.31 = f32[4,16,256]{2,1,0:T(8,128)S(1)} collective-permute-done((f32[4,16,256]{2,1,0:T(8,128)S(1)}, f32[4,16,256]{2,1,0:T(8,128)S(1)}, u32[]{:S(2)}, u32[]{:S(2)}) %collective-permute-start.31) | collective-permute-done | bytes 65568 | tf_op jit(solution)/shard_map/ppermute | solution.py:476
  194.8 9.4 %collective-permute-start.34 = (f32[4,16,256]{2,1,0:T(8,128)S(1)}, f32[4,16,256]{2,1,0:T(8,128)S(1)}, u32[]{:S(2)}, u32[]{:S(2)}) collective-permute-start(f32[4,16,256]{2,1,0:T(8,128)S(1)} %add_add_fusion.1), channel_id=1, source_target_pairs={{0,76},{1,77},{2,78},{3,79},{4,64},{5,65},{6,66},{7,67},{8,68},{9,... | collective-permute-start | bytes 196616 | tf_op jit(solution)/shard_map/ppermute | solution.py:476
  204.2 1.9 collective-permute-start.35
  206.1 1.5 collective-permute-start.36
  207.6 4.6 %collective-permute-done.35 = f32[4,16,256]{2,1,0:T(8,128)S(1)} collective-permute-done((f32[4,16,256]{2,1,0:T(8,128)S(1)}, f32[4,16,256]{2,1,0:T(8,128)S(1)}, u32[]{:S(2)}, u32[]{:S(2)}) %collective-permute-start.35) | collective-permute-done | bytes 65568 | tf_op jit(solution)/shard_map/ppermute | solution.py:476
  212.2 1.7 collective-permute-done.36
  214.0 1.4 shard_map.87
  215.3 8.2 %all-to-all-start.4 = ((f32[16,16,256]{2,1,0:T(8,128)}), f32[16,16,256]{2,1,0:T(8,128)S(1)}, u32[]{:S(2)}, u32[]{:S(2)}) async-start(f32[16,16,256]{2,1,0:T(8,128)} %shard_map.87), calls=%async_computation.4 | async-start | bytes 524288 | tf_op jit(solution)/shard_map/all_to_all | solution.py:479
  223.5 2.0 shard_map.86
  225.5 5.1 %all-to-all-done.4.x_ref = f32[16,16,256]{2,1,0:T(8,128)S(1)} async-done(((f32[16,16,256]{2,1,0:T(8,128)}), f32[16,16,256]{2,1,0:T(8,128)S(1)}, u32[]{:S(2)}, u32[]{:S(2)}) %all-to-all-start.4) | async-done | bytes 262176 | tf_op jit(solution)/shard_map/all_to_all | solution.py:479
  230.7 1.3 shard_map.88
  (99 shorter events, 7.0 us)
Async XLA Ops:
  0.6 9.5 %copy-start.14 = (s32[4]{0:T(128)S(1)}, s32[4]{0:T(128)}, u32[]{:S(2)}) copy-start(s32[4]{0:T(128)} %param.12) | copy-start | bytes 52
  0.6 10.4 %copy-start.15 = (s32[4]{0:T(128)S(1)}, s32[4]{0:T(128)}, u32[]{:S(2)}) copy-start(s32[4]{0:T(128)} %param.13) | copy-start | bytes 52
  0.7 1.3 copy-start.8
  2.0 8.2 %copy-start.13 = (s32[4,96]{1,0:T(4,128)S(1)}, s32[4,96]{1,0:T(4,128)}, u32[]{:S(2)}) copy-start(s32[4,96]{1,0:T(4,128)} %param.11) | copy-start | bytes 4612
  3.3 25.5 %all-to-all-start.2 = ((f32[16,10,8,256]{3,2,1,0:T(8,128)}), f32[16,10,8,256]{3,2,1,0:T(8,128)S(1)}, u32[]{:S(2)}, u32[]{:S(2)}) async-start(f32[16,10,8,256]{3,2,1,0:T(8,128)} %shard_map.85), calls=%async_computation.2 | async-start | bytes 2621440 | tf_op jit(solution)/shard_map/all_to_all | solution.py:414
  29.5 6.5 %collective-permute-start = (f32[28,8,256]{2,1,0:T(8,128)S(1)}, f32[28,8,256]{2,1,0:T(8,128)S(1)}, u32[]{:S(2)}, u32[]{:S(2)}) collective-permute-start(f32[28,8,256]{2,1,0:T(8,128)S(1)} %branch_0_fun.5), channel_id=1, source_target_pairs={{0,8},{8,0},{1,9},{9,1},{2,10},{10,2},{3,11},{11,3},{4,12},{12,4},... | collective-permute-start | bytes 688136 | tf_op jit(solution)/shard_map/cond/branch_0_fun/ppermute | solution.py:26
  29.9 9.1 %collective-permute-start.1 = (f32[28,8,256]{2,1,0:T(8,128)S(1)}, f32[28,8,256]{2,1,0:T(8,128)S(1)}, u32[]{:S(2)}, u32[]{:S(2)}) collective-permute-start(f32[28,8,256]{2,1,0:T(8,128)S(1)} %branch_0_fun.5), channel_id=1, source_target_pairs={{0,2},{2,4},{4,6},{6,0},{1,3},{3,5},{5,7},{7,1},{8,10},{10,12},{12... | collective-permute-start | bytes 688136 | tf_op jit(solution)/shard_map/cond/branch_0_fun/ppermute | solution.py:31
  36.0 5.5 %collective-permute-start.4 = (f32[28,8,256]{2,1,0:T(8,128)S(1)}, f32[28,8,256]{2,1,0:T(8,128)S(1)}, u32[]{:S(2)}, u32[]{:S(2)}) collective-permute-start(f32[28,8,256]{2,1,0:T(8,128)S(1)} %collective-permute-done), channel_id=1, source_target_pairs={{0,6},{2,0},{4,2},{6,4},{1,7},{3,1},{5,3},{7,5},{8,14},{10,8},{12,... | collective-permute-start | bytes 688136 | tf_op jit(solution)/shard_map/cond/branch_0_fun/ppermute | solution.py:31
  37.4 9.0 %collective-permute-start.2 = (f32[28,8,256]{2,1,0:T(8,128)S(1)}, f32[28,8,256]{2,1,0:T(8,128)S(1)}, u32[]{:S(2)}, u32[]{:S(2)}) collective-permute-start(f32[28,8,256]{2,1,0:T(8,128)S(1)} %branch_0_fun.5), channel_id=1, source_target_pairs={{0,6},{2,0},{4,2},{6,4},{1,7},{3,1},{5,3},{7,5},{8,14},{10,8},{12,... | collective-permute-start | bytes 688136 | tf_op jit(solution)/shard_map/cond/branch_0_fun/ppermute | solution.py:31
  37.8 13.5 %collective-permute-start.3 = (f32[28,8,256]{2,1,0:T(8,128)S(1)}, f32[28,8,256]{2,1,0:T(8,128)S(1)}, u32[]{:S(2)}, u32[]{:S(2)}) collective-permute-start(f32[28,8,256]{2,1,0:T(8,128)S(1)} %collective-permute-done), channel_id=1, source_target_pairs={{0,2},{2,4},{4,6},{6,0},{1,3},{3,5},{5,7},{7,1},{8,10},{10,12},{12... | collective-permute-start | bytes 688136 | tf_op jit(solution)/shard_map/cond/branch_0_fun/ppermute | solution.py:31
  38.9 12.3 %collective-permute-start.5 = (f32[28,8,256]{2,1,0:T(8,128)S(1)}, f32[28,8,256]{2,1,0:T(8,128)S(1)}, u32[]{:S(2)}, u32[]{:S(2)}) collective-permute-start(f32[28,8,256]{2,1,0:T(8,128)S(1)} %collective-permute-done.1), channel_id=1, source_target_pairs={{0,2},{2,4},{4,6},{6,0},{1,3},{3,5},{5,7},{7,1},{8,10},{10,12},{12... | collective-permute-start | bytes 688136 | tf_op jit(solution)/shard_map/cond/branch_0_fun/ppermute | solution.py:31
  41.5 9.8 %collective-permute-start.6 = (f32[28,8,256]{2,1,0:T(8,128)S(1)}, f32[28,8,256]{2,1,0:T(8,128)S(1)}, u32[]{:S(2)}, u32[]{:S(2)}) collective-permute-start(f32[28,8,256]{2,1,0:T(8,128)S(1)} %collective-permute-done.4), channel_id=1, source_target_pairs={{0,6},{2,0},{4,2},{6,4},{1,7},{3,1},{5,3},{7,5},{8,14},{10,8},{12,... | collective-permute-start | bytes 688136 | tf_op jit(solution)/shard_map/cond/branch_0_fun/ppermute | solution.py:31
  46.5 7.5 %collective-permute-start.7 = (f32[4,28,8,256]{3,2,1,0:T(8,128)S(1)}, f32[4,28,8,256]{3,2,1,0:T(8,128)S(1)}, u32[]{:S(2)}, u32[]{:S(2)}) collective-permute-start(f32[4,28,8,256]{3,2,1,0:T(8,128)S(1)} %pad_maximum_fusion.g0), channel_id=1, source_target_pairs={{0,1},{1,0},{2,3},{3,2},{4,5},{5,4},{6,7},{7,6},{8,9},{9,8},{10,11... | collective-permute-start | bytes 2752520 | tf_op jit(solution)/shard_map/cond/branch_0_fun/ppermute | solution.py:26
  51.4 4.8 %collective-permute-start.8 = (f32[4,28,8,256]{3,2,1,0:T(8,128)S(1)}, f32[4,28,8,256]{3,2,1,0:T(8,128)}, u32[]{:S(2)}, u32[]{:S(2)}) collective-permute-start(f32[4,28,8,256]{3,2,1,0:T(8,128)S(1)} %pad_maximum_fusion.1.g1), channel_id=1, source_target_pairs={{0,1},{1,0},{2,3},{3,2},{4,5},{5,4},{6,7},{7,6},{8,9},{9,8},{10,11... | collective-permute-start | bytes 2752520 | tf_op jit(solution)/shard_map/cond/branch_0_fun/ppermute | solution.py:26
  67.5 1.8 copy-start.1
  67.5 2.4 %copy-start.4 = (bf16[28,128,256]{2,1,0:T(8,128)(2,1)}, bf16[28,128,256]{2,1,0:T(8,128)(2,1)S(1)}, u32[]{:S(2)}) copy-start(bf16[28,128,256]{2,1,0:T(8,128)(2,1)S(1)} %get-tuple-element.23.hi_ref) | copy-start | bytes 5505028 | tf_op jit(solution)/shard_map/cond
  67.5 2.9 %copy-start.6 = (bf16[28,128,256]{2,1,0:T(8,128)(2,1)}, bf16[28,128,256]{2,1,0:T(8,128)(2,1)S(1)}, u32[]{:S(2)}) copy-start(bf16[28,128,256]{2,1,0:T(8,128)(2,1)S(1)} %get-tuple-element.24.lo_ref) | copy-start | bytes 5505028 | tf_op jit(solution)/shard_map/cond
  70.4 11.5 %collective-permute-start.9 = (f32[14,32,128]{2,1,0:T(8,128)S(1)}, f32[14,32,128]{2,1,0:T(8,128)S(1)}, u32[]{:S(2)}, u32[]{:S(2)}) collective-permute-start(f32[14,32,128]{2,1,0:T(8,128)S(1)} %get-tuple-element.53), channel_id=1, source_target_pairs={{0,32},{32,64},{64,96},{96,128},{128,160},{160,192},{192,224},{224... | collective-permute-start | bytes 688136 | tf_op jit(solution)/shard_map/cond/branch_0_fun/ppermute | solution.py:31
  74.0 9.1 %collective-permute-start.16 = (f32[2,7,32,128]{3,2,1,0:T(8,128)S(1)}, f32[2,7,32,128]{3,2,1,0:T(8,128)S(1)}, u32[]{:S(2)}, u32[]{:S(2)}) collective-permute-start(f32[2,7,32,128]{3,2,1,0:T(8,128)S(1)} %bitcast.93), channel_id=1, source_target_pairs={{0,224},{32,0},{64,32},{96,64},{128,96},{160,128},{192,160},{224,1... | collective-permute-start | bytes 688136 | tf_op jit(solution)/shard_map/cond/branch_0_fun/ppermute | solution.py:31
  82.9 7.9 %collective-permute-start.10 = (f32[14,32,128]{2,1,0:T(8,128)S(1)}, f32[14,32,128]{2,1,0:T(8,128)S(1)}, u32[]{:S(2)}, u32[]{:S(2)}) collective-permute-start(f32[14,32,128]{2,1,0:T(8,128)S(1)} %fusion.6), channel_id=1, source_target_pairs={{0,32},{32,64},{64,96},{96,128},{128,160},{160,192},{192,224},{224... | collective-permute-start | bytes 688136 | tf_op jit(solution)/shard_map/cond/branch_0_fun/ppermute | solution.py:31
  83.1 8.8 %collective-permute-start.17 = (f32[2,7,32,128]{3,2,1,0:T(8,128)S(1)}, f32[2,7,32,128]{3,2,1,0:T(8,128)S(1)}, u32[]{:S(2)}, u32[]{:S(2)}) collective-permute-start(f32[2,7,32,128]{3,2,1,0:T(8,128)S(1)} %add.381), channel_id=1, source_target_pairs={{0,224},{32,0},{64,32},{96,64},{128,96},{160,128},{192,160},{224,1... | collective-permute-start | bytes 688136 | tf_op jit(solution)/shard_map/cond/branch_0_fun/ppermute | solution.py:31
  91.8 7.0 %collective-permute-start.11 = (f32[14,32,128]{2,1,0:T(8,128)S(1)}, f32[14,32,128]{2,1,0:T(8,128)S(1)}, u32[]{:S(2)}, u32[]{:S(2)}) collective-permute-start(f32[14,32,128]{2,1,0:T(8,128)S(1)} %fusion.5), channel_id=1, source_target_pairs={{0,32},{32,64},{64,96},{96,128},{128,160},{160,192},{192,224},{224... | collective-permute-start | bytes 688136 | tf_op jit(solution)/shard_map/cond/branch_0_fun/ppermute | solution.py:31
  91.9 7.9 %collective-permute-start.18 = (f32[2,7,32,128]{3,2,1,0:T(8,128)S(1)}, f32[2,7,32,128]{3,2,1,0:T(8,128)S(1)}, u32[]{:S(2)}, u32[]{:S(2)}) collective-permute-start(f32[2,7,32,128]{3,2,1,0:T(8,128)S(1)} %add.385), channel_id=1, source_target_pairs={{0,224},{32,0},{64,32},{96,64},{128,96},{160,128},{192,160},{224,1... | collective-permute-start | bytes 688136 | tf_op jit(solution)/shard_map/cond/branch_0_fun/ppermute | solution.py:31
  99.7 6.2 %collective-permute-start.12 = (f32[14,32,128]{2,1,0:T(8,128)S(1)}, f32[14,32,128]{2,1,0:T(8,128)S(1)}, u32[]{:S(2)}, u32[]{:S(2)}) collective-permute-start(f32[14,32,128]{2,1,0:T(8,128)S(1)} %fusion.4), channel_id=1, source_target_pairs={{0,32},{32,64},{64,96},{96,128},{128,160},{160,192},{192,224},{224... | collective-permute-start | bytes 688136 | tf_op jit(solution)/shard_map/cond/branch_0_fun/ppermute | solution.py:31
  99.9 7.1 %collective-permute-start.19 = (f32[2,7,32,128]{3,2,1,0:T(8,128)S(1)}, f32[2,7,32,128]{3,2,1,0:T(8,128)S(1)}, u32[]{:S(2)}, u32[]{:S(2)}) collective-permute-start(f32[2,7,32,128]{3,2,1,0:T(8,128)S(1)} %add.389), channel_id=1, source_target_pairs={{0,224},{32,0},{64,32},{96,64},{128,96},{160,128},{192,160},{224,1... | collective-permute-start | bytes 688136 | tf_op jit(solution)/shard_map/cond/branch_0_fun/ppermute | solution.py:31
  106.8 6.2 %collective-permute-start.13 = (f32[14,32,128]{2,1,0:T(8,128)S(1)}, f32[14,32,128]{2,1,0:T(8,128)S(1)}, u32[]{:S(2)}, u32[]{:S(2)}) collective-permute-start(f32[14,32,128]{2,1,0:T(8,128)S(1)} %fusion.3), channel_id=1, source_target_pairs={{0,32},{32,64},{64,96},{96,128},{128,160},{160,192},{192,224},{224... | collective-permute-start | bytes 688136 | tf_op jit(solution)/shard_map/cond/branch_0_fun/ppermute | solution.py:31
  107.0 7.1 %collective-permute-start.20 = (f32[2,7,32,128]{3,2,1,0:T(8,128)S(1)}, f32[2,7,32,128]{3,2,1,0:T(8,128)S(1)}, u32[]{:S(2)}, u32[]{:S(2)}) collective-permute-start(f32[2,7,32,128]{3,2,1,0:T(8,128)S(1)} %add.393), channel_id=1, source_target_pairs={{0,224},{32,0},{64,32},{96,64},{128,96},{160,128},{192,160},{224,1... | collective-permute-start | bytes 688136 | tf_op jit(solution)/shard_map/cond/branch_0_fun/ppermute | solution.py:31
  114.0 6.2 %collective-permute-start.14 = (f32[14,32,128]{2,1,0:T(8,128)S(1)}, f32[14,32,128]{2,1,0:T(8,128)S(1)}, u32[]{:S(2)}, u32[]{:S(2)}) collective-permute-start(f32[14,32,128]{2,1,0:T(8,128)S(1)} %fusion.2), channel_id=1, source_target_pairs={{0,32},{32,64},{64,96},{96,128},{128,160},{160,192},{192,224},{224... | collective-permute-start | bytes 688136 | tf_op jit(solution)/shard_map/cond/branch_0_fun/ppermute | solution.py:31
  114.1 55.0 %copy-start.5 = (bf16[28,128,256]{2,1,0:T(8,128)(2,1)S(1)}, bf16[28,128,256]{2,1,0:T(8,128)(2,1)}, u32[]{:S(2)}) copy-start(bf16[28,128,256]{2,1,0:T(8,128)(2,1)} %copy-done.4) | copy-start | bytes 5505028 | tf_op jit(solution)/shard_map/cond
  114.1 7.1 %collective-permute-start.21 = (f32[2,7,32,128]{3,2,1,0:T(8,128)S(1)}, f32[2,7,32,128]{3,2,1,0:T(8,128)S(1)}, u32[]{:S(2)}, u32[]{:S(2)}) collective-permute-start(f32[2,7,32,128]{3,2,1,0:T(8,128)S(1)} %add.397), channel_id=1, source_target_pairs={{0,224},{32,0},{64,32},{96,64},{128,96},{160,128},{192,160},{224,1... | collective-permute-start | bytes 688136 | tf_op jit(solution)/shard_map/cond/branch_0_fun/ppermute | solution.py:31
  121.1 6.6 %collective-permute-start.15 = (f32[14,32,128]{2,1,0:T(8,128)S(1)}, f32[14,32,128]{2,1,0:T(8,128)S(1)}, u32[]{:S(2)}, u32[]{:S(2)}) collective-permute-start(f32[14,32,128]{2,1,0:T(8,128)S(1)} %fusion.1), channel_id=1, source_target_pairs={{0,32},{32,64},{64,96},{96,128},{128,160},{160,192},{192,224},{224... | collective-permute-start | bytes 688136 | tf_op jit(solution)/shard_map/cond/branch_0_fun/ppermute | solution.py:31
  121.2 47.9 %copy-start.7 = (bf16[28,128,256]{2,1,0:T(8,128)(2,1)S(1)}, bf16[28,128,256]{2,1,0:T(8,128)(2,1)}, u32[]{:S(2)}) copy-start(bf16[28,128,256]{2,1,0:T(8,128)(2,1)} %copy-done.6) | copy-start | bytes 5505028 | tf_op jit(solution)/shard_map/cond
  121.3 7.4 %collective-permute-start.22 = (f32[2,7,32,128]{3,2,1,0:T(8,128)S(1)}, f32[2,7,32,128]{3,2,1,0:T(8,128)S(1)}, u32[]{:S(2)}, u32[]{:S(2)}) collective-permute-start(f32[2,7,32,128]{3,2,1,0:T(8,128)S(1)} %add.401), channel_id=1, source_target_pairs={{0,224},{32,0},{64,32},{96,64},{128,96},{160,128},{192,160},{224,1... | collective-permute-start | bytes 688136 | tf_op jit(solution)/shard_map/cond/branch_0_fun/ppermute | solution.py:31
  128.8 11.9 %collective-permute-start.23 = (f32[28,16,128]{2,1,0:T(8,128)S(1)}, f32[28,16,128]{2,1,0:T(8,128)S(1)}, u32[]{:S(2)}, u32[]{:S(2)}) collective-permute-start(f32[28,16,128]{2,1,0:T(8,128)S(1)} %pad_maximum_fusion.2), channel_id=1, source_target_pairs={{0,0},{1,15},{2,14},{3,13},{4,12},{5,11},{6,10},{7,9},{8,8},{9,7},... | collective-permute-start | bytes 688136 | tf_op jit(solution)/shard_map/cond/branch_0_fun/ppermute | solution.py:349
  132.2 17.0 %collective-permute-start.24 = (f32[28,16,128]{2,1,0:T(8,128)S(1)}, f32[28,16,128]{2,1,0:T(8,128)S(1)}, u32[]{:S(2)}, u32[]{:S(2)}) collective-permute-start(f32[28,16,128]{2,1,0:T(8,128)S(1)} %pad_maximum_fusion.3), channel_id=1, source_target_pairs={{0,31},{1,30},{2,29},{3,28},{4,27},{5,26},{6,25},{7,24},{8,23},{9,... | collective-permute-start | bytes 688136 | tf_op jit(solution)/shard_map/cond/branch_0_fun/ppermute | solution.py:349
  149.2 15.0 %collective-permute-start.25 = (f32[28,16,128]{2,1,0:T(8,128)S(1)}, f32[28,16,128]{2,1,0:T(8,128)S(1)}, u32[]{:S(2)}, u32[]{:S(2)}) collective-permute-start(f32[28,16,128]{2,1,0:T(8,128)S(1)} %add.407), channel_id=1, source_target_pairs={{0,0},{1,241},{2,226},{3,211},{4,196},{5,181},{6,166},{7,151},{8,1... | collective-permute-start | bytes 688136 | tf_op jit(solution)/shard_map/cond/branch_0_fun/ppermute | solution.py:350
  164.2 7.1 %collective-permute-start.26 = (f32[28,16,128]{2,1,0:T(8,128)S(1)}, f32[28,16,128]{2,1,0:T(8,128)S(1)}, u32[]{:S(2)}, u32[]{:S(2)}) collective-permute-start(f32[28,16,128]{2,1,0:T(8,128)S(1)} %pad_maximum_fusion.3), channel_id=1, source_target_pairs={{0,16},{16,0},{1,17},{17,1},{2,18},{18,2},{3,19},{19,3},{4,20},{20... | collective-permute-start | bytes 688136 | tf_op jit(solution)/shard_map/cond/branch_0_fun/ppermute | solution.py:26
  172.4 0.7 copy-start.12
  173.1 57.6 %copy-start.9 = (f32[1,256,256]{2,1,0:T(8,128)S(1)}, f32[1,256,256]{2,1,0:T(8,128)}, u32[]{:S(2)}) copy-start(f32[1,256,256]{2,1,0:T(8,128)} %param.10) | copy-start | bytes 786436
  173.1 40.9 %all-to-all-start.3 = ((f32[16,16,1280]{2,1,0:T(8,128)}), f32[16,16,1280]{2,1,0:T(8,128)S(1)}, u32[]{:S(2)}, u32[]{:S(2)}) async-start(f32[16,16,1280]{2,1,0:T(8,128)} %get-tuple-element.43), calls=%async_computation.3 | async-start | bytes 2621440 | tf_op jit(solution)/shard_map/all_to_all | solution.py:467
  178.7 16.1 %collective-permute-start.31 = (f32[4,16,256]{2,1,0:T(8,128)S(1)}, f32[4,16,256]{2,1,0:T(8,128)S(1)}, u32[]{:S(2)}, u32[]{:S(2)}) collective-permute-start(f32[4,16,256]{2,1,0:T(8,128)S(1)} %get-tuple-element.44), channel_id=1, source_target_pairs={{0,31},{1,16},{2,17},{3,18},{4,19},{5,20},{6,21},{7,22},{8,23},{9,... | collective-permute-start | bytes 196616 | tf_op jit(solution)/shard_map/ppermute | solution.py:476
  180.1 14.7 %collective-permute-start.32 = (f32[4,16,256]{2,1,0:T(8,128)S(1)}, f32[4,16,256]{2,1,0:T(8,128)S(1)}, u32[]{:S(2)}, u32[]{:S(2)}) collective-permute-start(f32[4,16,256]{2,1,0:T(8,128)S(1)} %get-tuple-element.44), channel_id=1, source_target_pairs={{0,46},{1,47},{2,32},{3,33},{4,34},{5,35},{6,36},{7,37},{8,38},{9,... | collective-permute-start | bytes 196616 | tf_op jit(solution)/shard_map/ppermute | solution.py:476
  185.4 9.4 %collective-permute-start.33 = (f32[4,16,256]{2,1,0:T(8,128)S(1)}, f32[4,16,256]{2,1,0:T(8,128)S(1)}, u32[]{:S(2)}, u32[]{:S(2)}) collective-permute-start(f32[4,16,256]{2,1,0:T(8,128)S(1)} %get-tuple-element.44), channel_id=1, source_target_pairs={{0,61},{1,62},{2,63},{3,48},{4,49},{5,50},{6,51},{7,52},{8,53},{9,... | collective-permute-start | bytes 196616 | tf_op jit(solution)/shard_map/ppermute | solution.py:476
  194.8 12.8 %collective-permute-start.34 = (f32[4,16,256]{2,1,0:T(8,128)S(1)}, f32[4,16,256]{2,1,0:T(8,128)S(1)}, u32[]{:S(2)}, u32[]{:S(2)}) collective-permute-start(f32[4,16,256]{2,1,0:T(8,128)S(1)} %add_add_fusion.1), channel_id=1, source_target_pairs={{0,76},{1,77},{2,78},{3,79},{4,64},{5,65},{6,66},{7,67},{8,68},{9,... | collective-permute-start | bytes 196616 | tf_op jit(solution)/shard_map/ppermute | solution.py:476
  204.2 8.0 %collective-permute-start.35 = (f32[4,16,256]{2,1,0:T(8,128)S(1)}, f32[4,16,256]{2,1,0:T(8,128)S(1)}, u32[]{:S(2)}, u32[]{:S(2)}) collective-permute-start(f32[4,16,256]{2,1,0:T(8,128)S(1)} %add_add_fusion.1), channel_id=1, source_target_pairs={{0,136},{1,137},{2,138},{3,139},{4,140},{5,141},{6,142},{7,143},{8... | collective-permute-start | bytes 196616 | tf_op jit(solution)/shard_map/ppermute | solution.py:476
  206.1 7.8 %collective-permute-start.36 = (f32[4,16,256]{2,1,0:T(8,128)S(1)}, f32[4,16,256]{2,1,0:T(8,128)S(1)}, u32[]{:S(2)}, u32[]{:S(2)}) collective-permute-start(f32[4,16,256]{2,1,0:T(8,128)S(1)} %add_add_fusion.1), channel_id=1, source_target_pairs={{0,196},{1,197},{2,198},{3,199},{4,200},{5,201},{6,202},{7,203},{8... | collective-permute-start | bytes 196616 | tf_op jit(solution)/shard_map/ppermute | solution.py:476
  215.3 15.4 %all-to-all-start.4 = ((f32[16,16,256]{2,1,0:T(8,128)}), f32[16,16,256]{2,1,0:T(8,128)S(1)}, u32[]{:S(2)}, u32[]{:S(2)}) async-start(f32[16,16,256]{2,1,0:T(8,128)} %shard_map.87), calls=%async_computation.4 | async-start | bytes 524288 | tf_op jit(solution)/shard_map/all_to_all | solution.py:479

commit v4 on v2

--- a/solution.py
+++ b/solution.py
@@ -12,7 +12,7 @@
 SUB = 8
 ROW = ("row_0", "row_1")
 COL = ("col_y", "col_x", "core")
-CAPS = (28,)
+CAPS = (30,)
 
 ROW_BLOCK, ROW_START, COL_BLOCK, COL_START = 0, 64, 72, 136
 PIECE, ROW_SLOT, COL_SLOT, SOURCE, OWNER, PRESENT, AT_ROW = 144, 160, 224, 288, 352, 360, 361
@@ -315,7 +315,7 @@
     )(table, g0, g1, c0, c1, a_hi, a_lo)
     z = lax.axis_index("row_0")
     if cap < sib * blocks:
-        strands = [(0, cap // 2, 1, 1), (cap // 2, cap, 2, -1)]
+        strands = [(0, cap // 2, 1, 1), (cap // 2, cap, 3, -1)]
         near = [ring_term(u, z - way, first, last, lead) for first, last, lead, way in strands]
         for step in range(1, near_chunks):
             near = [

time: 238 us -> 241 us (1.013)
  starting transfers between devices: 96.4 us -> 90.4 us
  Pallas kernels: 23.5 us -> 29.3 us
    pallas_call x1, Pallas kernels: 12.7 us -> 18.3 us  [listed_products(): pl.pallas_call(functools.partial(product_kernel, cap, sib), out_shape=(ja...]
    ppermute x1, starting transfers between devices: 13.1 us -> 8.37 us  [listed_products(): lax.ppermute(sent, ROW + COL, over)]
    ppermute x1, starting transfers between devices: 6.53 us -> 1.92 us  [listed_products(): lax.ppermute(kept, ROW + COL, across) + lax.ppermute(sent, ROW + COL, over)]
    all_to_all x1, starting transfers between devices: 6.89 us -> 11.2 us  [per_device(): parts = lax.all_to_all(place(inner), COL, 0, 0, tiled=True)]
    ppermute x6, starting transfers between devices: 19.6 us -> 15.9 us  [per_device(): others.append(lax.ppermute(inner, ROW + COL, pairs))]
    ppermute x4, starting transfers between devices: 7.79 us -> 10.5 us  [swapped(): return lax.ppermute(x, axis, [(i, i ^ bit) for i in range(length)])]
  transfers between devices with their start and end apart: 36 -> 36, of which waited for: 21 -> 19; matrix products, arithmetic and copies ran while one was open for 7% -> 7% of each run, Pallas kernels for 3% -> 3%
where the time goes in v4:
time: 241 us; the launch traced here: 240 us
  waiting for transfers between devices  93.6 us (39%)
  starting transfers between devices  90.4 us (38%)
  Pallas kernels  29.3 us (12%)
  other arithmetic  16.5 us (7%)
  local copies, waits for them, and re-layouts  6.88 us (3%)
    ppermute x20, waiting for transfers between devices, turned(): lax.ppermute(x, axis, [(i, (i + shift) % length) for i in range(length)])  34.4 us
    ppermute x20, starting transfers between devices, turned(): lax.ppermute(x, axis, [(i, (i + shift) % length) for i in range(length)])  26 us
    pallas_call x1, Pallas kernels, listed_products(): pl.pallas_call(functools.partial(product_kernel, cap, sib), out_shape=(ja...  18.3 us
    ppermute x6, starting transfers between devices, per_device(): others.append(lax.ppermute(inner, ROW + COL, pairs))  15.9 us
    ppermute x6, waiting for transfers between devices, per_device(): others.append(lax.ppermute(inner, ROW + COL, pairs))  15.2 us
    ppermute x1, waiting for transfers between devices, listed_products(): moved = lax.ppermute(midway, ROW + COL, along)  12.1 us
    all_to_all x1, starting transfers between devices, per_device(): parts = lax.all_to_all(place(inner), COL, 0, 0, tiled=True)  11.2 us
    ppermute x1, waiting for transfers between devices, listed_products(): lax.ppermute(sent, ROW + COL, over)  10.6 us
  transfers between devices with their start and end apart: 36, of which 19 were waited for; matrix products, arithmetic and copies ran while one was open for 7% of the time, Pallas kernels for 3%

profile of v4, /device:TPU:1, one launch (start us, length us, event | category | flops | bytes accessed | tf_op | source)
XLA Modules:
  0.0 239.6 jit_solution(1888490316943412520)
XLA Ops:
  0.7 2.5 %copy.12 = f32[16,10,8,256]{3,2,1,0:T(8,128)} copy(f32[16,10,8,256]{3,2,0,1:T(8,128)} %bitcast.77) | data formatting | bytes 2621440 | tf_op jit(solution)/shard_map/transpose | solution.py:395
  3.2 6.8 %all-to-all-start.2 = ((f32[16,10,8,256]{3,2,1,0:T(8,128)}), f32[16,10,8,256]{3,2,1,0:T(8,128)S(1)}, u32[]{:S(2)}, u32[]{:S(2)}) async-start(f32[16,10,8,256]{3,2,1,0:T(8,128)} %copy.12), calls=%async_computation.2 | async-start | bytes 2621440 | tf_op jit(solution)/shard_map/all_to_all | solution.py:396
  11.0 0.6 compare_reduce_fusion
  13.1 0.6 reduce_max.9
  14.5 6.6 %fusion.8 = (bf16[1280,1280]{1,0:T(8,128)(2,1)}, bf16[1280,1280]{1,0:T(8,128)(2,1)}) fusion(f32[1280,1280]{1,0:T(8,128)} %param.8), kind=kLoop, calls=%fused_computation.36 | loop fusion | flops 6553600 | bytes 13107200 | tf_op jit(solution)/shard_map/convert_element_type | solution.py:399
  21.1 7.6 %all-to-all-done.2 = f32[16,10,8,256]{3,2,1,0:T(8,128)S(1)} async-done(((f32[16,10,8,256]{3,2,1,0:T(8,128)}), f32[16,10,8,256]{3,2,1,0:T(8,128)S(1)}, u32[]{:S(2)}, u32[]{:S(2)}) %all-to-all-start.2) | async-done | bytes 1310752 | tf_op jit(solution)/shard_map/all_to_all | solution.py:396
  28.7 151.1 %conditional.1 = (f32[4,16,1280]{2,1,0:T(8,128)S(1)}, f32[16,16,1280]{2,1,0:T(8,128)}, f32[4,16,256]{2,1,0:T(8,128)S(1)}) conditional(s32[]{:T(128)} %clamp.3, (f32[16,10,8,256]{3,2,1,0:T(8,128)S(1)}, s32[362]{0:T(512)S(1)}, bf16[1280,1280]{1,0:T(8,128)(2,1)}, bf16[1280,1280]{1,0:T(8,128)(2,1)}) %tuple.19, (f32[16,10,8,256]{3,2,1,0:T(8,128)S(1)}, ...), branch_computations={%region_12.13_spmd, %region_13.15_spmd} | conditional | flops 127139856 | bytes 134283808 | solution.py:434
  28.7 0.7 branch_0_fun.5
  30.0 6.3 %collective-permute-done = f32[30,8,256]{2,1,0:T(8,128)S(1)} collective-permute-done((f32[30,8,256]{2,1,0:T(8,128)S(1)}, f32[30,8,256]{2,1,0:T(8,128)S(1)}, u32[]{:S(2)}, u32[]{:S(2)}) %collective-permute-start) | collective-permute-done | bytes 245792 | tf_op jit(solution)/shard_map/cond/branch_0_fun/ppermute | solution.py:26
  36.3 1.4 collective-permute-start.4
  38.1 1.1 collective-permute-start.3
  39.2 2.9 %collective-permute-done.4 = f32[30,8,256]{2,1,0:T(8,128)S(1)} collective-permute-done((f32[30,8,256]{2,1,0:T(8,128)S(1)}, f32[30,8,256]{2,1,0:T(8,128)S(1)}, u32[]{:S(2)}, u32[]{:S(2)}) %collective-permute-start.4) | collective-permute-done | bytes 245792 | tf_op jit(solution)/shard_map/cond/branch_0_fun/ppermute | solution.py:31
  42.1 3.4 %collective-permute-start.6 = (f32[30,8,256]{2,1,0:T(8,128)S(1)}, f32[30,8,256]{2,1,0:T(8,128)S(1)}, u32[]{:S(2)}, u32[]{:S(2)}) collective-permute-start(f32[30,8,256]{2,1,0:T(8,128)S(1)} %collective-permute-done.4), channel_id=1, source_target_pairs={{0,6},{2,0},{4,2},{6,4},{1,7},{3,1},{5,3},{7,5},{8,14},{10,8},{12,... | collective-permute-start | bytes 737288 | tf_op jit(solution)/shard_map/cond/branch_0_fun/ppermute | solution.py:31
  45.6 1.9 collective-permute-done.2
  47.5 4.7 %collective-permute-start.7 = (f32[4,30,8,256]{3,2,1,0:T(8,128)S(1)}, f32[4,30,8,256]{3,2,1,0:T(8,128)S(1)}, u32[]{:S(2)}, u32[]{:S(2)}) collective-permute-start(f32[4,30,8,256]{3,2,1,0:T(8,128)S(1)} %pad_maximum_fusion.g0), channel_id=1, source_target_pairs={{0,1},{1,0},{2,3},{3,2},{4,5},{5,4},{6,7},{7,6},{8,9},{9,8},{10,11... | collective-permute-start | bytes 2949128 | tf_op jit(solution)/shard_map/cond/branch_0_fun/ppermute | solution.py:26
  52.8 2.6 %collective-permute-start.8 = (f32[4,30,8,256]{3,2,1,0:T(8,128)S(1)}, f32[4,30,8,256]{3,2,1,0:T(8,128)}, u32[]{:S(2)}, u32[]{:S(2)}) collective-permute-start(f32[4,30,8,256]{3,2,1,0:T(8,128)S(1)} %pad_maximum_fusion.1.g1), channel_id=1, source_target_pairs={{0,1},{1,0},{2,3},{3,2},{4,5},{5,4},{6,7},{7,6},{8,9},{9,8},{10,11... | collective-permute-start | bytes 2949128 | tf_op jit(solution)/shard_map/cond/branch_0_fun/ppermute | solution.py:26
  55.4 2.3 collective-permute-done.8.c1
  57.7 18.3 %branch_0_fun.6 = (f32[8,30,32,128]{3,2,1,0:T(8,128)S(1)}, bf16[30,128,256]{2,1,0:T(8,128)(2,1)S(1)}, bf16[30,128,256]{2,1,0:T(8,128)(2,1)S(1)}) custom-call(s32[362]{0:T(512)S(1)} %get-tuple-element.16.tab, f32[4,30,8,256]{3,2,1,0:T(8,128)S(1)} %pad_maximum_fusion.g0, f32[4,30,8,256]{3,2,1,0:T(8,128)S(1)} %pad_maximum_fusion.1.g1, ...), custom_call_target="tpu_custom_call" | custom-call | tf_op jit(solution)/shard_map/cond/branch_0_fun/pallas_call | solution.py:300
  76.1 1.8 copy-done.1
  79.1 2.7 %collective-permute-start.16 = (f32[3,5,32,128]{3,2,1,0:T(8,128)S(1)}, f32[3,5,32,128]{3,2,1,0:T(8,128)S(1)}, u32[]{:S(2)}, u32[]{:S(2)}) collective-permute-start(f32[3,5,32,128]{3,2,1,0:T(8,128)S(1)} %bitcast.88), channel_id=1, source_target_pairs={{0,224},{32,0},{64,32},{96,64},{128,96},{160,128},{192,160},{224,1... | collective-permute-start | bytes 737288 | tf_op jit(solution)/shard_map/cond/branch_0_fun/ppermute | solution.py:31
  81.8 5.6 %collective-permute-done.9 = f32[15,32,128]{2,1,0:T(8,128)S(1)} collective-permute-done((f32[15,32,128]{2,1,0:T(8,128)S(1)}, f32[15,32,128]{2,1,0:T(8,128)S(1)}, u32[]{:S(2)}, u32[]{:S(2)}) %collective-permute-start.9) | collective-permute-done | bytes 245792 | tf_op jit(solution)/shard_map/cond/branch_0_fun/ppermute | solution.py:31
  87.4 1.0 fusion.6
  88.6 2.7 %collective-permute-start.17 = (f32[3,5,32,128]{3,2,1,0:T(8,128)S(1)}, f32[3,5,32,128]{3,2,1,0:T(8,128)S(1)}, u32[]{:S(2)}, u32[]{:S(2)}) collective-permute-start(f32[3,5,32,128]{3,2,1,0:T(8,128)S(1)} %add.381), channel_id=1, source_target_pairs={{0,224},{32,0},{64,32},{96,64},{128,96},{160,128},{192,160},{224,1... | collective-permute-start | bytes 737288 | tf_op jit(solution)/shard_map/cond/branch_0_fun/ppermute | solution.py:31
  91.3 4.6 %collective-permute-done.10 = f32[15,32,128]{2,1,0:T(8,128)S(1)} collective-permute-done((f32[15,32,128]{2,1,0:T(8,128)S(1)}, f32[15,32,128]{2,1,0:T(8,128)S(1)}, u32[]{:S(2)}, u32[]{:S(2)}) %collective-permute-start.10) | collective-permute-done | bytes 245792 | tf_op jit(solution)/shard_map/cond/branch_0_fun/ppermute | solution.py:31
  95.9 1.0 fusion.5
  97.0 2.7 %collective-permute-start.18 = (f32[3,5,32,128]{3,2,1,0:T(8,128)S(1)}, f32[3,5,32,128]{3,2,1,0:T(8,128)S(1)}, u32[]{:S(2)}, u32[]{:S(2)}) collective-permute-start(f32[3,5,32,128]{3,2,1,0:T(8,128)S(1)} %add.385), channel_id=1, source_target_pairs={{0,224},{32,0},{64,32},{96,64},{128,96},{160,128},{192,160},{224,1... | collective-permute-start | bytes 737288 | tf_op jit(solution)/shard_map/cond/branch_0_fun/ppermute | solution.py:31
  99.7 3.5 %collective-permute-done.11 = f32[15,32,128]{2,1,0:T(8,128)S(1)} collective-permute-done((f32[15,32,128]{2,1,0:T(8,128)S(1)}, f32[15,32,128]{2,1,0:T(8,128)S(1)}, u32[]{:S(2)}, u32[]{:S(2)}) %collective-permute-start.11) | collective-permute-done | bytes 245792 | tf_op jit(solution)/shard_map/cond/branch_0_fun/ppermute | solution.py:31
  103.2 1.0 fusion.4
  104.3 2.7 %collective-permute-start.19 = (f32[3,5,32,128]{3,2,1,0:T(8,128)S(1)}, f32[3,5,32,128]{3,2,1,0:T(8,128)S(1)}, u32[]{:S(2)}, u32[]{:S(2)}) collective-permute-start(f32[3,5,32,128]{3,2,1,0:T(8,128)S(1)} %add.389), channel_id=1, source_target_pairs={{0,224},{32,0},{64,32},{96,64},{128,96},{160,128},{192,160},{224,1... | collective-permute-start | bytes 737288 | tf_op jit(solution)/shard_map/cond/branch_0_fun/ppermute | solution.py:31
  107.0 3.5 %collective-permute-done.12 = f32[15,32,128]{2,1,0:T(8,128)S(1)} collective-permute-done((f32[15,32,128]{2,1,0:T(8,128)S(1)}, f32[15,32,128]{2,1,0:T(8,128)S(1)}, u32[]{:S(2)}, u32[]{:S(2)}) %collective-permute-start.12) | collective-permute-done | bytes 245792 | tf_op jit(solution)/shard_map/cond/branch_0_fun/ppermute | solution.py:31
  110.5 1.0 fusion.3
  111.6 2.7 %collective-permute-start.20 = (f32[3,5,32,128]{3,2,1,0:T(8,128)S(1)}, f32[3,5,32,128]{3,2,1,0:T(8,128)S(1)}, u32[]{:S(2)}, u32[]{:S(2)}) collective-permute-start(f32[3,5,32,128]{3,2,1,0:T(8,128)S(1)} %add.393), channel_id=1, source_target_pairs={{0,224},{32,0},{64,32},{96,64},{128,96},{160,128},{192,160},{224,1... | collective-permute-start | bytes 737288 | tf_op jit(solution)/shard_map/cond/branch_0_fun/ppermute | solution.py:31
  114.3 3.5 %collective-permute-done.13 = f32[15,32,128]{2,1,0:T(8,128)S(1)} collective-permute-done((f32[15,32,128]{2,1,0:T(8,128)S(1)}, f32[15,32,128]{2,1,0:T(8,128)S(1)}, u32[]{:S(2)}, u32[]{:S(2)}) %collective-permute-start.13) | collective-permute-done | bytes 245792 | tf_op jit(solution)/shard_map/cond/branch_0_fun/ppermute | solution.py:31
  117.8 1.0 fusion.2
  118.9 2.7 %collective-permute-start.21 = (f32[3,5,32,128]{3,2,1,0:T(8,128)S(1)}, f32[3,5,32,128]{3,2,1,0:T(8,128)S(1)}, u32[]{:S(2)}, u32[]{:S(2)}) collective-permute-start(f32[3,5,32,128]{3,2,1,0:T(8,128)S(1)} %add.397), channel_id=1, source_target_pairs={{0,224},{32,0},{64,32},{96,64},{128,96},{160,128},{192,160},{224,1... | collective-permute-start | bytes 737288 | tf_op jit(solution)/shard_map/cond/branch_0_fun/ppermute | solution.py:31
  121.7 3.7 %collective-permute-done.14 = f32[15,32,128]{2,1,0:T(8,128)S(1)} collective-permute-done((f32[15,32,128]{2,1,0:T(8,128)S(1)}, f32[15,32,128]{2,1,0:T(8,128)S(1)}, u32[]{:S(2)}, u32[]{:S(2)}) %collective-permute-start.14) | collective-permute-done | bytes 245792 | tf_op jit(solution)/shard_map/cond/branch_0_fun/ppermute | solution.py:31
  125.4 1.0 fusion.1
  126.6 2.7 %collective-permute-start.22 = (f32[3,5,32,128]{3,2,1,0:T(8,128)S(1)}, f32[3,5,32,128]{3,2,1,0:T(8,128)S(1)}, u32[]{:S(2)}, u32[]{:S(2)}) collective-permute-start(f32[3,5,32,128]{3,2,1,0:T(8,128)S(1)} %add.401), channel_id=1, source_target_pairs={{0,224},{32,0},{64,32},{96,64},{128,96},{160,128},{192,160},{224,1... | collective-permute-start | bytes 737288 | tf_op jit(solution)/shard_map/cond/branch_0_fun/ppermute | solution.py:31
  129.3 4.8 %collective-permute-done.15 = f32[15,32,128]{2,1,0:T(8,128)S(1)} collective-permute-done((f32[15,32,128]{2,1,0:T(8,128)S(1)}, f32[15,32,128]{2,1,0:T(8,128)S(1)}, u32[]{:S(2)}, u32[]{:S(2)}) %collective-permute-start.15) | collective-permute-done | bytes 245792 | tf_op jit(solution)/shard_map/cond/branch_0_fun/ppermute | solution.py:31
  134.1 1.0 fusion
  135.2 1.9 collective-permute-start.23
  137.2 8.4 %collective-permute-start.24 = (f32[30,16,128]{2,1,0:T(8,128)S(1)}, f32[30,16,128]{2,1,0:T(8,128)S(1)}, u32[]{:S(2)}, u32[]{:S(2)}) collective-permute-start(f32[30,16,128]{2,1,0:T(8,128)S(1)} %pad_maximum_fusion.3), channel_id=1, source_target_pairs={{0,31},{1,30},{2,29},{3,28},{4,27},{5,26},{6,25},{7,24},{8,23},{9,... | collective-permute-start | bytes 737288 | tf_op jit(solution)/shard_map/cond/branch_0_fun/ppermute | solution.py:337
  145.5 10.6 %collective-permute-done.24 = f32[30,16,128]{2,1,0:T(8,128)S(1)} collective-permute-done((f32[30,16,128]{2,1,0:T(8,128)S(1)}, f32[30,16,128]{2,1,0:T(8,128)S(1)}, u32[]{:S(2)}, u32[]{:S(2)}) %collective-permute-start.24) | collective-permute-done | bytes 245792 | tf_op jit(solution)/shard_map/cond/branch_0_fun/ppermute | solution.py:337
  156.1 2.9 %collective-permute-start.25 = (f32[30,16,128]{2,1,0:T(8,128)S(1)}, f32[30,16,128]{2,1,0:T(8,128)S(1)}, u32[]{:S(2)}, u32[]{:S(2)}) collective-permute-start(f32[30,16,128]{2,1,0:T(8,128)S(1)} %add.407), channel_id=1, source_target_pairs={{0,0},{1,241},{2,226},{3,211},{4,196},{5,181},{6,166},{7,151},{8,1... | collective-permute-start | bytes 737288 | tf_op jit(solution)/shard_map/cond/branch_0_fun/ppermute | solution.py:338
  159.1 12.1 %collective-permute-done.25.x_ref = f32[30,16,128]{2,1,0:T(8,128)S(1)} collective-permute-done((f32[30,16,128]{2,1,0:T(8,128)S(1)}, f32[30,16,128]{2,1,0:T(8,128)S(1)}, u32[]{:S(2)}, u32[]{:S(2)}) %collective-permute-start.25) | collective-permute-done | bytes 245792 | tf_op jit(solution)/shard_map/cond/branch_0_fun/ppermute | solution.py:338
  171.2 2.8 %collective-permute-start.26 = (f32[30,16,128]{2,1,0:T(8,128)S(1)}, f32[30,16,128]{2,1,0:T(8,128)S(1)}, u32[]{:S(2)}, u32[]{:S(2)}) collective-permute-start(f32[30,16,128]{2,1,0:T(8,128)S(1)} %pad_maximum_fusion.3), channel_id=1, source_target_pairs={{0,16},{16,0},{1,17},{17,1},{2,18},{18,2},{3,19},{19,3},{4,20},{20... | collective-permute-start | bytes 737288 | tf_op jit(solution)/shard_map/cond/branch_0_fun/ppermute | solution.py:26
  174.0 1.9 branch_0_fun.8
  175.9 2.9 %branch_0_fun.9 = f32[4,16,256]{2,1,0:T(8,128)S(1)} custom-call(s32[362]{0:T(512)S(1)} %get-tuple-element.16.tab, f32[30,16,128]{2,1,0:T(8,128)S(1)} %collective-permute-done.25.x_ref, bf16[30,128,256]{2,1,0:T(8,128)(2,1)S(1)} %copy-done.5, bf16[30,128,256]{2,1,0:T(8,128)(2,1)S(1)} %copy-done.7), custom_call_target="tpu_custom_call" | custom-call | flops 94371840 | bytes 6291456 | tf_op jit(solution)/shard_map/cond/branch_0_fun/pallas_call | solution.py:357
  178.9 0.7 branch_0_fun.7
  179.8 0.7 copy-done.11
  180.6 6.8 %all-to-all-start.3 = ((f32[16,16,1280]{2,1,0:T(8,128)}), f32[16,16,1280]{2,1,0:T(8,128)S(1)}, u32[]{:S(2)}, u32[]{:S(2)}) async-start(f32[16,16,1280]{2,1,0:T(8,128)} %get-tuple-element.43), calls=%async_computation.3 | async-start | bytes 2621440 | tf_op jit(solution)/shard_map/all_to_all | solution.py:449
  187.6 5.8 %collective-permute-start.32 = (f32[4,16,256]{2,1,0:T(8,128)S(1)}, f32[4,16,256]{2,1,0:T(8,128)S(1)}, u32[]{:S(2)}, u32[]{:S(2)}) collective-permute-start(f32[4,16,256]{2,1,0:T(8,128)S(1)} %get-tuple-element.44), channel_id=1, source_target_pairs={{0,46},{1,47},{2,32},{3,33},{4,34},{5,35},{6,36},{7,37},{8,38},{9,... | collective-permute-start | bytes 196616 | tf_op jit(solution)/shard_map/ppermute | solution.py:458
  193.5 0.7 collective-permute-start.33
  194.2 9.3 %collective-permute-done.31 = f32[4,16,256]{2,1,0:T(8,128)S(1)} collective-permute-done((f32[4,16,256]{2,1,0:T(8,128)S(1)}, f32[4,16,256]{2,1,0:T(8,128)S(1)}, u32[]{:S(2)}, u32[]{:S(2)}) %collective-permute-start.31) | collective-permute-done | bytes 65568 | tf_op jit(solution)/shard_map/ppermute | solution.py:458
  203.5 4.9 %collective-permute-start.34 = (f32[4,16,256]{2,1,0:T(8,128)S(1)}, f32[4,16,256]{2,1,0:T(8,128)S(1)}, u32[]{:S(2)}, u32[]{:S(2)}) collective-permute-start(f32[4,16,256]{2,1,0:T(8,128)S(1)} %add_add_fusion.1), channel_id=1, source_target_pairs={{0,76},{1,77},{2,78},{3,79},{4,64},{5,65},{6,66},{7,67},{8,68},{9,... | collective-permute-start | bytes 196616 | tf_op jit(solution)/shard_map/ppermute | solution.py:458
  208.4 1.7 collective-permute-start.35
  210.2 2.4 collective-permute-start.36
  212.6 4.0 %collective-permute-done.35 = f32[4,16,256]{2,1,0:T(8,128)S(1)} collective-permute-done((f32[4,16,256]{2,1,0:T(8,128)S(1)}, f32[4,16,256]{2,1,0:T(8,128)S(1)}, u32[]{:S(2)}, u32[]{:S(2)}) %collective-permute-start.35) | collective-permute-done | bytes 65568 | tf_op jit(solution)/shard_map/ppermute | solution.py:458
  216.5 2.0 collective-permute-done.36
  218.5 1.4 shard_map.86
  219.9 11.2 %all-to-all-start.4 = ((f32[16,16,256]{2,1,0:T(8,128)}), f32[16,16,256]{2,1,0:T(8,128)S(1)}, u32[]{:S(2)}, u32[]{:S(2)}) async-start(f32[16,16,256]{2,1,0:T(8,128)} %shard_map.86), calls=%async_computation.4 | async-start | bytes 524288 | tf_op jit(solution)/shard_map/all_to_all | solution.py:461
  231.1 2.0 shard_map.85
  233.1 5.1 %all-to-all-done.4.x_ref = f32[16,16,256]{2,1,0:T(8,128)S(1)} async-done(((f32[16,16,256]{2,1,0:T(8,128)}), f32[16,16,256]{2,1,0:T(8,128)S(1)}, u32[]{:S(2)}, u32[]{:S(2)}) %all-to-all-start.4) | async-done | bytes 262176 | tf_op jit(solution)/shard_map/all_to_all | solution.py:461
  238.3 1.3 shard_map.87
  (97 shorter events, 5.7 us)
Async XLA Ops:
  0.6 9.4 %copy-start.13 = (s32[4]{0:T(128)S(1)}, s32[4]{0:T(128)}, u32[]{:S(2)}) copy-start(s32[4]{0:T(128)} %param.12) | copy-start | bytes 52
  0.6 9.5 %copy-start.12 = (s32[4,96]{1,0:T(4,128)S(1)}, s32[4,96]{1,0:T(4,128)}, u32[]{:S(2)}) copy-start(s32[4,96]{1,0:T(4,128)} %param.11) | copy-start | bytes 4612
  0.7 10.3 %copy-start.14 = (s32[4]{0:T(128)S(1)}, s32[4]{0:T(128)}, u32[]{:S(2)}) copy-start(s32[4]{0:T(128)} %param.13) | copy-start | bytes 52
  3.2 25.5 %all-to-all-start.2 = ((f32[16,10,8,256]{3,2,1,0:T(8,128)}), f32[16,10,8,256]{3,2,1,0:T(8,128)S(1)}, u32[]{:S(2)}, u32[]{:S(2)}) async-start(f32[16,10,8,256]{3,2,1,0:T(8,128)} %copy.12), calls=%async_computation.2 | async-start | bytes 2621440 | tf_op jit(solution)/shard_map/all_to_all | solution.py:396
  29.4 6.9 %collective-permute-start = (f32[30,8,256]{2,1,0:T(8,128)S(1)}, f32[30,8,256]{2,1,0:T(8,128)S(1)}, u32[]{:S(2)}, u32[]{:S(2)}) collective-permute-start(f32[30,8,256]{2,1,0:T(8,128)S(1)} %branch_0_fun.5), channel_id=1, source_target_pairs={{0,8},{8,0},{1,9},{9,1},{2,10},{10,2},{3,11},{11,3},{4,12},{12,4},... | collective-permute-start | bytes 737288 | tf_op jit(solution)/shard_map/cond/branch_0_fun/ppermute | solution.py:26
  29.8 9.4 %collective-permute-start.1 = (f32[30,8,256]{2,1,0:T(8,128)S(1)}, f32[30,8,256]{2,1,0:T(8,128)S(1)}, u32[]{:S(2)}, u32[]{:S(2)}) collective-permute-start(f32[30,8,256]{2,1,0:T(8,128)S(1)} %branch_0_fun.5), channel_id=1, source_target_pairs={{0,2},{2,4},{4,6},{6,0},{1,3},{3,5},{5,7},{7,1},{8,10},{10,12},{12... | collective-permute-start | bytes 737288 | tf_op jit(solution)/shard_map/cond/branch_0_fun/ppermute | solution.py:31
  36.3 5.9 %collective-permute-start.4 = (f32[30,8,256]{2,1,0:T(8,128)S(1)}, f32[30,8,256]{2,1,0:T(8,128)S(1)}, u32[]{:S(2)}, u32[]{:S(2)}) collective-permute-start(f32[30,8,256]{2,1,0:T(8,128)S(1)} %collective-permute-done), channel_id=1, source_target_pairs={{0,6},{2,0},{4,2},{6,4},{1,7},{3,1},{5,3},{7,5},{8,14},{10,8},{12,... | collective-permute-start | bytes 737288 | tf_op jit(solution)/shard_map/cond/branch_0_fun/ppermute | solution.py:31
  37.7 9.7 %collective-permute-start.2 = (f32[30,8,256]{2,1,0:T(8,128)S(1)}, f32[30,8,256]{2,1,0:T(8,128)S(1)}, u32[]{:S(2)}, u32[]{:S(2)}) collective-permute-start(f32[30,8,256]{2,1,0:T(8,128)S(1)} %branch_0_fun.5), channel_id=1, source_target_pairs={{0,6},{2,0},{4,2},{6,4},{1,7},{3,1},{5,3},{7,5},{8,14},{10,8},{12,... | collective-permute-start | bytes 737288 | tf_op jit(solution)/shard_map/cond/branch_0_fun/ppermute | solution.py:31
  38.1 14.2 %collective-permute-start.3 = (f32[30,8,256]{2,1,0:T(8,128)S(1)}, f32[30,8,256]{2,1,0:T(8,128)S(1)}, u32[]{:S(2)}, u32[]{:S(2)}) collective-permute-start(f32[30,8,256]{2,1,0:T(8,128)S(1)} %collective-permute-done), channel_id=1, source_target_pairs={{0,2},{2,4},{4,6},{6,0},{1,3},{3,5},{5,7},{7,1},{8,10},{10,12},{12... | collective-permute-start | bytes 737288 | tf_op jit(solution)/shard_map/cond/branch_0_fun/ppermute | solution.py:31
  39.2 13.0 %collective-permute-start.5 = (f32[30,8,256]{2,1,0:T(8,128)S(1)}, f32[30,8,256]{2,1,0:T(8,128)S(1)}, u32[]{:S(2)}, u32[]{:S(2)}) collective-permute-start(f32[30,8,256]{2,1,0:T(8,128)S(1)} %collective-permute-done.1), channel_id=1, source_target_pairs={{0,2},{2,4},{4,6},{6,0},{1,3},{3,5},{5,7},{7,1},{8,10},{10,12},{12... | collective-permute-start | bytes 737288 | tf_op jit(solution)/shard_map/cond/branch_0_fun/ppermute | solution.py:31
  42.1 10.5 %collective-permute-start.6 = (f32[30,8,256]{2,1,0:T(8,128)S(1)}, f32[30,8,256]{2,1,0:T(8,128)S(1)}, u32[]{:S(2)}, u32[]{:S(2)}) collective-permute-start(f32[30,8,256]{2,1,0:T(8,128)S(1)} %collective-permute-done.4), channel_id=1, source_target_pairs={{0,6},{2,0},{4,2},{6,4},{1,7},{3,1},{5,3},{7,5},{8,14},{10,8},{12,... | collective-permute-start | bytes 737288 | tf_op jit(solution)/shard_map/cond/branch_0_fun/ppermute | solution.py:31
  47.5 7.9 %collective-permute-start.7 = (f32[4,30,8,256]{3,2,1,0:T(8,128)S(1)}, f32[4,30,8,256]{3,2,1,0:T(8,128)S(1)}, u32[]{:S(2)}, u32[]{:S(2)}) collective-permute-start(f32[4,30,8,256]{3,2,1,0:T(8,128)S(1)} %pad_maximum_fusion.g0), channel_id=1, source_target_pairs={{0,1},{1,0},{2,3},{3,2},{4,5},{5,4},{6,7},{7,6},{8,9},{9,8},{10,11... | collective-permute-start | bytes 2949128 | tf_op jit(solution)/shard_map/cond/branch_0_fun/ppermute | solution.py:26
  52.8 4.9 %collective-permute-start.8 = (f32[4,30,8,256]{3,2,1,0:T(8,128)S(1)}, f32[4,30,8,256]{3,2,1,0:T(8,128)}, u32[]{:S(2)}, u32[]{:S(2)}) collective-permute-start(f32[4,30,8,256]{3,2,1,0:T(8,128)S(1)} %pad_maximum_fusion.1.g1), channel_id=1, source_target_pairs={{0,1},{1,0},{2,3},{3,2},{4,5},{5,4},{6,7},{7,6},{8,9},{9,8},{10,11... | collective-permute-start | bytes 2949128 | tf_op jit(solution)/shard_map/cond/branch_0_fun/ppermute | solution.py:26
  76.0 1.9 copy-start.1
  76.0 2.5 %copy-start.4 = (bf16[30,128,256]{2,1,0:T(8,128)(2,1)}, bf16[30,128,256]{2,1,0:T(8,128)(2,1)S(1)}, u32[]{:S(2)}) copy-start(bf16[30,128,256]{2,1,0:T(8,128)(2,1)S(1)} %get-tuple-element.23.hi_ref) | copy-start | bytes 5898244 | tf_op jit(solution)/shard_map/cond
  76.1 3.1 %copy-start.6 = (bf16[30,128,256]{2,1,0:T(8,128)(2,1)}, bf16[30,128,256]{2,1,0:T(8,128)(2,1)S(1)}, u32[]{:S(2)}) copy-start(bf16[30,128,256]{2,1,0:T(8,128)(2,1)S(1)} %get-tuple-element.24.lo_ref) | copy-start | bytes 5898244 | tf_op jit(solution)/shard_map/cond
  79.1 8.3 %collective-permute-start.9 = (f32[15,32,128]{2,1,0:T(8,128)S(1)}, f32[15,32,128]{2,1,0:T(8,128)S(1)}, u32[]{:S(2)}, u32[]{:S(2)}) collective-permute-start(f32[15,32,128]{2,1,0:T(8,128)S(1)} %get-tuple-element.61), channel_id=1, source_target_pairs={{0,32},{32,64},{64,96},{96,128},{128,160},{160,192},{192,224},{224... | collective-permute-start | bytes 737288 | tf_op jit(solution)/shard_map/cond/branch_0_fun/ppermute | solution.py:31
  79.1 9.4 %collective-permute-start.16 = (f32[3,5,32,128]{3,2,1,0:T(8,128)S(1)}, f32[3,5,32,128]{3,2,1,0:T(8,128)S(1)}, u32[]{:S(2)}, u32[]{:S(2)}) collective-permute-start(f32[3,5,32,128]{3,2,1,0:T(8,128)S(1)} %bitcast.88), channel_id=1, source_target_pairs={{0,224},{32,0},{64,32},{96,64},{128,96},{160,128},{192,160},{224,1... | collective-permute-start | bytes 737288 | tf_op jit(solution)/shard_map/cond/branch_0_fun/ppermute | solution.py:31
  88.4 7.5 %collective-permute-start.10 = (f32[15,32,128]{2,1,0:T(8,128)S(1)}, f32[15,32,128]{2,1,0:T(8,128)S(1)}, u32[]{:S(2)}, u32[]{:S(2)}) collective-permute-start(f32[15,32,128]{2,1,0:T(8,128)S(1)} %fusion.6), channel_id=1, source_target_pairs={{0,32},{32,64},{64,96},{96,128},{128,160},{160,192},{192,224},{224... | collective-permute-start | bytes 737288 | tf_op jit(solution)/shard_map/cond/branch_0_fun/ppermute | solution.py:31
  88.6 8.4 %collective-permute-start.17 = (f32[3,5,32,128]{3,2,1,0:T(8,128)S(1)}, f32[3,5,32,128]{3,2,1,0:T(8,128)S(1)}, u32[]{:S(2)}, u32[]{:S(2)}) collective-permute-start(f32[3,5,32,128]{3,2,1,0:T(8,128)S(1)} %add.381), channel_id=1, source_target_pairs={{0,224},{32,0},{64,32},{96,64},{128,96},{160,128},{192,160},{224,1... | collective-permute-start | bytes 737288 | tf_op jit(solution)/shard_map/cond/branch_0_fun/ppermute | solution.py:31
  96.8 6.3 %collective-permute-start.11 = (f32[15,32,128]{2,1,0:T(8,128)S(1)}, f32[15,32,128]{2,1,0:T(8,128)S(1)}, u32[]{:S(2)}, u32[]{:S(2)}) collective-permute-start(f32[15,32,128]{2,1,0:T(8,128)S(1)} %fusion.5), channel_id=1, source_target_pairs={{0,32},{32,64},{64,96},{96,128},{128,160},{160,192},{192,224},{224... | collective-permute-start | bytes 737288 | tf_op jit(solution)/shard_map/cond/branch_0_fun/ppermute | solution.py:31
  97.0 7.3 %collective-permute-start.18 = (f32[3,5,32,128]{3,2,1,0:T(8,128)S(1)}, f32[3,5,32,128]{3,2,1,0:T(8,128)S(1)}, u32[]{:S(2)}, u32[]{:S(2)}) collective-permute-start(f32[3,5,32,128]{3,2,1,0:T(8,128)S(1)} %add.385), channel_id=1, source_target_pairs={{0,224},{32,0},{64,32},{96,64},{128,96},{160,128},{192,160},{224,1... | collective-permute-start | bytes 737288 | tf_op jit(solution)/shard_map/cond/branch_0_fun/ppermute | solution.py:31
  104.2 6.3 %collective-permute-start.12 = (f32[15,32,128]{2,1,0:T(8,128)S(1)}, f32[15,32,128]{2,1,0:T(8,128)S(1)}, u32[]{:S(2)}, u32[]{:S(2)}) collective-permute-start(f32[15,32,128]{2,1,0:T(8,128)S(1)} %fusion.4), channel_id=1, source_target_pairs={{0,32},{32,64},{64,96},{96,128},{128,160},{160,192},{192,224},{224... | collective-permute-start | bytes 737288 | tf_op jit(solution)/shard_map/cond/branch_0_fun/ppermute | solution.py:31
  104.3 7.3 %collective-permute-start.19 = (f32[3,5,32,128]{3,2,1,0:T(8,128)S(1)}, f32[3,5,32,128]{3,2,1,0:T(8,128)S(1)}, u32[]{:S(2)}, u32[]{:S(2)}) collective-permute-start(f32[3,5,32,128]{3,2,1,0:T(8,128)S(1)} %add.389), channel_id=1, source_target_pairs={{0,224},{32,0},{64,32},{96,64},{128,96},{160,128},{192,160},{224,1... | collective-permute-start | bytes 737288 | tf_op jit(solution)/shard_map/cond/branch_0_fun/ppermute | solution.py:31
  111.5 6.3 %collective-permute-start.13 = (f32[15,32,128]{2,1,0:T(8,128)S(1)}, f32[15,32,128]{2,1,0:T(8,128)S(1)}, u32[]{:S(2)}, u32[]{:S(2)}) collective-permute-start(f32[15,32,128]{2,1,0:T(8,128)S(1)} %fusion.3), channel_id=1, source_target_pairs={{0,32},{32,64},{64,96},{96,128},{128,160},{160,192},{192,224},{224... | collective-permute-start | bytes 737288 | tf_op jit(solution)/shard_map/cond/branch_0_fun/ppermute | solution.py:31
  111.6 7.3 %collective-permute-start.20 = (f32[3,5,32,128]{3,2,1,0:T(8,128)S(1)}, f32[3,5,32,128]{3,2,1,0:T(8,128)S(1)}, u32[]{:S(2)}, u32[]{:S(2)}) collective-permute-start(f32[3,5,32,128]{3,2,1,0:T(8,128)S(1)} %add.393), channel_id=1, source_target_pairs={{0,224},{32,0},{64,32},{96,64},{128,96},{160,128},{192,160},{224,1... | collective-permute-start | bytes 737288 | tf_op jit(solution)/shard_map/cond/branch_0_fun/ppermute | solution.py:31
  118.8 6.6 %collective-permute-start.14 = (f32[15,32,128]{2,1,0:T(8,128)S(1)}, f32[15,32,128]{2,1,0:T(8,128)S(1)}, u32[]{:S(2)}, u32[]{:S(2)}) collective-permute-start(f32[15,32,128]{2,1,0:T(8,128)S(1)} %fusion.2), channel_id=1, source_target_pairs={{0,32},{32,64},{64,96},{96,128},{128,160},{160,192},{192,224},{224... | collective-permute-start | bytes 737288 | tf_op jit(solution)/shard_map/cond/branch_0_fun/ppermute | solution.py:31
  118.9 7.6 %collective-permute-start.21 = (f32[3,5,32,128]{3,2,1,0:T(8,128)S(1)}, f32[3,5,32,128]{3,2,1,0:T(8,128)S(1)}, u32[]{:S(2)}, u32[]{:S(2)}) collective-permute-start(f32[3,5,32,128]{3,2,1,0:T(8,128)S(1)} %add.397), channel_id=1, source_target_pairs={{0,224},{32,0},{64,32},{96,64},{128,96},{160,128},{192,160},{224,1... | collective-permute-start | bytes 737288 | tf_op jit(solution)/shard_map/cond/branch_0_fun/ppermute | solution.py:31
  126.4 49.5 %copy-start.5 = (bf16[30,128,256]{2,1,0:T(8,128)(2,1)S(1)}, bf16[30,128,256]{2,1,0:T(8,128)(2,1)}, u32[]{:S(2)}) copy-start(bf16[30,128,256]{2,1,0:T(8,128)(2,1)} %copy-done.4) | copy-start | bytes 5898244 | tf_op jit(solution)/shard_map/cond
  126.4 7.7 %collective-permute-start.15 = (f32[15,32,128]{2,1,0:T(8,128)S(1)}, f32[15,32,128]{2,1,0:T(8,128)S(1)}, u32[]{:S(2)}, u32[]{:S(2)}) collective-permute-start(f32[15,32,128]{2,1,0:T(8,128)S(1)} %fusion.1), channel_id=1, source_target_pairs={{0,32},{32,64},{64,96},{96,128},{128,160},{160,192},{192,224},{224... | collective-permute-start | bytes 737288 | tf_op jit(solution)/shard_map/cond/branch_0_fun/ppermute | solution.py:31
  126.5 49.4 %copy-start.7 = (bf16[30,128,256]{2,1,0:T(8,128)(2,1)S(1)}, bf16[30,128,256]{2,1,0:T(8,128)(2,1)}, u32[]{:S(2)}) copy-start(bf16[30,128,256]{2,1,0:T(8,128)(2,1)} %copy-done.6) | copy-start | bytes 5898244 | tf_op jit(solution)/shard_map/cond
  126.6 8.5 %collective-permute-start.22 = (f32[3,5,32,128]{3,2,1,0:T(8,128)S(1)}, f32[3,5,32,128]{3,2,1,0:T(8,128)S(1)}, u32[]{:S(2)}, u32[]{:S(2)}) collective-permute-start(f32[3,5,32,128]{3,2,1,0:T(8,128)S(1)} %add.401), channel_id=1, source_target_pairs={{0,224},{32,0},{64,32},{96,64},{128,96},{160,128},{192,160},{224,1... | collective-permute-start | bytes 737288 | tf_op jit(solution)/shard_map/cond/branch_0_fun/ppermute | solution.py:31
  135.2 10.3 %collective-permute-start.23 = (f32[30,16,128]{2,1,0:T(8,128)S(1)}, f32[30,16,128]{2,1,0:T(8,128)S(1)}, u32[]{:S(2)}, u32[]{:S(2)}) collective-permute-start(f32[30,16,128]{2,1,0:T(8,128)S(1)} %pad_maximum_fusion.2), channel_id=1, source_target_pairs={{0,0},{1,15},{2,14},{3,13},{4,12},{5,11},{6,10},{7,9},{8,8},{9,7},... | collective-permute-start | bytes 737288 | tf_op jit(solution)/shard_map/cond/branch_0_fun/ppermute | solution.py:337
  137.2 18.9 %collective-permute-start.24 = (f32[30,16,128]{2,1,0:T(8,128)S(1)}, f32[30,16,128]{2,1,0:T(8,128)S(1)}, u32[]{:S(2)}, u32[]{:S(2)}) collective-permute-start(f32[30,16,128]{2,1,0:T(8,128)S(1)} %pad_maximum_fusion.3), channel_id=1, source_target_pairs={{0,31},{1,30},{2,29},{3,28},{4,27},{5,26},{6,25},{7,24},{8,23},{9,... | collective-permute-start | bytes 737288 | tf_op jit(solution)/shard_map/cond/branch_0_fun/ppermute | solution.py:337
  156.1 15.1 %collective-permute-start.25 = (f32[30,16,128]{2,1,0:T(8,128)S(1)}, f32[30,16,128]{2,1,0:T(8,128)S(1)}, u32[]{:S(2)}, u32[]{:S(2)}) collective-permute-start(f32[30,16,128]{2,1,0:T(8,128)S(1)} %add.407), channel_id=1, source_target_pairs={{0,0},{1,241},{2,226},{3,211},{4,196},{5,181},{6,166},{7,151},{8,1... | collective-permute-start | bytes 737288 | tf_op jit(solution)/shard_map/cond/branch_0_fun/ppermute | solution.py:338
  171.2 7.6 %collective-permute-start.26 = (f32[30,16,128]{2,1,0:T(8,128)S(1)}, f32[30,16,128]{2,1,0:T(8,128)S(1)}, u32[]{:S(2)}, u32[]{:S(2)}) collective-permute-start(f32[30,16,128]{2,1,0:T(8,128)S(1)} %pad_maximum_fusion.3), channel_id=1, source_target_pairs={{0,16},{16,0},{1,17},{17,1},{2,18},{18,2},{3,19},{19,3},{4,20},{20... | collective-permute-start | bytes 737288 | tf_op jit(solution)/shard_map/cond/branch_0_fun/ppermute | solution.py:26
  179.8 0.7 copy-start.11
  180.6 57.7 %copy-start.8 = (f32[1,256,256]{2,1,0:T(8,128)S(1)}, f32[1,256,256]{2,1,0:T(8,128)}, u32[]{:S(2)}) copy-start(f32[1,256,256]{2,1,0:T(8,128)} %param.10) | copy-start | bytes 786436
  180.6 38.0 %all-to-all-start.3 = ((f32[16,16,1280]{2,1,0:T(8,128)}), f32[16,16,1280]{2,1,0:T(8,128)S(1)}, u32[]{:S(2)}, u32[]{:S(2)}) async-start(f32[16,16,1280]{2,1,0:T(8,128)} %get-tuple-element.43), calls=%async_computation.3 | async-start | bytes 2621440 | tf_op jit(solution)/shard_map/all_to_all | solution.py:449
  187.4 16.1 %collective-permute-start.31 = (f32[4,16,256]{2,1,0:T(8,128)S(1)}, f32[4,16,256]{2,1,0:T(8,128)S(1)}, u32[]{:S(2)}, u32[]{:S(2)}) collective-permute-start(f32[4,16,256]{2,1,0:T(8,128)S(1)} %get-tuple-element.44), channel_id=1, source_target_pairs={{0,31},{1,16},{2,17},{3,18},{4,19},{5,20},{6,21},{7,22},{8,23},{9,... | collective-permute-start | bytes 196616 | tf_op jit(solution)/shard_map/ppermute | solution.py:458
  187.6 15.8 %collective-permute-start.32 = (f32[4,16,256]{2,1,0:T(8,128)S(1)}, f32[4,16,256]{2,1,0:T(8,128)S(1)}, u32[]{:S(2)}, u32[]{:S(2)}) collective-permute-start(f32[4,16,256]{2,1,0:T(8,128)S(1)} %get-tuple-element.44), channel_id=1, source_target_pairs={{0,46},{1,47},{2,32},{3,33},{4,34},{5,35},{6,36},{7,37},{8,38},{9,... | collective-permute-start | bytes 196616 | tf_op jit(solution)/shard_map/ppermute | solution.py:458
  193.5 10.0 %collective-permute-start.33 = (f32[4,16,256]{2,1,0:T(8,128)S(1)}, f32[4,16,256]{2,1,0:T(8,128)S(1)}, u32[]{:S(2)}, u32[]{:S(2)}) collective-permute-start(f32[4,16,256]{2,1,0:T(8,128)S(1)} %get-tuple-element.44), channel_id=1, source_target_pairs={{0,61},{1,62},{2,63},{3,48},{4,49},{5,50},{6,51},{7,52},{8,53},{9,... | collective-permute-start | bytes 196616 | tf_op jit(solution)/shard_map/ppermute | solution.py:458
  203.5 9.1 %collective-permute-start.34 = (f32[4,16,256]{2,1,0:T(8,128)S(1)}, f32[4,16,256]{2,1,0:T(8,128)S(1)}, u32[]{:S(2)}, u32[]{:S(2)}) collective-permute-start(f32[4,16,256]{2,1,0:T(8,128)S(1)} %add_add_fusion.1), channel_id=1, source_target_pairs={{0,76},{1,77},{2,78},{3,79},{4,64},{5,65},{6,66},{7,67},{8,68},{9,... | collective-permute-start | bytes 196616 | tf_op jit(solution)/shard_map/ppermute | solution.py:458
  208.4 8.1 %collective-permute-start.35 = (f32[4,16,256]{2,1,0:T(8,128)S(1)}, f32[4,16,256]{2,1,0:T(8,128)S(1)}, u32[]{:S(2)}, u32[]{:S(2)}) collective-permute-start(f32[4,16,256]{2,1,0:T(8,128)S(1)} %add_add_fusion.1), channel_id=1, source_target_pairs={{0,136},{1,137},{2,138},{3,139},{4,140},{5,141},{6,142},{7,143},{8... | collective-permute-start | bytes 196616 | tf_op jit(solution)/shard_map/ppermute | solution.py:458
  210.2 8.3 %collective-permute-start.36 = (f32[4,16,256]{2,1,0:T(8,128)S(1)}, f32[4,16,256]{2,1,0:T(8,128)S(1)}, u32[]{:S(2)}, u32[]{:S(2)}) collective-permute-start(f32[4,16,256]{2,1,0:T(8,128)S(1)} %add_add_fusion.1), channel_id=1, source_target_pairs={{0,196},{1,197},{2,198},{3,199},{4,200},{5,201},{6,202},{7,203},{8... | collective-permute-start | bytes 196616 | tf_op jit(solution)/shard_map/ppermute | solution.py:458
  219.9 18.4 %all-to-all-start.4 = ((f32[16,16,256]{2,1,0:T(8,128)}), f32[16,16,256]{2,1,0:T(8,128)S(1)}, u32[]{:S(2)}, u32[]{:S(2)}) async-start(f32[16,16,256]{2,1,0:T(8,128)} %shard_map.86), calls=%async_computation.4 | async-start | bytes 524288 | tf_op jit(solution)/shard_map/all_to_all | solution.py:461
